TPU v7x, 32 devices: a whole 2x2x4 slice. The times are simulated.
32 devices in a mesh: groups: 2 (over x), rows: 16 (over z, y, core).
Axes of the slice: x: 2, y: 2, z: 4, core: 2. Of those that a mesh axis runs over, the one named last changes fastest.
Arguments:
- tokens: bfloat16 [64, 256, 1024], P(('groups', 'rows')), parts along dimension 0, may hold values from -6 to 6
- peg_weight: float32 [3, 3, 1024], replicated, may hold values from -2 to 2
- peg_bias: float32 [1024], replicated, may hold values from -3 to 3
- norm_gain: float32 [1024], replicated, may hold values from 0.25 to 1.75
- norm_bias: float32 [1024], replicated, may hold values from -3 to 3
- qkv_weight: bfloat16 [1024, 3072], replicated, may hold values from -1 to 1
- qkv_bias: float32 [3072], replicated, may hold values from -3 to 3
- out_weight: bfloat16 [1024, 1024], replicated, may hold values from -0.1875 to 0.1875
- out_bias: float32 [1024], replicated, may hold values from -3 to 3
Outputs:
- result: bfloat16 [64, 256, 1024], P(('groups', 'rows')), parts along dimension 0
There are 2 independent parts, one for each index of `groups`. A program takes and returns all parts, laid end to end along the dimension named above; an argument that names none is the same for every part. Nothing has to cross between parts.
All inputs are finite; a program needn't handle non-finite values.
Results may differ from a plain program's by a relative error of at most 0.006.
Values may be sent and summed in bfloat16 or wider, within the bound.
No kernel may reach another device: no remote copies, remote signals or barrier semaphores. Data moves between devices by JAX's collectives and lax.ppermute only.
A program may use at most 64 MiB of HBM per device.

v0:
```python
import math

import jax
import jax.numpy as jnp
from jax import lax
from jax.sharding import PartitionSpec as P

HEADS = 16
DH = 64
ROW_HEADS = 8


def with_halo(value, sides, width):
    for axis, dim in sides:
        devices, length = (lax.axis_size(axis), value.shape[dim])
        up = [(i, (i + 1) % devices) for i in range(devices - 1)]
        down = [(j, i) for i, j in up]
        last = lax.slice_in_dim(value, length - width, length, axis=dim)
        leading = lax.slice_in_dim(value, 0, width, axis=dim)
        before = lax.ppermute(last, axis, up)
        after = lax.ppermute(leading, axis, down)
        value = jnp.concatenate([before, value, after], axis=dim)
    return value


def convolve(padded, peg_weight, peg_bias, count_rows, count_cols):
    total = padded[1 : count_rows + 1, 1 : count_cols + 1, :].astype(jnp.float32) + peg_bias
    for offset_row in range(3):
        for offset_col in range(3):
            piece = padded[
                offset_row : offset_row + count_rows, offset_col : offset_col + count_cols, :
            ]
            total = total + piece.astype(jnp.float32) * peg_weight[offset_row, offset_col]
    return total.astype(jnp.bfloat16)


def layer_norm(mixed, norm_gain, norm_bias):
    values = mixed.astype(jnp.float32)
    center = jnp.mean(values, axis=-1, keepdims=True)
    spread = jnp.mean((values - center) ** 2, axis=-1, keepdims=True)
    return ((values - center) * lax.rsqrt(spread + 1e-06) * norm_gain + norm_bias).astype(
        jnp.bfloat16
    )


def project_three(normed, qkv_weight, qkv_bias, first_col, last_col):
    model = normed.shape[-1]
    flat_rows = normed.reshape(-1, model)
    outputs = []
    for part_index in range(3):
        lower = part_index * model + first_col
        upper = part_index * model + last_col
        projected = (
            jnp.dot(flat_rows, qkv_weight[:, lower:upper], preferred_element_type=jnp.float32)
            + qkv_bias[lower:upper]
        )
        outputs.append(
            projected.astype(jnp.bfloat16).reshape(normed.shape[:-1] + (last_col - first_col,))
        )
    return (outputs[0], outputs[1], outputs[2])


def attend_heads(
    query_all, key_all, value_all, head_count, softmax_divisor, scoring_equation, mixing_equation
):
    outputs = []
    for head_index in range(head_count):
        lower = head_index * DH
        query_rows = query_all[..., lower : lower + DH]
        key_operand = key_all[..., lower : lower + DH]
        value_operand = value_all[..., lower : lower + DH]
        attention_logits = (
            jnp.einsum(
                scoring_equation, query_rows, key_operand, preferred_element_type=jnp.float32
            )
            * softmax_divisor
        )
        highest = jnp.max(attention_logits, axis=-1, keepdims=True)
        attention_weights = jnp.exp(attention_logits - highest)
        attention_weights = (
            attention_weights / jnp.sum(attention_weights, axis=-1, keepdims=True)
        ).astype(jnp.bfloat16)
        outputs.append(
            jnp.einsum(
                mixing_equation,
                attention_weights,
                value_operand,
                preferred_element_type=jnp.float32,
            ).astype(jnp.bfloat16)
        )
    return jnp.concatenate(outputs, axis=-1)


def on_device(
    tokens, peg_weight, peg_bias, norm_gain, norm_bias, qkv_weight, qkv_bias, out_weight, out_bias
):
    bands = tokens.shape[0]
    width = tokens.shape[1]
    model = tokens.shape[2]
    height = bands * lax.axis_size("rows")
    row_features = ROW_HEADS * DH
    col_count = HEADS - ROW_HEADS
    padded = with_halo(tokens, (("rows", 0),), 1)
    padded = jnp.pad(padded, ((0, 0), (1, 1), (0, 0)))
    mixed = convolve(padded, peg_weight, peg_bias, bands, width)
    normed = layer_norm(mixed, norm_gain, norm_bias)
    row_query, row_key, row_value = project_three(normed, qkv_weight, qkv_bias, 0, row_features)
    arrived = lax.all_to_all(normed, "rows", split_axis=1, concat_axis=0, tiled=True)
    col_query, col_key, col_value = project_three(
        arrived, qkv_weight, qkv_bias, row_features, model
    )
    tau_row = math.log(width) / (math.log(16.0) * math.sqrt(DH))
    tau_col = math.log(height) / (math.log(16.0) * math.sqrt(DH))
    row_heads = attend_heads(
        row_query, row_key, row_value, ROW_HEADS, tau_row, "bld,bmd->blm", "blm,bmd->bld"
    )
    col_heads = attend_heads(
        col_query, col_key, col_value, col_count, tau_col, "lbd,mbd->blm", "blm,mbd->lbd"
    )
    returned = lax.all_to_all(col_heads, "rows", split_axis=0, concat_axis=1, tiled=True)
    attended = jnp.concatenate([row_heads, returned], axis=2).reshape(bands * width, model)
    result = (
        mixed.reshape(bands * width, model).astype(jnp.float32)
        + jnp.dot(attended, out_weight, preferred_element_type=jnp.float32)
        + out_bias
    )
    return result.astype(jnp.bfloat16).reshape(bands, width, model)


def solution(mesh):
    placed = (P(("groups", "rows"), None, None), P(), P(), P(), P(), P(), P(), P(), P())
    return jax.shard_map(
        on_device,
        mesh=mesh,
        in_specs=placed,
        out_specs=P(("groups", "rows"), None, None),
        check_vma=False,
    )
```

profile of v0, /device:TPU:0, one launch (start us, length us, event | category | flops | bytes accessed | tf_op | source)
XLA Modules:
  0.0 165.9 jit_solution(17638637918727739005)
XLA Ops:
  1.4 2.4 %collective-permute-start = (bf16[1,256,1024]{2,1,0:T(8,128)(2,1)S(1)}, bf16[1,256,1024]{2,1,0:T(8,128)(2,1)S(1)}, u32[]{:S(2)}, u32[]{:S(2)}) collective-permute-start(bf16[1,256,1024]{2,1,0:T(8,128)(2,1)S(1)} %get-tuple-element.7), channel_id=1, source_target_pairs={{0,1},{1,2},{2,3},{3,4},{4,5},{5,6},{6,7},{7,8},{8,9},{9,10},{10,1... | collective-permute-start | bytes 1572872 | tf_op jit(solution)/shard_map/ppermute | solution.py:20
  5.3 4.4 %collective-permute-done.1 = bf16[1,256,1024]{2,1,0:T(8,128)(2,1)S(1)} collective-permute-done((bf16[1,256,1024]{2,1,0:T(8,128)(2,1)S(1)}, bf16[1,256,1024]{2,1,0:T(8,128)(2,1)S(1)}, u32[]{:S(2)}, u32[]{:S(2)}) %collective-permute-start.1) | collective-permute-done | bytes 524320 | tf_op jit(solution)/shard_map/ppermute | solution.py:21
  10.5 2.6 %convert_reduce_fusion = (f32[2,256]{1,0:T(2,128)S(1)}, bf16[2,256,1024]{2,1,0:T(8,128)(2,1)S(1)}) fusion(f32[1024]{0:T(1024)S(1)} %bitcast.137, bf16[4,258,1024]{2,1,0:T(8,128)(2,1)S(1)} %fusion.21, f32[1024]{0:T(1024)S(1)} %bitcast.138, bf16[1,256,1024]{2,1,0:T(8,128)(2,1)S(1)} %collective-permute-done.1, bf16[2,256,1024]{2,1,0:T(8,128)(2,1)S(1)} %copy-done.1, ...), kind=kLoop, calls=%fused_computation.41 | loop fusion | flops 17300992 | bytes 9480192 | tf_op jit(solution)/shard_map/reduce_sum | solution.py:39
  14.0 3.1 %fusion.35 = bf16[512,512]{1,0:T(8,128)(2,1)} fusion(bf16[512,1024]{1,0:T(8,128)(2,1)S(1)} %bitcast.79, bf16[1024,3072]{1,0:T(8,128)(2,1)} %param.14, f32[512]{0:T(512)S(1)} %get-tuple-element.45), kind=kOutput, calls=%fused_computation.49 | convolution fusion | flops 537395200 | bytes 2623488 | tf_op jit(solution)/shard_map/dot_general | solution.py:54
  17.1 2.8 %fusion.34 = bf16[512,512]{1,0:T(8,128)(2,1)} fusion(bf16[512,1024]{1,0:T(8,128)(2,1)S(1)} %bitcast.80, bf16[1024,3072]{1,0:T(8,128)(2,1)} %param.14, f32[512]{0:T(512)S(1)} %get-tuple-element.46), kind=kOutput, calls=%fused_computation.48 | convolution fusion | flops 537395200 | bytes 2623488 | tf_op jit(solution)/shard_map/dot_general | solution.py:54
  26.7 2.1 %convolution_multiply_fusion.1 = f32[2,256,256]{1,2,0:T(8,128)} fusion(bf16[2,256,512]{2,1,0:T(8,128)(2,1)} %bitcast.90, bf16[2,256,512]{2,1,0:T(8,128)(2,1)} %bitcast.106), kind=kOutput, calls=%fused_computation.71 | convolution fusion | flops 16908288 | bytes 786432 | tf_op jit(solution)/shard_map/bld,bmd->blm/dot_general | solution.py:73
  28.7 2.1 %convolution_multiply_fusion.2 = f32[2,256,256]{1,2,0:T(8,128)} fusion(bf16[2,256,512]{2,1,0:T(8,128)(2,1)} %bitcast.91, bf16[2,256,512]{2,1,0:T(8,128)(2,1)} %bitcast.107), kind=kOutput, calls=%fused_computation.72 | convolution fusion | flops 16908288 | bytes 786432 | tf_op jit(solution)/shard_map/bld,bmd->blm/dot_general | solution.py:73
  30.8 2.0 %copy.367 = bf16[2,256,1024]{2,0,1:T(2,128)(2,1)} copy(bf16[2,256,1024]{2,1,0:T(8,128)(2,1)S(1)} %copy-done.3) | data formatting | bytes 2097152 | tf_op jit(solution)/shard_map/convert_element_type | solution.py:41
  32.9 2.7 %fusion.36 = bf16[512,512]{1,0:T(8,128)(2,1)} fusion(bf16[512,1024]{1,0:T(8,128)(2,1)S(1)} %bitcast.81, bf16[1024,3072]{1,0:T(8,128)(2,1)} %param.14, f32[512]{0:T(512)S(1)} %get-tuple-element.44), kind=kOutput, calls=%fused_computation.50 | convolution fusion | flops 537395200 | bytes 2623488 | tf_op jit(solution)/shard_map/dot_general | solution.py:54
  35.6 14.6 %all-to-all-start = ((bf16[2,256,1024]{2,0,1:T(2,128)(2,1)}), bf16[2,256,1024]{2,0,1:T(2,128)(2,1)}, u32[]{:S(2)}, u32[]{:S(2)}) async-start(bf16[2,256,1024]{2,0,1:T(2,128)(2,1)} %copy.367), calls=%async_computation | async-start | bytes 2097152 | tf_op jit(solution)/shard_map/all_to_all | solution.py:108
  50.3 2.1 %convolution_convert_fusion.9 = bf16[2,256,64]{1,2,0:T(8,128)(2,1)} fusion(f32[2,256]{1,0:T(2,128)S(1)} %fusion.275, bf16[2,256,512]{2,1,0:T(8,128)(2,1)} %bitcast.139, f32[2,256,256]{1,2,0:T(8,128)} %convolution_multiply_fusion.1), kind=kOutput, calls=%fused_computation.119 | convolution fusion | flops 17203968 | bytes 1247232 | tf_op jit(solution)/shard_map/blm,bmd->bld/dot_general | solution.py:84
  52.4 2.2 %convolution_convert_fusion.10 = bf16[2,256,64]{1,2,0:T(8,128)(2,1)} fusion(f32[2,256]{1,0:T(2,128)S(1)} %fusion.270, bf16[2,256,512]{2,1,0:T(8,128)(2,1)} %bitcast.140, f32[2,256,256]{1,2,0:T(8,128)} %convolution_multiply_fusion.2), kind=kOutput, calls=%fused_computation.120 | convolution fusion | flops 17203968 | bytes 1247232 | tf_op jit(solution)/shard_map/blm,bmd->bld/dot_general | solution.py:84
  54.6 2.0 %fusion.250 = f32[2,256]{1,0:T(2,128)} fusion(bf16[2,256,512]{2,1,0:T(8,128)(2,1)} %bitcast.92, bf16[2,256,512]{2,1,0:T(8,128)(2,1)} %bitcast.108), kind=kOutput, calls=%fused_computation.247 | convolution fusion | flops 17170688 | bytes 264192 | tf_op jit(solution)/shard_map/sub | solution.py:79
  56.6 2.0 %convolution_multiply_fusion.3 = f32[2,256,256]{1,2,0:T(8,128)} fusion(bf16[2,256,512]{2,1,0:T(8,128)(2,1)} %bitcast.93, bf16[2,256,512]{2,1,0:T(8,128)(2,1)} %bitcast.109), kind=kOutput, calls=%fused_computation.73 | convolution fusion | flops 16908288 | bytes 786432 | tf_op jit(solution)/shard_map/bld,bmd->blm/dot_general | solution.py:73
  58.6 2.2 %convolution_convert_fusion.11 = bf16[2,256,64]{1,2,0:T(8,128)(2,1)} fusion(f32[2,256]{1,0:T(2,128)S(1)} %fusion.265, bf16[2,256,512]{2,1,0:T(8,128)(2,1)} %bitcast.141, f32[2,256,256]{1,2,0:T(8,128)} %convolution_multiply_fusion.3), kind=kOutput, calls=%fused_computation.121 | convolution fusion | flops 17203968 | bytes 1247232 | tf_op jit(solution)/shard_map/blm,bmd->bld/dot_general | solution.py:84
  60.7 2.1 %convolution_multiply_fusion.4 = f32[2,256,256]{1,2,0:T(8,128)} fusion(bf16[2,256,512]{2,1,0:T(8,128)(2,1)} %bitcast.94, bf16[2,256,512]{2,1,0:T(8,128)(2,1)} %bitcast.110), kind=kOutput, calls=%fused_computation.74 | convolution fusion | flops 16908288 | bytes 786432 | tf_op jit(solution)/shard_map/bld,bmd->blm/dot_general | solution.py:73
  62.8 2.2 %convolution_convert_fusion.12 = bf16[2,256,64]{1,2,0:T(8,128)(2,1)} fusion(f32[2,256]{1,0:T(2,128)S(1)} %fusion.260, bf16[2,256,512]{2,1,0:T(8,128)(2,1)} %bitcast.142, f32[2,256,256]{1,2,0:T(8,128)} %convolution_multiply_fusion.4), kind=kOutput, calls=%fused_computation.122 | convolution fusion | flops 17203968 | bytes 1247232 | tf_op jit(solution)/shard_map/blm,bmd->bld/dot_general | solution.py:84
  65.0 2.0 %convolution_multiply_fusion.5 = f32[2,256,256]{1,2,0:T(8,128)} fusion(bf16[2,256,512]{2,1,0:T(8,128)(2,1)} %bitcast.95, bf16[2,256,512]{2,1,0:T(8,128)(2,1)} %bitcast.111), kind=kOutput, calls=%fused_computation.75 | convolution fusion | flops 16908288 | bytes 786432 | tf_op jit(solution)/shard_map/bld,bmd->blm/dot_general | solution.py:73
  67.0 2.2 %convolution_convert_fusion.13 = bf16[2,256,64]{1,2,0:T(8,128)(2,1)} fusion(f32[2,256]{1,0:T(2,128)S(1)} %fusion.255, bf16[2,256,512]{2,1,0:T(8,128)(2,1)} %bitcast.143, f32[2,256,256]{1,2,0:T(8,128)} %convolution_multiply_fusion.5), kind=kOutput, calls=%fused_computation.123 | convolution fusion | flops 17203968 | bytes 1247232 | tf_op jit(solution)/shard_map/blm,bmd->bld/dot_general | solution.py:84
  69.2 2.1 %convolution_multiply_fusion.6 = f32[2,256,256]{1,2,0:T(8,128)} fusion(bf16[2,256,512]{2,1,0:T(8,128)(2,1)} %bitcast.96, bf16[2,256,512]{2,1,0:T(8,128)(2,1)} %bitcast.112), kind=kOutput, calls=%fused_computation.76 | convolution fusion | flops 16908288 | bytes 786432 | tf_op jit(solution)/shard_map/bld,bmd->blm/dot_general | solution.py:73
  71.2 2.0 %convolution_multiply_fusion.7 = f32[2,256,256]{1,2,0:T(8,128)} fusion(bf16[2,256,512]{2,1,0:T(8,128)(2,1)} %bitcast.97, bf16[2,256,512]{2,1,0:T(8,128)(2,1)} %bitcast.113), kind=kOutput, calls=%fused_computation.77 | convolution fusion | flops 16908288 | bytes 786432 | tf_op jit(solution)/shard_map/bld,bmd->blm/dot_general | solution.py:73
  74.9 2.3 %fusion.39 = bf16[512,512]{1,0:T(8,128)(2,1)S(1)} fusion(bf16[512,1024]{1,0:T(8,128)(2,1)S(1)} %bitcast.119, bf16[1024,3072]{1,0:T(8,128)(2,1)} %param.14, f32[512]{0:T(512)S(1)} %get-tuple-element.47), kind=kOutput, calls=%fused_computation.53 | convolution fusion | flops 537395200 | bytes 2623488 | tf_op jit(solution)/shard_map/dot_general | solution.py:54
  77.2 1.9 %fusion.38 = bf16[512,512]{1,0:T(8,128)(2,1)S(1)} fusion(bf16[512,1024]{1,0:T(8,128)(2,1)S(1)} %bitcast.120, bf16[1024,3072]{1,0:T(8,128)(2,1)} %param.14, f32[512]{0:T(512)S(1)} %get-tuple-element.42), kind=kOutput, calls=%fused_computation.52 | convolution fusion | flops 537395200 | bytes 2623488 | tf_op jit(solution)/shard_map/dot_general | solution.py:54
  81.8 1.9 %convolution_multiply_fusion.8 = f32[16,32,32]{1,2,0:T(8,128)} fusion(bf16[32,16,64]{2,1,0:T(8,128)(2,1)} %get-tuple-element.55, bf16[32,16,64]{2,1,0:T(8,128)(2,1)} %get-tuple-element.9), kind=kOutput, calls=%fused_computation.86 | convolution fusion | flops 2113536 | bytes 196608 | tf_op jit(solution)/shard_map/lbd,mbd->blm/dot_general | solution.py:73
  83.7 1.8 %fusion.315 = f32[16,32]{1,0:T(8,128)} fusion(bf16[32,16,64]{2,1,0:T(8,128)(2,1)} %get-tuple-element.54, bf16[32,16,64]{2,1,0:T(8,128)(2,1)} %get-tuple-element.10), kind=kOutput, calls=%fused_computation.260 | convolution fusion | flops 2146335 | bytes 133120 | tf_op jit(solution)/shard_map/sub | solution.py:79
  85.5 1.8 %convolution_multiply_fusion.9 = f32[16,32,32]{1,2,0:T(8,128)} fusion(bf16[32,16,64]{2,1,0:T(8,128)(2,1)} %get-tuple-element.54, bf16[32,16,64]{2,1,0:T(8,128)(2,1)} %get-tuple-element.10), kind=kOutput, calls=%fused_computation.87 | convolution fusion | flops 2113536 | bytes 196608 | tf_op jit(solution)/shard_map/lbd,mbd->blm/dot_general | solution.py:73
  89.1 1.9 %convolution_multiply_fusion.10 = f32[16,32,32]{1,2,0:T(8,128)} fusion(bf16[32,16,64]{2,1,0:T(8,128)(2,1)} %get-tuple-element.53, bf16[32,16,64]{2,1,0:T(8,128)(2,1)} %get-tuple-element.11), kind=kOutput, calls=%fused_computation.88 | convolution fusion | flops 2113536 | bytes 196608 | tf_op jit(solution)/shard_map/lbd,mbd->blm/dot_general | solution.py:73
  92.8 1.9 %convolution_multiply_fusion.11 = f32[16,32,32]{1,2,0:T(8,128)} fusion(bf16[32,16,64]{2,1,0:T(8,128)(2,1)} %get-tuple-element.52, bf16[32,16,64]{2,1,0:T(8,128)(2,1)} %get-tuple-element.12), kind=kOutput, calls=%fused_computation.89 | convolution fusion | flops 2113536 | bytes 196608 | tf_op jit(solution)/shard_map/lbd,mbd->blm/dot_general | solution.py:73
  96.5 1.9 %convolution_multiply_fusion.12 = f32[16,32,32]{1,2,0:T(8,128)} fusion(bf16[32,16,64]{2,1,0:T(8,128)(2,1)} %get-tuple-element.51, bf16[32,16,64]{2,1,0:T(8,128)(2,1)} %get-tuple-element.13), kind=kOutput, calls=%fused_computation.90 | convolution fusion | flops 2113536 | bytes 196608 | tf_op jit(solution)/shard_map/lbd,mbd->blm/dot_general | solution.py:73
  98.4 1.8 %fusion.295 = f32[16,32]{1,0:T(8,128)} fusion(bf16[32,16,64]{2,1,0:T(8,128)(2,1)} %get-tuple-element.50, bf16[32,16,64]{2,1,0:T(8,128)(2,1)} %get-tuple-element.14), kind=kOutput, calls=%fused_computation.256 | convolution fusion | flops 2146335 | bytes 133120 | tf_op jit(solution)/shard_map/sub | solution.py:79
  100.2 1.9 %convolution_multiply_fusion.13 = f32[16,32,32]{1,2,0:T(8,128)} fusion(bf16[32,16,64]{2,1,0:T(8,128)(2,1)} %get-tuple-element.50, bf16[32,16,64]{2,1,0:T(8,128)(2,1)} %get-tuple-element.14), kind=kOutput, calls=%fused_computation.91 | convolution fusion | flops 2113536 | bytes 196608 | tf_op jit(solution)/shard_map/lbd,mbd->blm/dot_general | solution.py:73
  107.3 2.2 %fusion.37 = bf16[512,512]{1,0:T(8,128)(2,1)S(1)} fusion(bf16[512,1024]{1,0:T(8,128)(2,1)} %bitcast.121, bf16[1024,3072]{1,0:T(8,128)(2,1)} %param.14, f32[512]{0:T(512)S(1)} %get-tuple-element.43), kind=kOutput, calls=%fused_computation.51 | convolution fusion | flops 537395200 | bytes 2623488 | tf_op jit(solution)/shard_map/dot_general | solution.py:54
  112.0 2.0 %fusion.78 = bf16[32,16,64]{2,0,1:T(8,128)(2,1)} fusion(bf16[32,16,64]{2,1,0:T(8,128)(2,1)} %get-tuple-element.26, f32[16,32]{1,0:T(8,128)} %fusion.315, f32[16,32,32]{1,2,0:T(8,128)} %convolution_multiply_fusion.9), kind=kOutput, calls=%fused_computation.116 | convolution fusion | flops 2179615 | bytes 198656 | tf_op jit(solution)/shard_map/blm,mbd->lbd/dot_general | solution.py:84
  114.0 2.0 %fusion.77 = bf16[32,16,64]{2,0,1:T(8,128)(2,1)} fusion(bf16[32,16,64]{2,1,0:T(8,128)(2,1)} %get-tuple-element.27, f32[16,32]{1,0:T(8,128)} %fusion.310, f32[16,32,32]{1,2,0:T(8,128)} %convolution_multiply_fusion.10), kind=kOutput, calls=%fused_computation.115 | convolution fusion | flops 2179615 | bytes 198656 | tf_op jit(solution)/shard_map/blm,mbd->lbd/dot_general | solution.py:84
  116.0 2.0 %fusion.76 = bf16[32,16,64]{2,0,1:T(8,128)(2,1)} fusion(bf16[32,16,64]{2,1,0:T(8,128)(2,1)} %get-tuple-element.28, f32[16,32]{1,0:T(8,128)} %fusion.305, f32[16,32,32]{1,2,0:T(8,128)} %convolution_multiply_fusion.11), kind=kOutput, calls=%fused_computation.114 | convolution fusion | flops 2179615 | bytes 198656 | tf_op jit(solution)/shard_map/blm,mbd->lbd/dot_general | solution.py:84
  118.0 2.0 %fusion.75 = bf16[32,16,64]{2,0,1:T(8,128)(2,1)} fusion(bf16[32,16,64]{2,1,0:T(8,128)(2,1)} %get-tuple-element.29, f32[16,32]{1,0:T(8,128)S(1)} %copy-done.13, f32[16,32,32]{1,2,0:T(8,128)} %convolution_multiply_fusion.12), kind=kOutput, calls=%fused_computation.113 | convolution fusion | flops 2179615 | bytes 198656 | tf_op jit(solution)/shard_map/blm,mbd->lbd/dot_general | solution.py:84
  120.0 2.0 %fusion.74 = bf16[32,16,64]{2,0,1:T(8,128)(2,1)} fusion(bf16[32,16,64]{2,1,0:T(8,128)(2,1)} %get-tuple-element.30, f32[16,32]{1,0:T(8,128)S(1)} %copy-done.14, f32[16,32,32]{1,2,0:T(8,128)} %convolution_multiply_fusion.13), kind=kOutput, calls=%fused_computation.112 | convolution fusion | flops 2179615 | bytes 198656 | tf_op jit(solution)/shard_map/blm,mbd->lbd/dot_general | solution.py:84
  122.1 2.0 %fusion.73 = bf16[32,16,64]{2,0,1:T(8,128)(2,1)} fusion(bf16[32,16,64]{2,1,0:T(8,128)(2,1)S(1)} %get-tuple-element.31, f32[16,32]{1,0:T(8,128)} %fusion.290, f32[16,32,32]{1,2,0:T(8,128)} %convolution_multiply_fusion.14), kind=kOutput, calls=%fused_computation.111 | convolution fusion | flops 2179615 | bytes 198656 | tf_op jit(solution)/shard_map/blm,mbd->lbd/dot_general | solution.py:84
  125.3 2.1 %concatenate.45 = bf16[32,16,512]{2,0,1:T(8,128)(2,1)} concatenate(bf16[32,16,64]{2,0,1:T(8,128)(2,1)S(1)} %fusion.72, bf16[32,16,64]{2,0,1:T(8,128)(2,1)} %fusion.73, bf16[32,16,64]{2,0,1:T(8,128)(2,1)} %fusion.74, bf16[32,16,64]{2,0,1:T(8,128)(2,1)} %fusion.75, bf16[32,16,64]{2,0,1:T(8,128)(2,1)} %fusion.76, bf16[32,16,64]{2,0,1:T(8,128)(2,1)} %fusion.77, ...), dimensions={2} | concatenate | bytes 1048576 | tf_op jit(solution)/shard_map/concatenate | solution.py:91
  127.4 2.2 %copy.402 = bf16[32,16,512]{2,1,0:T(8,128)(2,1)} copy(bf16[32,16,512]{2,0,1:T(8,128)(2,1)} %concatenate.45) | data formatting | bytes 1048576 | tf_op jit(solution)/shard_map/concatenate | solution.py:91
  129.6 6.9 %all-to-all-start.1 = ((bf16[32,16,512]{2,1,0:T(8,128)(2,1)}), bf16[32,16,512]{2,1,0:T(8,128)(2,1)}, u32[]{:S(2)}, u32[]{:S(2)}) async-start(bf16[32,16,512]{2,1,0:T(8,128)(2,1)} %copy.402), calls=%async_computation.1 | async-start | bytes 1048576 | tf_op jit(solution)/shard_map/all_to_all | solution.py:120
  136.6 2.2 %convolution_convert_fusion.14 = bf16[2,256,64]{1,2,0:T(8,128)(2,1)} fusion(f32[2,256]{1,0:T(2,128)S(1)} %copy-done.16, bf16[2,256,512]{2,1,0:T(8,128)(2,1)} %bitcast.144, f32[2,256,256]{1,2,0:T(8,128)} %convolution_multiply_fusion.6), kind=kOutput, calls=%fused_computation.124 | convolution fusion | flops 17203968 | bytes 1247232 | tf_op jit(solution)/shard_map/blm,bmd->bld/dot_general | solution.py:84
  146.1 2.2 %convolution_convert_fusion.15 = bf16[2,256,64]{1,2,0:T(8,128)(2,1)} fusion(f32[2,256]{1,0:T(2,128)S(1)} %fusion.245, bf16[2,256,512]{2,1,0:T(8,128)(2,1)} %bitcast.145, f32[2,256,256]{1,2,0:T(8,128)} %convolution_multiply_fusion.7), kind=kOutput, calls=%fused_computation.125 | convolution fusion | flops 17203968 | bytes 1247232 | tf_op jit(solution)/shard_map/blm,bmd->bld/dot_general | solution.py:84
  151.2 2.1 %convolution_multiply_fusion = f32[2,256,256]{1,2,0:T(8,128)} fusion(bf16[2,256,512]{2,1,0:T(8,128)(2,1)} %bitcast.100, bf16[2,256,512]{2,1,0:T(8,128)(2,1)} %bitcast.116), kind=kOutput, calls=%fused_computation.70 | convolution fusion | flops 16908288 | bytes 786432 | tf_op jit(solution)/shard_map/bld,bmd->blm/dot_general | solution.py:73
  153.3 2.1 %convolution_convert_fusion.8 = bf16[2,256,64]{1,2,0:T(8,128)(2,1)} fusion(f32[2,256]{1,0:T(2,128)S(1)} %fusion.280, bf16[2,256,512]{2,1,0:T(8,128)(2,1)} %bitcast.146, f32[2,256,256]{1,2,0:T(8,128)} %convolution_multiply_fusion), kind=kOutput, calls=%fused_computation.118 | convolution fusion | flops 17203968 | bytes 1247232 | tf_op jit(solution)/shard_map/blm,bmd->bld/dot_general | solution.py:84
  157.0 1.9 %copy.403 = bf16[2,16,16,512]{3,2,1,0:T(8,128)(2,1)} copy(bf16[2,16,16,512]{3,2,0,1:T(8,128)(2,1)} %bitcast.37) | data formatting | bytes 1048576 | tf_op jit(solution)/shard_map/all_to_all | solution.py:120
  158.9 3.5 %concatenate.47 = bf16[512,1024]{1,0:T(8,128)(2,1)} concatenate(bf16[512,64]{1,0:T(8,128)(2,1)} %bitcast.128, bf16[512,64]{1,0:T(8,128)(2,1)} %bitcast.127, bf16[512,64]{1,0:T(8,128)(2,1)} %bitcast.126, bf16[512,64]{1,0:T(8,128)(2,1)} %bitcast.125, bf16[512,64]{1,0:T(8,128)(2,1)S(1)} %bitcast.124, bf16[512,64]{1,0:T(8,128)(2,1)S(1)} %bitcast.123, bf16[512,64]{1,0:T(8,128)(2,1)S(1)} %bitcast.122, ...), dimensions={1} | concatenate | bytes 2097152 | tf_op jit(solution)/shard_map/concatenate | solution.py:121
  162.4 3.5 %fusion.33 = bf16[512,1024]{1,0:T(8,128)(2,1)} fusion(bf16[2,256,1024]{2,1,0:T(8,128)(2,1)S(1)} %get-tuple-element.6, bf16[512,1024]{1,0:T(8,128)(2,1)} %concatenate.47, bf16[1024,1024]{1,0:T(8,128)(2,1)S(1)} %copy-done, f32[1024]{0:T(1024)S(1)} %copy-done.12), kind=kOutput, calls=%fused_computation.38 | convolution fusion | flops 1075838976 | bytes 5246976 | tf_op jit(solution)/shard_map/dot_general | solution.py:124
  (75 shorter events, 41.8 us)
Async XLA Ops:
  0.0 162.4 %copy-start = (bf16[1024,1024]{1,0:T(8,128)(2,1)S(1)}, bf16[1024,1024]{1,0:T(8,128)(2,1)}, u32[]{:S(2)}) copy-start(bf16[1024,1024]{1,0:T(8,128)(2,1)} %param.16) | copy-start | bytes 6291460
  0.0 9.7 %copy-start.1 = (bf16[2,256,1024]{2,1,0:T(8,128)(2,1)S(1)}, bf16[2,256,1024]{2,1,0:T(8,128)(2,1)}, u32[]{:S(2)}) copy-start(bf16[2,256,1024]{2,1,0:T(8,128)(2,1)} %param.9) | copy-start | bytes 3145732
  0.0 5.1 %copy-start.8 = (f32[3072]{0:T(1024)S(1)}, f32[3072]{0:T(1024)}, u32[]{:S(2)}) copy-start(f32[3072]{0:T(1024)} %param.15) | copy-start | bytes 36868
  0.0 5.2 %copy-start.7 = (f32[3,3,1024]{2,1,0:T(4,128)S(1)}, f32[3,3,1024]{2,1,0:T(4,128)}, u32[]{:S(2)}) copy-start(f32[3,3,1024]{2,1,0:T(4,128)} %param.10) | copy-start | bytes 110596
  1.4 3.9 %collective-permute-start = (bf16[1,256,1024]{2,1,0:T(8,128)(2,1)S(1)}, bf16[1,256,1024]{2,1,0:T(8,128)(2,1)S(1)}, u32[]{:S(2)}, u32[]{:S(2)}) collective-permute-start(bf16[1,256,1024]{2,1,0:T(8,128)(2,1)S(1)} %get-tuple-element.7), channel_id=1, source_target_pairs={{0,1},{1,2},{2,3},{3,4},{4,5},{5,6},{6,7},{7,8},{8,9},{9,10},{10,1... | collective-permute-start | bytes 1572872 | tf_op jit(solution)/shard_map/ppermute | solution.py:20
  3.8 5.9 %collective-permute-start.1 = (bf16[1,256,1024]{2,1,0:T(8,128)(2,1)S(1)}, bf16[1,256,1024]{2,1,0:T(8,128)(2,1)S(1)}, u32[]{:S(2)}, u32[]{:S(2)}) collective-permute-start(bf16[1,256,1024]{2,1,0:T(8,128)(2,1)S(1)} %get-tuple-element.8), channel_id=1, source_target_pairs={{1,0},{2,1},{3,2},{4,3},{5,4},{6,5},{7,6},{8,7},{9,8},{10,9},{11,1... | collective-permute-start | bytes 1572872 | tf_op jit(solution)/shard_map/ppermute | solution.py:21
  5.2 5.2 %copy-start.9 = (f32[1024]{0:T(1024)S(1)}, f32[1024]{0:T(1024)}, u32[]{:S(2)}) copy-start(f32[1024]{0:T(1024)} %param.11) | copy-start | bytes 12292
  10.4 3.1 %copy-start.10 = (f32[1024]{0:T(1024)S(1)}, f32[1024]{0:T(1024)}, u32[]{:S(2)}) copy-start(f32[1024]{0:T(1024)} %param.13) | copy-start | bytes 12292
  10.4 3.1 %copy-start.11 = (f32[1024]{0:T(1024)S(1)}, f32[1024]{0:T(1024)}, u32[]{:S(2)}) copy-start(f32[1024]{0:T(1024)} %param.12) | copy-start | bytes 12292
  14.0 5.9 %copy-start.2 = (bf16[2,256,1024]{2,1,0:T(8,128)(2,1)}, bf16[2,256,1024]{2,1,0:T(8,128)(2,1)S(1)}, u32[]{:S(2)}) copy-start(bf16[2,256,1024]{2,1,0:T(8,128)(2,1)S(1)} %add_convert_fusion) | copy-start | bytes 3145732
  26.7 4.2 %copy-start.3 = (bf16[2,256,1024]{2,1,0:T(8,128)(2,1)S(1)}, bf16[2,256,1024]{2,1,0:T(8,128)(2,1)}, u32[]{:S(2)}) copy-start(bf16[2,256,1024]{2,1,0:T(8,128)(2,1)} %copy-done.2) | copy-start | bytes 3145732
  35.6 37.6 %all-to-all-start = ((bf16[2,256,1024]{2,0,1:T(2,128)(2,1)}), bf16[2,256,1024]{2,0,1:T(2,128)(2,1)}, u32[]{:S(2)}, u32[]{:S(2)}) async-start(bf16[2,256,1024]{2,0,1:T(2,128)(2,1)} %copy.367), calls=%async_computation | async-start | bytes 2097152 | tf_op jit(solution)/shard_map/all_to_all | solution.py:108
  74.9 4.3 %copy-start.4 = (bf16[16,2,16,1024]{3,2,1,0:T(8,128)(2,1)}, bf16[16,2,16,1024]{3,2,1,0:T(8,128)(2,1)S(1)}, u32[]{:S(2)}) copy-start(bf16[16,2,16,1024]{3,2,1,0:T(8,128)(2,1)S(1)} %copy.369) | copy-start | bytes 3145732
  111.9 6.1 %copy-start.13 = (f32[16,32]{1,0:T(8,128)S(1)}, f32[16,32]{1,0:T(8,128)}, u32[]{:S(2)}) copy-start(f32[16,32]{1,0:T(8,128)} %fusion.300) | copy-start | bytes 6148
  114.0 6.1 %copy-start.14 = (f32[16,32]{1,0:T(8,128)S(1)}, f32[16,32]{1,0:T(8,128)}, u32[]{:S(2)}) copy-start(f32[16,32]{1,0:T(8,128)} %fusion.295) | copy-start | bytes 6148
  120.0 4.0 %copy-start.15 = (f32[16,32]{1,0:T(8,128)S(1)}, f32[16,32]{1,0:T(8,128)}, u32[]{:S(2)}) copy-start(f32[16,32]{1,0:T(8,128)} %fusion.285) | copy-start | bytes 6148
  125.3 11.2 %copy-start.16 = (f32[2,256]{1,0:T(2,128)S(1)}, f32[2,256]{1,0:T(2,128)}, u32[]{:S(2)}) copy-start(f32[2,256]{1,0:T(2,128)} %fusion.250) | copy-start | bytes 6148
  127.4 11.3 %copy-start.5 = (bf16[2,256,64]{1,2,0:T(8,128)(2,1)S(1)}, bf16[2,256,64]{1,2,0:T(8,128)(2,1)}, u32[]{:S(2)}) copy-start(bf16[2,256,64]{1,2,0:T(8,128)(2,1)} %convolution_convert_fusion.9) | copy-start | bytes 196612
  127.4 11.4 %copy-start.6 = (bf16[2,256,64]{1,2,0:T(8,128)(2,1)S(1)}, bf16[2,256,64]{1,2,0:T(8,128)(2,1)}, u32[]{:S(2)}) copy-start(bf16[2,256,64]{1,2,0:T(8,128)(2,1)} %convolution_convert_fusion.10) | copy-start | bytes 196612
  129.6 27.4 %all-to-all-start.1 = ((bf16[32,16,512]{2,1,0:T(8,128)(2,1)}), bf16[32,16,512]{2,1,0:T(8,128)(2,1)}, u32[]{:S(2)}, u32[]{:S(2)}) async-start(bf16[32,16,512]{2,1,0:T(8,128)(2,1)} %copy.402), calls=%async_computation.1 | async-start | bytes 1048576 | tf_op jit(solution)/shard_map/all_to_all | solution.py:120
  155.4 7.0 %copy-start.12 = (f32[1024]{0:T(1024)S(1)}, f32[1024]{0:T(1024)}, u32[]{:S(2)}) copy-start(f32[1024]{0:T(1024)} %param.17) | copy-start | bytes 12292
where the time goes:
time: 168 us; the launch traced here: 166 us
  matrix products  105 us (62%)
  local copies, waits for them, and re-layouts  26.5 us (16%)
  starting transfers between devices  25.3 us (15%)
  waiting for transfers between devices  4.53 us (3%)
  other arithmetic  4.12 us (2%)
    dot_general x16, matrix products, attend_heads(): jnp.einsum(mixing_equation, attention_weights, value_operand, preferred_e...  31.9 us
    dot_general x16, matrix products, attend_heads(): jnp.einsum(scoring_equation, query_rows, key_operand, preferred_element_t...  30.3 us
    sub x16, matrix products, attend_heads(): attention_weights = jnp.exp(attention_logits - highest)  24.3 us
    dot_general x6, matrix products, project_three(): jnp.dot(flat_rows, qkv_weight[:, lower:upper], preferred_element_type=jnp...  15.1 us
    all_to_all x1, starting transfers between devices, on_device(): lax.all_to_all(normed, 'rows', split_axis=1, concat_axis=0, tiled=True)  14.6 us
    concatenate x9, local copies, waits for them, and re-layouts, on_device(): jnp.concatenate([row_heads, returned], axis=2).reshape(bands * width, model)  12.6 us
    all_to_all x1, starting transfers between devices, on_device(): lax.all_to_all(col_heads, 'rows', split_axis=0, concat_axis=1, tiled=True)  6.93 us
    ppermute x1, waiting for transfers between devices, with_halo(): after = lax.ppermute(leading, axis, down)  4.42 us
  transfers between devices with their start and end apart: 4, of which 2 were waited for; matrix products, arithmetic and copies ran while one was open for 26% of the time, Pallas kernels for 0%

commit v1 on v0

v1 whole, which is shorter than its diff:
```python
import functools
import math

import jax
import jax.numpy as jnp
from jax import lax
from jax.experimental import pallas as pl
from jax.experimental.pallas import tpu as pltpu
from jax.sharding import PartitionSpec as P

HEADS = 16
DH = 64
ROW_HEADS = 8
LANES = 128
SUB = 8
HALF = SUB // 2
PAIR = LANES // DH
EPS = 1e-06
LOG2E = math.log2(math.e)
MIB = 1024 * 1024


def halo_rows(tokens):
    devices, bands = lax.axis_size("rows"), tokens.shape[0]
    up = [(i, i + 1) for i in range(devices - 1)]
    down = [(j, i) for i, j in up]
    before = lax.ppermute(tokens[bands - 1 :], "rows", up)
    after = lax.ppermute(tokens[:1], "rows", down)
    return before, after


def plain_convolve(padded, peg_weight, peg_bias, count_rows, count_cols):
    total = padded[1 : count_rows + 1, 1 : count_cols + 1, :].astype(jnp.float32) + peg_bias
    for offset_row in range(3):
        for offset_col in range(3):
            piece = padded[
                offset_row : offset_row + count_rows, offset_col : offset_col + count_cols, :
            ]
            total = total + piece.astype(jnp.float32) * peg_weight[offset_row, offset_col]
    return total.astype(jnp.bfloat16)


def plain_layer_norm(mixed, norm_gain, norm_bias):
    values = mixed.astype(jnp.float32)
    center = jnp.mean(values, axis=-1, keepdims=True)
    spread = jnp.mean((values - center) ** 2, axis=-1, keepdims=True)
    return ((values - center) * lax.rsqrt(spread + EPS) * norm_gain + norm_bias).astype(
        jnp.bfloat16
    )


def plain_project(normed, qkv_weight, qkv_bias, first_col, last_col):
    model = normed.shape[-1]
    flat_rows = normed.reshape(-1, model)
    outputs = []
    for part_index in range(3):
        lower = part_index * model + first_col
        upper = part_index * model + last_col
        projected = (
            jnp.dot(flat_rows, qkv_weight[:, lower:upper], preferred_element_type=jnp.float32)
            + qkv_bias[lower:upper]
        )
        outputs.append(
            projected.astype(jnp.bfloat16).reshape(normed.shape[:-1] + (last_col - first_col,))
        )
    return outputs


def plain_attend(query, key, value, head_count, tau, scoring, mixing):
    outputs = []
    for head in range(head_count):
        cols = slice(head * DH, (head + 1) * DH)
        logits = (
            jnp.einsum(
                scoring, query[..., cols], key[..., cols], preferred_element_type=jnp.float32
            )
            * tau
        )
        probs = jnp.exp(logits - jnp.max(logits, axis=-1, keepdims=True))
        probs = (probs / jnp.sum(probs, axis=-1, keepdims=True)).astype(jnp.bfloat16)
        outputs.append(
            jnp.einsum(
                mixing, probs, value[..., cols], preferred_element_type=jnp.float32
            ).astype(jnp.bfloat16)
        )
    return jnp.concatenate(outputs, axis=-1)


def plain(
    tokens, peg_weight, peg_bias, norm_gain, norm_bias, qkv_weight, qkv_bias, out_weight, out_bias
):
    bands, width, model = tokens.shape
    height = bands * lax.axis_size("rows")
    row_features = ROW_HEADS * DH
    before, after = halo_rows(tokens)
    padded = jnp.pad(
        jnp.concatenate([before, tokens, after], axis=0), ((0, 0), (1, 1), (0, 0))
    )
    mixed = plain_convolve(padded, peg_weight, peg_bias, bands, width)
    normed = plain_layer_norm(mixed, norm_gain, norm_bias)
    row_qkv = plain_project(normed, qkv_weight, qkv_bias, 0, row_features)
    arrived = lax.all_to_all(normed, "rows", split_axis=1, concat_axis=0, tiled=True)
    col_qkv = plain_project(arrived, qkv_weight, qkv_bias, row_features, model)
    row_heads = plain_attend(
        *row_qkv, ROW_HEADS, score_scale(width), "bld,bmd->blm", "blm,bmd->bld"
    )
    col_heads = plain_attend(
        *col_qkv, HEADS - ROW_HEADS, score_scale(height), "lbd,mbd->blm", "blm,mbd->lbd"
    )
    returned = lax.all_to_all(col_heads, "rows", split_axis=0, concat_axis=1, tiled=True)
    attended = jnp.concatenate([row_heads, returned], axis=2).reshape(bands * width, model)
    result = (
        mixed.reshape(bands * width, model).astype(jnp.float32)
        + jnp.dot(attended, out_weight, preferred_element_type=jnp.float32)
        + out_bias
    )
    return result.astype(jnp.bfloat16).reshape(bands, width, model)


def score_scale(count):
    return math.log(count) / (math.log(16.0) * math.sqrt(DH))


def interleave(first, second):
    upper = lax.broadcasted_iota(jnp.int32, first.shape, 0) < HALF
    low = jnp.where(upper, first, pltpu.roll(second, HALF, 0))
    high = jnp.where(upper, pltpu.roll(first, HALF, 0), second)
    return low, high


def pack_kernel(devices, per_step, own_ref, left_ref, right_ref, out_ref):
    model = own_ref.shape[2]
    cols = own_ref.shape[1] // per_step
    slabs = model // LANES
    tiles = cols // HALF
    step = pl.program_id(0)
    place = lax.broadcasted_iota(jnp.int32, (SUB, LANES), 0)
    for k in range(per_step):
        dest = step * per_step + k
        for eight in range(cols // SUB):
            start = k * cols + eight * SUB
            pair = interleave(
                own_ref[0, start : start + SUB, :].astype(jnp.float32),
                own_ref[1, start : start + SUB, :].astype(jnp.float32),
            )
            for which in range(2):
                tile = pair[which].astype(jnp.bfloat16)
                for slab in range(slabs):
                    base = (slab * tiles + eight * 2 + which) * SUB
                    out_ref[k, base : base + SUB, :] = tile[:, slab * LANES : (slab + 1) * LANES]
        lefts, rights = [], []
        for band in range(2):
            if k == 0:
                left = left_ref[band].astype(jnp.float32)[cols - 1 : cols]
            else:
                left = own_ref[band, (k - 1) * cols : k * cols, :].astype(jnp.float32)
                left = left[cols - 1 : cols]
            if k == per_step - 1:
                right = right_ref[band].astype(jnp.float32)[0:1]
            else:
                right = own_ref[band, (k + 1) * cols : (k + 2) * cols, :]
                right = right.astype(jnp.float32)[0:1]
            lefts.append(jnp.where(dest > 0, left, 0.0))
            rights.append(jnp.where(dest < devices - 1, right, 0.0))
        for two in range(slabs // 2):
            one = slice(2 * two * LANES, (2 * two + 1) * LANES)
            other = slice((2 * two + 1) * LANES, (2 * two + 2) * LANES)
            order = [rights[0][:, one], rights[0][:, other], lefts[0][:, other], lefts[0][:, one]]
            order += [rights[1][:, one], rights[1][:, other], lefts[1][:, other], lefts[1][:, one]]
            tile = jnp.broadcast_to(order[0], (SUB, LANES))
            for index in range(1, SUB):
                tile = jnp.where(place == index, order[index], tile)
            base = (slabs * tiles + two) * SUB
            out_ref[k, base : base + SUB, :] = tile.astype(jnp.bfloat16)


def pack(tokens, devices):
    bands, width, model = tokens.shape
    cols = width // devices
    slabs = model // LANES
    rows = slabs * bands * (cols + 2)
    per_step = 4
    last = devices - 1
    return pl.pallas_call(
        functools.partial(pack_kernel, devices, per_step),
        grid=(devices // per_step,),
        in_specs=[
            pl.BlockSpec((bands, per_step * cols, model), lambda i: (0, i, 0)),
            pl.BlockSpec(
                (bands, cols, model), lambda i: (0, jnp.maximum(i * per_step - 1, 0), 0)
            ),
            pl.BlockSpec(
                (bands, cols, model), lambda i: (0, jnp.minimum((i + 1) * per_step, last), 0)
            ),
        ],
        out_specs=pl.BlockSpec((per_step, rows, LANES), lambda i: (i, 0, 0)),
        out_shape=jax.ShapeDtypeStruct((devices, rows, LANES), jnp.bfloat16),
        compiler_params=pltpu.CompilerParams(vmem_limit_bytes=6 * MIB),
        name="pack_columns",
    )(*[in_hbm(tokens)] * 3)


def gate_kernel(*refs):
    pass


def gate(values, *after):
    hbm = pl.BlockSpec(memory_space=pltpu.HBM)
    anywhere = pl.BlockSpec(memory_space=pl.ANY)
    count = len(values)
    return pl.pallas_call(
        gate_kernel,
        in_specs=[hbm] * count + [anywhere] * len(after),
        out_specs=[hbm] * count,
        out_shape=[jax.ShapeDtypeStruct(value.shape, value.dtype) for value in values],
        input_output_aliases={index: index for index in range(count)},
        name="gate",
    )(*values, *after)


def in_hbm(value):
    return pltpu.with_memory_space_constraint(value, pltpu.HBM)


def normalise(values, gain, bias):
    center = jnp.mean(values, axis=-1, keepdims=True)
    shifted = values - center
    spread = jnp.mean(shifted * shifted, axis=-1, keepdims=True)
    return (shifted * lax.rsqrt(spread + EPS) * gain + bias).astype(jnp.bfloat16)


def attend_pair(query, key, value, scale, mask):
    count = query.shape[0]
    lane = lax.broadcasted_iota(jnp.int32, query.shape, 1)
    zero = jnp.zeros_like(query)
    both = jnp.concatenate(
        [jnp.where(lane < DH, query, zero), jnp.where(lane < DH, zero, query)], axis=0
    )
    scores = lax.dot_general(
        both, key, (((1,), (1,)), ((), ())), preferred_element_type=jnp.float32
    )
    if mask is not None:
        scores = jnp.where(mask, scores, -1e30)
    highest = jnp.max(scores, axis=-1, keepdims=True)
    probs = jnp.exp2((scores - highest) * (scale * LOG2E))
    total = jnp.sum(probs, axis=-1, keepdims=True)
    probs = (probs * (1.0 / total)).astype(jnp.bfloat16)
    mixed = jnp.dot(probs, value, preferred_element_type=jnp.float32)
    return jnp.where(lane < DH, mixed[:count], mixed[count:])


def weight_copies(qkv_hbm, weight_scr, sems, first):
    model = qkv_hbm.shape[0]
    width = weight_scr.shape[2]
    return [
        pltpu.make_async_copy(
            qkv_hbm.at[:, pl.ds(part * model + first, width)], weight_scr.at[part], sems.at[part]
        )
        for part in range(3)
    ]


def column_kernel(
    recv_ref,
    edge_ref,
    peg_ref,
    peg_bias_ref,
    gain_ref,
    nbias_ref,
    qkv_bias_ref,
    qkv_hbm,
    out_ref,
    mixed_scr,
    normed_scr,
    qkv_scr,
    weight_scr,
    sems,
):
    step = pl.program_id(0)
    devices = recv_ref.shape[0]
    tiles = recv_ref.shape[1] // (2 * SUB)
    height = 2 * devices
    first = ROW_HEADS * DH
    features = weight_scr.shape[2]
    group = devices * SUB

    @pl.when(step == 0)
    def _():
        for copy in weight_copies(qkv_hbm, weight_scr, sems, first):
            copy.start()

    place = lax.broadcasted_iota(jnp.int32, (1, 1, SUB, LANES), 2)
    upper = place < HALF
    column = lax.rem(place, HALF)

    def with_neighbours(value):
        swapped = pltpu.roll(value, HALF, 2)
        zero = jnp.zeros((1,) + value.shape[1:], jnp.float32)
        between = jnp.where(
            upper,
            jnp.concatenate([zero, swapped], axis=0),
            jnp.concatenate([swapped, zero], axis=0),
        )
        return between[:-1], value, between[1:]

    def stencil(triple, lanes, offset_col):
        total = None
        for offset_row in range(3):
            weight = peg_ref[offset_row, offset_col : offset_col + 1, lanes]
            term = triple[offset_row] * weight
            total = term if total is None else total + term
        return total

    edges = edge_ref[...].astype(jnp.float32).reshape(devices, 1, SUB, LANES)
    for local in range(2):
        lanes = slice(local * LANES, (local + 1) * LANES)
        own = recv_ref[:, local * tiles * SUB : (local + 1) * tiles * SUB, :]
        own = own.astype(jnp.float32).reshape(devices, tiles, SUB, LANES)
        triple = with_neighbours(own)
        if local == 0:
            left_edge = right_edge = with_neighbours(edges)
        else:
            left_edge = with_neighbours(pltpu.roll(edges, 1, 2))
            right_edge = with_neighbours(pltpu.roll(edges, SUB - 1, 2))
        wide = jnp.concatenate(
            [stencil(left_edge, lanes, 0), stencil(triple, lanes, 0)], axis=1
        )
        from_left = jnp.where(
            column == 0, pltpu.roll(wide[:, :-1], SUB - 3, 2), pltpu.roll(wide[:, 1:], 1, 2)
        )
        wide = jnp.concatenate(
            [stencil(triple, lanes, 2), stencil(right_edge, lanes, 2)], axis=1
        )
        from_right = jnp.where(
            column == HALF - 1,
            pltpu.roll(wide[:, 1:], 3, 2),
            pltpu.roll(wide[:, :-1], SUB - 1, 2),
        )
        total = (
            own + peg_bias_ref[:, lanes] + stencil(triple, lanes, 1) + from_left + from_right
        )
        mixed_scr[2 * step + local] = total.astype(jnp.bfloat16).astype(jnp.float32)

    @pl.when(step == pl.num_programs(0) - 1)
    def _():
        count = mixed_scr.shape[0]
        for tile in range(tiles):
            for start in range(0, devices, HALF):
                values = jnp.concatenate(
                    [
                        mixed_scr[slab, start : start + HALF, tile].reshape(HALF * SUB, LANES)
                        for slab in range(count)
                    ],
                    axis=1,
                )
                base = tile * group + start * SUB
                normed_scr[base : base + HALF * SUB, :] = normalise(
                    values, gain_ref[...], nbias_ref[...]
                )
        for part, copy in enumerate(weight_copies(qkv_hbm, weight_scr, sems, first)):
            copy.wait()
            projected = (
                jnp.dot(normed_scr[...], weight_scr[part], preferred_element_type=jnp.float32)
                + qkv_bias_ref[part : part + 1, :]
            )
            qkv_scr[part] = projected.astype(jnp.bfloat16)
        row_id = lax.broadcasted_iota(jnp.int32, (PAIR * group, group), 0)
        col_id = lax.broadcasted_iota(jnp.int32, (PAIR * group, group), 1)
        mask = lax.rem(row_id, HALF) == lax.rem(col_id, HALF)
        scale = score_scale(height)
        for tile in range(tiles):
            rows = slice(tile * group, (tile + 1) * group)
            for pair in range(features // LANES):
                lanes = slice(pair * LANES, (pair + 1) * LANES)
                heads = attend_pair(
                    qkv_scr[0, rows, lanes],
                    qkv_scr[1, rows, lanes],
                    qkv_scr[2, rows, lanes],
                    scale,
                    mask,
                )
                out_ref[:, tile, :, lanes] = heads.astype(jnp.bfloat16).reshape(
                    devices, SUB, LANES
                )


def column_part(recv, peg_weight, peg_bias, gain, nbias, qkv_weight, qkv_bias):
    devices, rows, _ = recv.shape
    model = gain.shape[-1]
    slabs = model // LANES
    cols = rows // (2 * slabs) - 2
    tiles = cols // HALF
    first = ROW_HEADS * DH
    features = model - first
    tokens = 2 * devices * cols
    whole2 = lambda i: (0, 0)
    steps = slabs // 2
    return pl.pallas_call(
        column_kernel,
        grid=(steps,),
        in_specs=[
            pl.BlockSpec((devices, 2 * tiles * SUB, LANES), lambda i: (0, i, 0)),
            pl.BlockSpec((devices, SUB, LANES), lambda i: (0, slabs * tiles + i, 0)),
            pl.BlockSpec((3, 3, 2 * LANES), lambda i: (0, 0, i)),
            pl.BlockSpec((1, 2 * LANES), lambda i: (0, i)),
            pl.BlockSpec((1, model), whole2),
            pl.BlockSpec((1, model), whole2),
            pl.BlockSpec((3, features), whole2),
            pl.BlockSpec(memory_space=pltpu.HBM),
        ],
        out_specs=pl.BlockSpec((devices, tiles, SUB, features), lambda i: (0, 0, 0, 0)),
        out_shape=pltpu.HBM((devices, tiles, SUB, features), jnp.bfloat16),
        scratch_shapes=[
            pltpu.VMEM((slabs, devices, tiles, SUB, LANES), jnp.float32),
            pltpu.VMEM((tokens, model), jnp.bfloat16),
            pltpu.VMEM((3, tokens, features), jnp.bfloat16),
            pltpu.VMEM((3, model, features), jnp.bfloat16),
            pltpu.SemaphoreType.DMA((3,)),
        ],
        compiler_params=pltpu.CompilerParams(vmem_limit_bytes=20 * MIB),
        cost_estimate=pl.CostEstimate(
            flops=2 * tokens * model * 3 * features,
            transcendentals=tokens * LANES * features // DH,
            bytes_accessed=8 * MIB,
        ),
        name="column_heads",
    )(recv, recv, peg_weight, peg_bias, gain, nbias, qkv_bias[:, first:], in_hbm(qkv_weight))


def row_kernel(
    tokens_ref,
    intra_ref,
    inter_ref,
    peg_ref,
    peg_bias_ref,
    gain_ref,
    nbias_ref,
    qkv_bias_ref,
    out_bias_ref,
    qkv_hbm,
    out_hbm,
    partial_ref,
    mixed_scr,
    normed_scr,
    qkv_scr,
    heads_scr,
    weight_scr,
    out_scr,
    sems,
):
    step = pl.program_id(0)
    slabs = pl.num_programs(0)
    bands, width, _ = tokens_ref.shape
    features = weight_scr.shape[2]

    def copies():
        copy = pltpu.make_async_copy(out_hbm.at[pl.ds(0, features), :], out_scr, sems.at[3])
        return weight_copies(qkv_hbm, weight_scr, sems, 0) + [copy]

    @pl.when(step == 0)
    def _():
        for copy in copies():
            copy.start()

    odd = lax.rem(lax.axis_index("rows"), 2) == 1
    intra = intra_ref[0].astype(jnp.float32)
    inter = inter_ref[0].astype(jnp.float32)
    rows = [jnp.where(odd, intra, inter)]
    rows += [tokens_ref[band].astype(jnp.float32) for band in range(bands)]
    rows += [jnp.where(odd, inter, intra)]
    position = lax.broadcasted_iota(jnp.int32, (width, LANES), 0)
    for band in range(bands):

        def stencil(offset_col):
            return (
                rows[band] * peg_ref[0, offset_col : offset_col + 1, :]
                + rows[band + 1] * peg_ref[1, offset_col : offset_col + 1, :]
                + rows[band + 2] * peg_ref[2, offset_col : offset_col + 1, :]
            )

        from_left = jnp.where(position == 0, 0.0, pltpu.roll(stencil(0), 1, 0))
        from_right = jnp.where(position == width - 1, 0.0, pltpu.roll(stencil(2), width - 1, 0))
        total = rows[band + 1] + peg_bias_ref[...] + stencil(1) + from_left + from_right
        mixed_scr[step, band * width : (band + 1) * width, :] = total.astype(
            jnp.bfloat16
        ).astype(jnp.float32)

    @pl.when(step == slabs - 1)
    def _():
        count = mixed_scr.shape[0]
        chunk = 64
        for start in range(0, bands * width, chunk):
            values = jnp.concatenate(
                [mixed_scr[slab, start : start + chunk, :] for slab in range(count)], axis=1
            )
            normed_scr[start : start + chunk, :] = normalise(
                values, gain_ref[...], nbias_ref[...]
            )
        waits = copies()
        for part in range(3):
            waits[part].wait()
            projected = (
                jnp.dot(normed_scr[...], weight_scr[part], preferred_element_type=jnp.float32)
                + qkv_bias_ref[part : part + 1, :]
            )
            qkv_scr[part] = projected.astype(jnp.bfloat16)
        scale = score_scale(width)
        for band in range(bands):
            span = slice(band * width, (band + 1) * width)
            for pair in range(features // LANES):
                lanes = slice(pair * LANES, (pair + 1) * LANES)
                heads_scr[span, lanes] = attend_pair(
                    qkv_scr[0, span, lanes],
                    qkv_scr[1, span, lanes],
                    qkv_scr[2, span, lanes],
                    scale,
                    None,
                ).astype(jnp.bfloat16)
        waits[3].wait()
        for slab in range(count):
            lanes = slice(slab * LANES, (slab + 1) * LANES)
            partial_ref[:, lanes] = (
                jnp.dot(heads_scr[...], out_scr[:, lanes], preferred_element_type=jnp.float32)
                + mixed_scr[slab]
                + out_bias_ref[:, lanes]
            )


def row_part(
    tokens,
    intra,
    inter,
    peg_weight,
    peg_bias,
    gain,
    nbias,
    qkv_weight,
    qkv_bias,
    out_weight,
    out_bias,
):
    bands, width, model = tokens.shape
    slabs = model // LANES
    features = ROW_HEADS * DH
    count = bands * width
    whole2 = lambda i: (0, 0)
    return pl.pallas_call(
        row_kernel,
        grid=(slabs,),
        in_specs=[
            pl.BlockSpec((bands, width, LANES), lambda i: (0, 0, i)),
            pl.BlockSpec((1, width, LANES), lambda i: (0, 0, i)),
            pl.BlockSpec((1, width, LANES), lambda i: (0, 0, i)),
            pl.BlockSpec((3, 3, LANES), lambda i: (0, 0, i)),
            pl.BlockSpec((1, LANES), lambda i: (0, i)),
            pl.BlockSpec((1, model), whole2),
            pl.BlockSpec((1, model), whole2),
            pl.BlockSpec((3, features), whole2),
            pl.BlockSpec((1, model), whole2),
            pl.BlockSpec(memory_space=pltpu.HBM),
            pl.BlockSpec(memory_space=pltpu.HBM),
        ],
        out_specs=pl.BlockSpec((count, model), whole2),
        out_shape=pltpu.HBM((count, model), jnp.float32),
        scratch_shapes=[
            pltpu.VMEM((slabs, count, LANES), jnp.float32),
            pltpu.VMEM((count, model), jnp.bfloat16),
            pltpu.VMEM((3, count, features), jnp.bfloat16),
            pltpu.VMEM((count, features), jnp.bfloat16),
            pltpu.VMEM((3, model, features), jnp.bfloat16),
            pltpu.VMEM((features, model), jnp.bfloat16),
            pltpu.SemaphoreType.DMA((4,)),
        ],
        compiler_params=pltpu.CompilerParams(vmem_limit_bytes=20 * MIB),
        cost_estimate=pl.CostEstimate(
            flops=2 * count * model * 4 * features,
            transcendentals=count * width * ROW_HEADS,
            bytes_accessed=10 * 1024 * 1024,
        ),
        name="row_heads",
    )(
        tokens,
        intra,
        inter,
        peg_weight,
        peg_bias,
        gain,
        nbias,
        qkv_bias[:, :features],
        out_bias,
        in_hbm(qkv_weight),
        in_hbm(out_weight),
    )


def last_kernel(partial_ref, heads_ref, out_weight_ref, result_ref):
    devices, tiles, sub, features = heads_ref.shape
    lanes = result_ref.shape[2]
    heads = heads_ref[...].reshape(devices * tiles * sub, features)
    projected = jnp.dot(heads, out_weight_ref[...], preferred_element_type=jnp.float32)
    pairs = projected.reshape(devices * tiles // 2, 2, sub, lanes)
    low, high = pairs[:, 0], pairs[:, 1]
    upper = lax.broadcasted_iota(jnp.int32, (1, sub, lanes), 1) < HALF
    first = jnp.where(upper, low, pltpu.roll(high, HALF, 1))
    second = jnp.where(upper, pltpu.roll(low, HALF, 1), high)
    width = result_ref.shape[1]
    for band, value in enumerate((first, second)):
        result_ref[band] = (
            partial_ref[band * width : (band + 1) * width, :] + value.reshape(width, lanes)
        ).astype(jnp.bfloat16)


def last_part(partial, heads, out_weight, bands, width):
    devices, tiles, sub, features = heads.shape
    model = out_weight.shape[1]
    first = ROW_HEADS * DH
    lanes = model // 4
    return pl.pallas_call(
        last_kernel,
        grid=(model // lanes,),
        in_specs=[
            pl.BlockSpec((bands * width, lanes), lambda i: (0, i)),
            pl.BlockSpec((devices, tiles, sub, features), lambda i: (0, 0, 0, 0)),
            pl.BlockSpec((features, lanes), lambda i: (first // features, i)),
        ],
        out_specs=pl.BlockSpec((bands, width, lanes), lambda i: (0, 0, i)),
        out_shape=jax.ShapeDtypeStruct((bands, width, model), jnp.bfloat16),
        compiler_params=pltpu.CompilerParams(vmem_limit_bytes=10 * MIB),
        cost_estimate=pl.CostEstimate(
            flops=2 * bands * width * features * model,
            transcendentals=0,
            bytes_accessed=5 * MIB,
        ),
        name="last_projection",
    )(in_hbm(partial), heads, out_weight)


def on_device(
    tokens, peg_weight, peg_bias, norm_gain, norm_bias, qkv_weight, qkv_bias, out_weight, out_bias
):
    devices = lax.axis_size("rows")
    bands, width, model = tokens.shape
    cols = width // devices
    fits = (
        bands == 2
        and width % LANES == 0
        and cols % 16 == 0
        and devices * SUB == LANES
        and model == 2 * ROW_HEADS * DH
        and model % LANES == 0
    )
    if not fits:
        return plain(
            tokens,
            peg_weight,
            peg_bias,
            norm_gain,
            norm_bias,
            qkv_weight,
            qkv_bias,
            out_weight,
            out_bias,
        )
    peg_bias = peg_bias.reshape(1, model)
    gain = norm_gain.reshape(1, model)
    nbias = norm_bias.reshape(1, model)
    out_bias = out_bias.reshape(1, model)
    qkv_bias = qkv_bias.reshape(3, model)

    packed = pack(tokens, devices)
    received = lax.all_to_all(packed, "rows", split_axis=0, concat_axis=0, tiled=True)
    odd = lax.rem(lax.axis_index("rows"), 2)
    intra = lax.dynamic_slice_in_dim(tokens, 1 - odd, 1, axis=0)
    inter = lax.dynamic_slice_in_dim(tokens, odd, 1, axis=0)
    intra, inter = gate((intra, inter), received[0, :SUB])
    same_chip = [(i, i ^ 1) for i in range(devices)]
    other_chip = [(i, i + 1 if i % 2 else i - 1) for i in range(1, devices - 1)]
    intra = lax.ppermute(intra, "rows", same_chip)
    inter = lax.ppermute(inter, "rows", other_chip)
    col_heads = column_part(
        received, peg_weight, peg_bias, gain, nbias, qkv_weight, qkv_bias
    )
    (col_heads,) = gate((col_heads,), intra[0, :SUB, :LANES], inter[0, :SUB, :LANES])
    returned = lax.all_to_all(col_heads, "rows", split_axis=0, concat_axis=0, tiled=True)
    partial = row_part(
        tokens,
        intra,
        inter,
        peg_weight,
        peg_bias,
        gain,
        nbias,
        qkv_weight,
        qkv_bias,
        out_weight,
        out_bias,
    )
    return last_part(partial, returned, out_weight, bands, width)


def solution(mesh):
    placed = (P(("groups", "rows"), None, None), P(), P(), P(), P(), P(), P(), P(), P())
    return jax.shard_map(
        on_device,
        mesh=mesh,
        in_specs=placed,
        out_specs=P(("groups", "rows"), None, None),
        check_vma=False,
    )
```

time: 168 us -> 81.2 us (0.48)
  matrix products: 105 us -> 0 us
  Pallas kernels: 0 us -> 26.4 us
  waiting for transfers between devices: 4.53 us -> 25.8 us
  local copies, waits for them, and re-layouts: 26.5 us -> 5.77 us
  other arithmetic: 4.12 us -> 0 us
  starting transfers between devices: 25.3 us -> 22.5 us
    dot_general x39 -> x0, matrix products: 80.9 us -> none  [the longest x16 31.9 us: attend_heads(): jnp.einsum(mixing_equation, attention_weights, value_operand, preferred_e...]
    pallas_call x0 -> x6, Pallas kernels: none -> 26.4 us  [the longest x1 10.6 us: row_part(): pl.pallas_call(row_kernel, grid=(slabs,), in_specs=[pl.BlockSpec((bands,...]
    all_to_all x2, waiting for transfers between devices: 0.01 us -> 25.8 us  [the longest x1 24 us: on_device(): lax.all_to_all(packed, 'rows', split_axis=0, concat_axis=0, tiled=True)]
    sub x16 -> x0, matrix products: 24.3 us -> none  [attend_heads(): attention_weights = jnp.exp(attention_logits - highest)]
    concatenate x11 -> x0, local copies, waits for them, and re-layouts: 16.9 us -> none  [the longest x9 12.6 us: on_device(): jnp.concatenate([row_heads, returned], axis=2).reshape(bands * width, model)]
    ppermute x2, waiting for transfers between devices: 4.52 us -> 0.01 us  [the longest x1 0.01 us: on_device(): intra = lax.ppermute(intra, 'rows', same_chip)]
    slice x5 -> x1, local copies, waits for them, and re-layouts: 3.97 us -> 0.01 us  [column_part(): qkv_bias[:, first:]]
    all_to_all x3 -> x0, local copies, waits for them, and re-layouts: 3.47 us -> none  [the longest x1 1.87 us: on_device(): lax.all_to_all(col_heads, 'rows', split_axis=0, concat_axis=1, tiled=True)]
  transfers between devices with their start and end apart: 4 -> 4, of which waited for: 2 -> 2; matrix products, arithmetic and copies ran while one was open for 26% -> 2% of each run, Pallas kernels for 0% -> 23%
where the time goes in v1:
time: 81.2 us; the launch traced here: 80.7 us
  Pallas kernels  26.4 us (33%)
  waiting for transfers between devices  25.8 us (32%)
  starting transfers between devices  22.5 us (28%)
  local copies, waits for them, and re-layouts  5.77 us (7%)
    all_to_all x1, waiting for transfers between devices, on_device(): lax.all_to_all(packed, 'rows', split_axis=0, concat_axis=0, tiled=True)  24 us
    all_to_all x1, starting transfers between devices, on_device(): lax.all_to_all(col_heads, 'rows', split_axis=0, concat_axis=0, tiled=True)  13.6 us
    pallas_call x1, Pallas kernels, row_part(): pl.pallas_call(row_kernel, grid=(slabs,), in_specs=[pl.BlockSpec((bands,...  10.6 us
    pallas_call x1, Pallas kernels, column_part(): pl.pallas_call(column_kernel, grid=(steps,), in_specs=[pl.BlockSpec((devi...  7.8 us
    all_to_all x1, starting transfers between devices, on_device(): lax.all_to_all(packed, 'rows', split_axis=0, concat_axis=0, tiled=True)  7.52 us
    pallas_call x1, Pallas kernels, last_part(): pl.pallas_call(last_kernel, grid=(model // lanes,), in_specs=[pl.BlockSpe...  4.3 us
    pallas_call x1, Pallas kernels, pack(): pl.pallas_call(functools.partial(pack_kernel, devices, per_step), grid=(d...  3.65 us
    unnamed x24, local copies, waits for them, and re-layouts  2.92 us
  transfers between devices with their start and end apart: 4, of which 2 were waited for; matrix products, arithmetic and copies ran while one was open for 2% of the time, Pallas kernels for 23%

profile of v1, /device:TPU:0, one launch (start us, length us, event | category | flops | bytes accessed | tf_op | source)
XLA Modules:
  0.0 80.7 jit_solution(17873749502357341208)
XLA Ops:
  0.0 3.7 %pack_columns.1 = bf16[16,288,128]{2,1,0:T(8,128)(2,1)} custom-call(bf16[2,256,1024]{2,1,0:T(8,128)(2,1)} %tokens_ref.1, bf16[2,256,1024]{2,1,0:T(8,128)(2,1)} %tokens_ref.1, bf16[2,256,1024]{2,1,0:T(8,128)(2,1)} %tokens_ref.1), custom_call_target="tpu_custom_call" | custom-call | tf_op jit(solution)/shard_map/pack_columns/pallas_call | solution.py:184
  3.7 0.0 copy-start
  3.7 7.5 %all-to-all-start = ((bf16[16,288,128]{2,1,0:T(8,128)(2,1)}), bf16[16,288,128]{2,1,0:T(8,128)(2,1)S(1)}, u32[]{:S(2)}, u32[]{:S(2)}) async-start(bf16[16,288,128]{2,1,0:T(8,128)(2,1)} %pack_columns.1), calls=%async_computation | async-start | bytes 2359296 | tf_op jit(solution)/shard_map/all_to_all | solution.py:671
  11.2 0.0 copy-start.11
  11.2 0.0 copy-start.6
  11.2 0.0 copy-start.7
  11.2 0.0 copy-start.8
  11.2 0.0 copy-start.9
  11.2 0.0 copy-done
  11.3 1.0 %constant_dynamic-slice_fusion = (bf16[1,256,1024]{2,1,0:T(8,128)(2,1)}, bf16[1,256,1024]{2,1,0:T(8,128)(2,1)}) fusion(bf16[2,256,1024]{2,1,0:T(8,128)(2,1)S(1)} %copy-done, s32[]{:T(128)S(6)} %select_n.7, s32[]{:T(128)S(6)} %select_n.6), kind=kLoop, calls=%fused_computation.3 | loop fusion | bytes 2097160 | tf_op jit(solution)/shard_map/dynamic_slice | solution.py:674
  12.3 24.0 %all-to-all-done.recv_ref.edge_ref = bf16[16,288,128]{2,1,0:T(8,128)(2,1)S(1)} async-done(((bf16[16,288,128]{2,1,0:T(8,128)(2,1)}), bf16[16,288,128]{2,1,0:T(8,128)(2,1)S(1)}, u32[]{:S(2)}, u32[]{:S(2)}) %all-to-all-start) | async-done | bytes 1179680 | tf_op jit(solution)/shard_map/all_to_all | solution.py:671
  36.3 0.6 slice_bitcast_fusion.2.refs_2_
  36.9 0.8 collective-permute-start
  37.7 0.0 copy-done.11
  37.7 0.7 collective-permute-start.1
  38.4 0.0 copy-done.6
  38.4 0.0 copy-done.7
  38.4 0.0 copy-done.8
  38.4 0.0 copy-done.9
  38.4 7.8 %column_heads.1.refs_0_ = bf16[16,4,8,512]{3,2,1,0:T(8,128)(2,1)} custom-call(bf16[16,288,128]{2,1,0:T(8,128)(2,1)S(1)} %all-to-all-done.recv_ref.edge_ref, bf16[16,288,128]{2,1,0:T(8,128)(2,1)S(1)} %all-to-all-done.recv_ref.edge_ref, f32[3,3,1024]{2,1,0:T(4,128)S(1)} %copy-done.6, f32[1,1024]{1,0:T(1,128)S(1)} %bitcast.10, f32[1,1024]{1,0:T(1,128)S(1)} %bitcast.12, ...), custom_call_target="tpu_custom_call" | custom-call | flops 1610612736 | bytes 8388608 | tf_op jit(solution)/shard_map/column_heads/pallas_call | solution.py:398
  46.3 0.0 copy-start.10
  46.3 0.0 collective-permute-done.intra_ref
  46.3 0.0 copy-start.2
  46.3 0.6 slice_bitcast_fusion.1.refs_1_
  46.9 0.0 collective-permute-done.1.inter_ref
  46.9 0.6 slice_bitcast_fusion.refs_2_
  47.5 0.0 copy-start.4
  47.5 0.8 copy-done.4
  48.3 13.6 %all-to-all-start.1 = ((bf16[16,4,8,512]{3,2,1,0:T(8,128)(2,1)}), bf16[16,4,8,512]{3,2,1,0:T(8,128)(2,1)}, u32[]{:S(2)}, u32[]{:S(2)}) async-start(bf16[16,4,8,512]{3,2,1,0:T(8,128)(2,1)} %gate.3), calls=%async_computation.1 | async-start | bytes 1048576 | tf_op jit(solution)/shard_map/all_to_all | solution.py:684
  61.9 0.0 copy-done.2
  61.9 0.0 copy-done.10
  61.9 0.0 copy-start.3
  61.9 1.0 %copy-done.3 = bf16[1,256,1024]{2,1,0:T(8,128)(2,1)S(1)} copy-done((bf16[1,256,1024]{2,1,0:T(8,128)(2,1)S(1)}, bf16[1,256,1024]{2,1,0:T(8,128)(2,1)}, u32[]{:S(2)}) %copy-start.3) | copy-done | bytes 524312
  62.9 0.0 copy-start.5
  62.9 1.0 %copy-done.5 = bf16[1,256,1024]{2,1,0:T(8,128)(2,1)S(1)} copy-done((bf16[1,256,1024]{2,1,0:T(8,128)(2,1)S(1)}, bf16[1,256,1024]{2,1,0:T(8,128)(2,1)}, u32[]{:S(2)}) %copy-start.5) | copy-done | bytes 524312
  64.0 0.0 copy-start.1
  64.0 10.6 %row_heads.1.partial_ref = f32[512,1024]{1,0:T(8,128)} custom-call(bf16[2,256,1024]{2,1,0:T(8,128)(2,1)S(1)} %copy-done, bf16[1,256,1024]{2,1,0:T(8,128)(2,1)S(1)} %copy-done.3, bf16[1,256,1024]{2,1,0:T(8,128)(2,1)S(1)} %copy-done.5, f32[3,3,1024]{2,1,0:T(4,128)S(1)} %copy-done.6, f32[1,1024]{1,0:T(1,128)S(1)} %bitcast.11, f32[1,1024]{1,0:T(1,128)S(1)} %bitcast.13, ...), custom_call_target="tpu_custom_call" | custom-call | flops 2147483648 | bytes 10485760 | tf_op jit(solution)/shard_map/row_heads/pallas_call | solution.py:547
  74.6 1.8 %all-to-all-done.1.heads_ref = bf16[16,4,8,512]{3,2,1,0:T(8,128)(2,1)} async-done(((bf16[16,4,8,512]{3,2,1,0:T(8,128)(2,1)}), bf16[16,4,8,512]{3,2,1,0:T(8,128)(2,1)}, u32[]{:S(2)}, u32[]{:S(2)}) %all-to-all-start.1) | async-done | bytes 524320 | tf_op jit(solution)/shard_map/all_to_all | solution.py:684
  76.4 0.0 copy-done.1
  76.4 4.3 %last_projection.1 = bf16[2,256,1024]{2,1,0:T(8,128)(2,1)} custom-call(f32[512,1024]{1,0:T(8,128)} %row_heads.1.partial_ref, bf16[16,4,8,512]{3,2,1,0:T(8,128)(2,1)} %all-to-all-done.1.heads_ref, bf16[1024,1024]{1,0:T(8,128)(2,1)S(1)} %copy-done.1), custom_call_target="tpu_custom_call" | custom-call | flops 536870912 | bytes 5242880 | tf_op jit(solution)/shard_map/last_projection/pallas_call | solution.py:618
  (4 shorter events, 0.0 us)
Async XLA Ops:
  3.7 7.6 %copy-start = (bf16[2,256,1024]{2,1,0:T(8,128)(2,1)S(1)}, bf16[2,256,1024]{2,1,0:T(8,128)(2,1)}, u32[]{:S(2)}) copy-start(bf16[2,256,1024]{2,1,0:T(8,128)(2,1)} %tokens_ref.1) | copy-start | bytes 3145732
  3.7 32.7 %all-to-all-start = ((bf16[16,288,128]{2,1,0:T(8,128)(2,1)}), bf16[16,288,128]{2,1,0:T(8,128)(2,1)S(1)}, u32[]{:S(2)}, u32[]{:S(2)}) async-start(bf16[16,288,128]{2,1,0:T(8,128)(2,1)} %pack_columns.1), calls=%async_computation | async-start | bytes 2359296 | tf_op jit(solution)/shard_map/all_to_all | solution.py:671
  11.2 26.5 %copy-start.11 = (f32[3072]{0:T(1024)S(1)}, f32[3072]{0:T(1024)}, u32[]{:S(2)}) copy-start(f32[3072]{0:T(1024)} %param.15) | copy-start | bytes 36868
  11.2 27.2 %copy-start.6 = (f32[3,3,1024]{2,1,0:T(4,128)S(1)}, f32[3,3,1024]{2,1,0:T(4,128)}, u32[]{:S(2)}) copy-start(f32[3,3,1024]{2,1,0:T(4,128)} %peg_ref.3) | copy-start | bytes 110596
  11.2 27.2 %copy-start.7 = (f32[1024]{0:T(1024)S(1)}, f32[1024]{0:T(1024)}, u32[]{:S(2)}) copy-start(f32[1024]{0:T(1024)} %param.11) | copy-start | bytes 12292
  11.2 27.2 %copy-start.8 = (f32[1024]{0:T(1024)S(1)}, f32[1024]{0:T(1024)}, u32[]{:S(2)}) copy-start(f32[1024]{0:T(1024)} %param.12) | copy-start | bytes 12292
  11.2 27.2 %copy-start.9 = (f32[1024]{0:T(1024)S(1)}, f32[1024]{0:T(1024)}, u32[]{:S(2)}) copy-start(f32[1024]{0:T(1024)} %param.13) | copy-start | bytes 12292
  36.9 9.4 %collective-permute-start = (bf16[1,256,1024]{2,1,0:T(8,128)(2,1)}, bf16[1,256,1024]{2,1,0:T(8,128)(2,1)S(1)}, u32[]{:S(2)}, u32[]{:S(2)}) collective-permute-start(bf16[1,256,1024]{2,1,0:T(8,128)(2,1)} %get-tuple-element.7), channel_id=1, source_target_pairs={{0,1},{1,0},{2,3},{3,2},{4,5},{5,4},{6,7},{7,6},{8,9},{9,8},{10,11... | collective-permute-start | bytes 1572872 | tf_op jit(solution)/shard_map/ppermute | solution.py:678
  37.7 9.2 %collective-permute-start.1 = (bf16[1,256,1024]{2,1,0:T(8,128)(2,1)}, bf16[1,256,1024]{2,1,0:T(8,128)(2,1)S(1)}, u32[]{:S(2)}, u32[]{:S(2)}) collective-permute-start(bf16[1,256,1024]{2,1,0:T(8,128)(2,1)} %get-tuple-element.8), channel_id=1, source_target_pairs={{1,2},{2,1},{3,4},{4,3},{5,6},{6,5},{7,8},{8,7},{9,10},{10,9},{11,... | collective-permute-start | bytes 1572872 | tf_op jit(solution)/shard_map/ppermute | solution.py:679
  46.3 15.6 %copy-start.10 = (f32[1024]{0:T(1024)S(1)}, f32[1024]{0:T(1024)}, u32[]{:S(2)}) copy-start(f32[1024]{0:T(1024)} %param.17) | copy-start | bytes 12292
  46.3 15.6 %copy-start.2 = (bf16[1,256,1024]{2,1,0:T(8,128)(2,1)}, bf16[1,256,1024]{2,1,0:T(8,128)(2,1)S(1)}, u32[]{:S(2)}) copy-start(bf16[1,256,1024]{2,1,0:T(8,128)(2,1)S(1)} %collective-permute-done.intra_ref) | copy-start | bytes 1572868
  47.5 0.8 copy-start.4
  48.3 28.1 %all-to-all-start.1 = ((bf16[16,4,8,512]{3,2,1,0:T(8,128)(2,1)}), bf16[16,4,8,512]{3,2,1,0:T(8,128)(2,1)}, u32[]{:S(2)}, u32[]{:S(2)}) async-start(bf16[16,4,8,512]{3,2,1,0:T(8,128)(2,1)} %gate.3), calls=%async_computation.1 | async-start | bytes 1048576 | tf_op jit(solution)/shard_map/all_to_all | solution.py:684
  61.9 1.0 %copy-start.3 = (bf16[1,256,1024]{2,1,0:T(8,128)(2,1)S(1)}, bf16[1,256,1024]{2,1,0:T(8,128)(2,1)}, u32[]{:S(2)}) copy-start(bf16[1,256,1024]{2,1,0:T(8,128)(2,1)} %copy-done.2) | copy-start | bytes 1572868
  62.9 1.0 %copy-start.5 = (bf16[1,256,1024]{2,1,0:T(8,128)(2,1)S(1)}, bf16[1,256,1024]{2,1,0:T(8,128)(2,1)}, u32[]{:S(2)}) copy-start(bf16[1,256,1024]{2,1,0:T(8,128)(2,1)} %copy-done.4) | copy-start | bytes 1572868
  64.0 12.4 %copy-start.1 = (bf16[1024,1024]{1,0:T(8,128)(2,1)S(1)}, bf16[1024,1024]{1,0:T(8,128)(2,1)}, u32[]{:S(2)}) copy-start(bf16[1024,1024]{1,0:T(8,128)(2,1)} %out_weight_ref.1) | copy-start | bytes 6291460

commit v2 on v1

--- a/solution.py
+++ b/solution.py
@@ -128,21 +128,22 @@
     return low, high
 
 
-def pack_kernel(devices, per_step, own_ref, left_ref, right_ref, out_ref):
-    model = own_ref.shape[2]
-    cols = own_ref.shape[1] // per_step
+def pack_kernel(devices, per_step, tokens_ref, out_ref):
+    _, width, model = tokens_ref.shape
+    cols = width // devices
     slabs = model // LANES
     tiles = cols // HALF
     step = pl.program_id(0)
     place = lax.broadcasted_iota(jnp.int32, (SUB, LANES), 0)
     for k in range(per_step):
         dest = step * per_step + k
+        start = pl.multiple_of(dest * cols, cols)
+        left_start = pl.multiple_of(jnp.maximum(dest - 1, 0) * cols, cols)
+        right_start = pl.multiple_of(jnp.minimum(dest + 1, devices - 1) * cols, cols)
+        own = [tokens_ref[band, pl.ds(start, cols), :].astype(jnp.float32) for band in range(2)]
         for eight in range(cols // SUB):
-            start = k * cols + eight * SUB
-            pair = interleave(
-                own_ref[0, start : start + SUB, :].astype(jnp.float32),
-                own_ref[1, start : start + SUB, :].astype(jnp.float32),
-            )
+            rows = slice(eight * SUB, (eight + 1) * SUB)
+            pair = interleave(own[0][rows], own[1][rows])
             for which in range(2):
                 tile = pair[which].astype(jnp.bfloat16)
                 for slab in range(slabs):
@@ -150,18 +151,10 @@
                     out_ref[k, base : base + SUB, :] = tile[:, slab * LANES : (slab + 1) * LANES]
         lefts, rights = [], []
         for band in range(2):
-            if k == 0:
-                left = left_ref[band].astype(jnp.float32)[cols - 1 : cols]
-            else:
-                left = own_ref[band, (k - 1) * cols : k * cols, :].astype(jnp.float32)
-                left = left[cols - 1 : cols]
-            if k == per_step - 1:
-                right = right_ref[band].astype(jnp.float32)[0:1]
-            else:
-                right = own_ref[band, (k + 1) * cols : (k + 2) * cols, :]
-                right = right.astype(jnp.float32)[0:1]
-            lefts.append(jnp.where(dest > 0, left, 0.0))
-            rights.append(jnp.where(dest < devices - 1, right, 0.0))
+            left = tokens_ref[band, pl.ds(left_start, cols), :].astype(jnp.float32)
+            right = tokens_ref[band, pl.ds(right_start, cols), :].astype(jnp.float32)
+            lefts.append(jnp.where(dest > 0, left[cols - 1 : cols], 0.0))
+            rights.append(jnp.where(dest < devices - 1, right[0:1], 0.0))
         for two in range(slabs // 2):
             one = slice(2 * two * LANES, (2 * two + 1) * LANES)
             other = slice((2 * two + 1) * LANES, (2 * two + 2) * LANES)
@@ -180,24 +173,15 @@
     slabs = model // LANES
     rows = slabs * bands * (cols + 2)
     per_step = 4
-    last = devices - 1
     return pl.pallas_call(
         functools.partial(pack_kernel, devices, per_step),
         grid=(devices // per_step,),
-        in_specs=[
-            pl.BlockSpec((bands, per_step * cols, model), lambda i: (0, i, 0)),
-            pl.BlockSpec(
-                (bands, cols, model), lambda i: (0, jnp.maximum(i * per_step - 1, 0), 0)
-            ),
-            pl.BlockSpec(
-                (bands, cols, model), lambda i: (0, jnp.minimum((i + 1) * per_step, last), 0)
-            ),
-        ],
+        in_specs=[pl.BlockSpec(memory_space=pltpu.VMEM)],
         out_specs=pl.BlockSpec((per_step, rows, LANES), lambda i: (i, 0, 0)),
         out_shape=jax.ShapeDtypeStruct((devices, rows, LANES), jnp.bfloat16),
         compiler_params=pltpu.CompilerParams(vmem_limit_bytes=6 * MIB),
         name="pack_columns",
-    )(*[in_hbm(tokens)] * 3)
+    )(tokens)
 
 
 def gate_kernel(*refs):
@@ -261,6 +245,7 @@
 
 
 def column_kernel(
+    waits,
     recv_ref,
     edge_ref,
     peg_ref,
@@ -269,13 +254,9 @@
     nbias_ref,
     qkv_bias_ref,
     qkv_hbm,
-    out_ref,
-    mixed_scr,
-    normed_scr,
-    qkv_scr,
-    weight_scr,
-    sems,
+    *refs,
 ):
+    out_ref, mixed_scr, normed_scr, qkv_scr, weight_scr, sems = refs[waits:]
     step = pl.program_id(0)
     devices = recv_ref.shape[0]
     tiles = recv_ref.shape[1] // (2 * SUB)
@@ -384,7 +365,7 @@
                 )
 
 
-def column_part(recv, peg_weight, peg_bias, gain, nbias, qkv_weight, qkv_bias):
+def column_part(recv, after, peg_weight, peg_bias, gain, nbias, qkv_weight, qkv_bias):
     devices, rows, _ = recv.shape
     model = gain.shape[-1]
     slabs = model // LANES
@@ -396,7 +377,7 @@
     whole2 = lambda i: (0, 0)
     steps = slabs // 2
     return pl.pallas_call(
-        column_kernel,
+        functools.partial(column_kernel, len(after)),
         grid=(steps,),
         in_specs=[
             pl.BlockSpec((devices, 2 * tiles * SUB, LANES), lambda i: (0, i, 0)),
@@ -407,7 +388,8 @@
             pl.BlockSpec((1, model), whole2),
             pl.BlockSpec((3, features), whole2),
             pl.BlockSpec(memory_space=pltpu.HBM),
-        ],
+        ]
+        + [pl.BlockSpec(memory_space=pltpu.HBM)] * len(after),
         out_specs=pl.BlockSpec((devices, tiles, SUB, features), lambda i: (0, 0, 0, 0)),
         out_shape=pltpu.HBM((devices, tiles, SUB, features), jnp.bfloat16),
         scratch_shapes=[
@@ -424,7 +406,7 @@
             bytes_accessed=8 * MIB,
         ),
         name="column_heads",
-    )(recv, recv, peg_weight, peg_bias, gain, nbias, qkv_bias[:, first:], in_hbm(qkv_weight))
+    )(recv, recv, peg_weight, peg_bias, gain, nbias, qkv_bias[:, first:], in_hbm(qkv_weight), *map(in_hbm, after))
 
 
 def row_kernel(
@@ -573,7 +555,7 @@
         ],
         compiler_params=pltpu.CompilerParams(vmem_limit_bytes=20 * MIB),
         cost_estimate=pl.CostEstimate(
-            flops=2 * count * model * 4 * features,
+            flops=40 * count * model * 4 * features,
             transcendentals=count * width * ROW_HEADS,
             bytes_accessed=10 * 1024 * 1024,
         ),
@@ -595,44 +577,52 @@
 
 def last_kernel(partial_ref, heads_ref, out_weight_ref, result_ref):
     devices, tiles, sub, features = heads_ref.shape
-    lanes = result_ref.shape[2]
+    _, width, model = result_ref.shape
+    first = ROW_HEADS * DH
     heads = heads_ref[...].reshape(devices * tiles * sub, features)
-    projected = jnp.dot(heads, out_weight_ref[...], preferred_element_type=jnp.float32)
-    pairs = projected.reshape(devices * tiles // 2, 2, sub, lanes)
-    low, high = pairs[:, 0], pairs[:, 1]
-    upper = lax.broadcasted_iota(jnp.int32, (1, sub, lanes), 1) < HALF
-    first = jnp.where(upper, low, pltpu.roll(high, HALF, 1))
-    second = jnp.where(upper, pltpu.roll(low, HALF, 1), high)
-    width = result_ref.shape[1]
-    for band, value in enumerate((first, second)):
-        result_ref[band] = (
-            partial_ref[band * width : (band + 1) * width, :] + value.reshape(width, lanes)
-        ).astype(jnp.bfloat16)
+    upper = lax.broadcasted_iota(jnp.int32, (1, sub, 2 * LANES), 1) < HALF
+    start = pl.multiple_of(pl.program_id(0) * width, width)
+    for slab in range(model // (2 * LANES)):
+        lanes = slice(slab * 2 * LANES, (slab + 1) * 2 * LANES)
+        projected = jnp.dot(
+            heads, out_weight_ref[first:, lanes], preferred_element_type=jnp.float32
+        )
+        pairs = projected.reshape(devices * tiles // 2, 2, sub, 2 * LANES)
+        low, high = pairs[:, 0], pairs[:, 1]
+        rows = (
+            jnp.where(upper, low, pltpu.roll(high, HALF, 1)),
+            jnp.where(upper, pltpu.roll(low, HALF, 1), high),
+        )
+        for band, value in enumerate(rows):
+            result_ref[band, :, lanes] = (
+                partial_ref[band, pl.ds(start, width), lanes]
+                + value.reshape(width, 2 * LANES)
+            ).astype(jnp.bfloat16)
 
 
 def last_part(partial, heads, out_weight, bands, width):
     devices, tiles, sub, features = heads.shape
     model = out_weight.shape[1]
-    first = ROW_HEADS * DH
-    lanes = model // 4
+    steps = 4
+    vmem = pl.BlockSpec(memory_space=pltpu.VMEM)
     return pl.pallas_call(
         last_kernel,
-        grid=(model // lanes,),
+        grid=(steps,),
         in_specs=[
-            pl.BlockSpec((bands * width, lanes), lambda i: (0, i)),
-            pl.BlockSpec((devices, tiles, sub, features), lambda i: (0, 0, 0, 0)),
-            pl.BlockSpec((features, lanes), lambda i: (first // features, i)),
+            vmem,
+            pl.BlockSpec((devices // steps, tiles, sub, features), lambda i: (i, 0, 0, 0)),
+            vmem,
         ],
-        out_specs=pl.BlockSpec((bands, width, lanes), lambda i: (0, 0, i)),
+        out_specs=pl.BlockSpec((bands, width // steps, model), lambda i: (0, i, 0)),
         out_shape=jax.ShapeDtypeStruct((bands, width, model), jnp.bfloat16),
-        compiler_params=pltpu.CompilerParams(vmem_limit_bytes=10 * MIB),
+        compiler_params=pltpu.CompilerParams(vmem_limit_bytes=8 * MIB),
         cost_estimate=pl.CostEstimate(
             flops=2 * bands * width * features * model,
             transcendentals=0,
             bytes_accessed=5 * MIB,
         ),
         name="last_projection",
-    )(in_hbm(partial), heads, out_weight)
+    )(partial.reshape(bands, width, model), heads, out_weight)
 
 
 def on_device(
@@ -668,24 +658,18 @@
     qkv_bias = qkv_bias.reshape(3, model)
 
     packed = pack(tokens, devices)
-    received = lax.all_to_all(packed, "rows", split_axis=0, concat_axis=0, tiled=True)
     odd = lax.rem(lax.axis_index("rows"), 2)
     intra = lax.dynamic_slice_in_dim(tokens, 1 - odd, 1, axis=0)
     inter = lax.dynamic_slice_in_dim(tokens, odd, 1, axis=0)
-    intra, inter = gate((intra, inter), received[0, :SUB])
     same_chip = [(i, i ^ 1) for i in range(devices)]
     other_chip = [(i, i + 1 if i % 2 else i - 1) for i in range(1, devices - 1)]
     intra = lax.ppermute(intra, "rows", same_chip)
     inter = lax.ppermute(inter, "rows", other_chip)
-    col_heads = column_part(
-        received, peg_weight, peg_bias, gain, nbias, qkv_weight, qkv_bias
-    )
-    (col_heads,) = gate((col_heads,), intra[0, :SUB, :LANES], inter[0, :SUB, :LANES])
-    returned = lax.all_to_all(col_heads, "rows", split_axis=0, concat_axis=0, tiled=True)
+    received = lax.all_to_all(packed, "rows", split_axis=0, concat_axis=0, tiled=True)
     partial = row_part(
         tokens,
-        intra,
-        inter,
+        in_hbm(intra),
+        in_hbm(inter),
         peg_weight,
         peg_bias,
         gain,
@@ -695,6 +679,10 @@
         out_weight,
         out_bias,
     )
+    col_heads = column_part(
+        received, (partial,), peg_weight, peg_bias, gain, nbias, qkv_weight, qkv_bias
+    )
+    returned = lax.all_to_all(col_heads, "rows", split_axis=0, concat_axis=0, tiled=True)
     return last_part(partial, returned, out_weight, bands, width)
 
 

time: 81.2 us -> 71.2 us (0.88)
  blocking collectives: 0 us -> 22 us
  waiting for transfers between devices: 25.8 us -> 11.2 us
  starting transfers between devices: 22.5 us -> 10.1 us
  local copies, waits for them, and re-layouts: 5.77 us -> 1.41 us
    all_to_all x0 -> x1, blocking collectives: none -> 22 us  [on_device(): lax.all_to_all(col_heads, 'rows', split_axis=0, concat_axis=0, tiled=True)]
    all_to_all x1 -> x0, starting transfers between devices: 13.6 us -> none  [on_device(): lax.all_to_all(col_heads, 'rows', split_axis=0, concat_axis=0, tiled=True)]
    all_to_all x1, waiting for transfers between devices: 24 us -> 11.1 us  [on_device(): lax.all_to_all(packed, 'rows', split_axis=0, concat_axis=0, tiled=True)]
    pallas_call x1, Pallas kernels: 10.6 us -> 13.9 us  [row_part(): pl.pallas_call(row_kernel, grid=(slabs,), in_specs=[pl.BlockSpec((bands,...]
    unnamed x24 -> x18, local copies, waits for them, and re-layouts: 2.92 us -> 0.04 us
    ppermute x1, starting transfers between devices: 0.77 us -> 3.64 us  [on_device(): intra = lax.ppermute(intra, 'rows', same_chip)]
    all_to_all x1, starting transfers between devices: 7.52 us -> 4.98 us  [on_device(): lax.all_to_all(packed, 'rows', split_axis=0, concat_axis=0, tiled=True)]
    pallas_call x4 -> x2, Pallas kernels: 12.1 us -> 10.2 us  [the longest x1 7.77 us: column_part(): pl.pallas_call(functools.partial(column_kernel, len(after)), grid=(steps,...]
  transfers between devices with their start and end apart: 4 -> 3, of which waited for: 2 -> 1; matrix products, arithmetic and copies ran while one was open for 2% -> 0% of each run, Pallas kernels for 23% -> 22%
where the time goes in v2:
time: 71.2 us; the launch traced here: 70.7 us
  Pallas kernels  25.9 us (36%)
  blocking collectives  22 us (31%)
  waiting for transfers between devices  11.2 us (16%)
  starting transfers between devices  10.1 us (14%)
  local copies, waits for them, and re-layouts  1.41 us (2%)
    all_to_all x1, blocking collectives, on_device(): lax.all_to_all(col_heads, 'rows', split_axis=0, concat_axis=0, tiled=True)  22 us
    pallas_call x1, Pallas kernels, row_part(): pl.pallas_call(row_kernel, grid=(slabs,), in_specs=[pl.BlockSpec((bands,...  13.9 us
    all_to_all x1, waiting for transfers between devices, on_device(): lax.all_to_all(packed, 'rows', split_axis=0, concat_axis=0, tiled=True)  11.1 us
    pallas_call x1, Pallas kernels, column_part(): pl.pallas_call(functools.partial(column_kernel, len(after)), grid=(steps,...  7.77 us
    all_to_all x1, starting transfers between devices, on_device(): lax.all_to_all(packed, 'rows', split_axis=0, concat_axis=0, tiled=True)  4.98 us
    ppermute x1, starting transfers between devices, on_device(): intra = lax.ppermute(intra, 'rows', same_chip)  3.64 us
    pallas_call x1, Pallas kernels, last_part(): pl.pallas_call(last_kernel, grid=(steps,), in_specs=[vmem, pl.BlockSpec((...  2.38 us
    pallas_call x1, Pallas kernels, pack(): pl.pallas_call(functools.partial(pack_kernel, devices, per_step), grid=(d...  1.87 us
  transfers between devices with their start and end apart: 3, of which 1 were waited for; matrix products, arithmetic and copies ran while one was open for 0% of the time, Pallas kernels for 22%

profile of v2, /device:TPU:0, one launch (start us, length us, event | category | flops | bytes accessed | tf_op | source)
XLA Modules:
  0.0 70.7 jit_solution(3003203073120092021)
XLA Ops:
  0.0 0.0 copy-start.1
  0.0 1.4 %constant_dynamic-slice_fusion = (bf16[1,256,1024]{2,1,0:T(8,128)(2,1)S(1)}, bf16[1,256,1024]{2,1,0:T(8,128)(2,1)S(1)}) fusion(bf16[2,256,1024]{2,1,0:T(8,128)(2,1)} %tokens_ref.3, s32[]{:T(128)S(6)} %select_n.7, s32[]{:T(128)S(6)} %select_n.6), kind=kLoop, calls=%fused_computation | loop fusion | bytes 2097160 | tf_op jit(solution)/shard_map/dynamic_slice | solution.py:663
  1.4 1.5 %collective-permute-start.1 = (bf16[1,256,1024]{2,1,0:T(8,128)(2,1)S(1)}, bf16[1,256,1024]{2,1,0:T(8,128)(2,1)}, u32[]{:S(2)}, u32[]{:S(2)}) collective-permute-start(bf16[1,256,1024]{2,1,0:T(8,128)(2,1)S(1)} %get-tuple-element.5), channel_id=1, source_target_pairs={{1,2},{2,1},{3,4},{4,3},{5,6},{6,5},{7,8},{8,7},{9,10},{10,9},{11,... | collective-permute-start | bytes 1572872 | tf_op jit(solution)/shard_map/ppermute | solution.py:667
  2.8 0.0 copy-start.8
  2.8 0.0 copy-start.3
  2.8 0.0 copy-start.4
  2.8 0.0 copy-start.5
  2.8 0.0 copy-start.6
  2.8 0.0 copy-start.7
  2.9 3.6 %collective-permute-start = (bf16[1,256,1024]{2,1,0:T(8,128)(2,1)S(1)}, bf16[1,256,1024]{2,1,0:T(8,128)(2,1)}, u32[]{:S(2)}, u32[]{:S(2)}) collective-permute-start(bf16[1,256,1024]{2,1,0:T(8,128)(2,1)S(1)} %get-tuple-element.6), channel_id=1, source_target_pairs={{0,1},{1,0},{2,3},{3,2},{4,5},{5,4},{6,7},{7,6},{8,9},{9,8},{10,11... | collective-permute-start | bytes 1572872 | tf_op jit(solution)/shard_map/ppermute | solution.py:666
  6.5 0.0 copy-done.1
  6.5 1.9 %pack_columns.1 = bf16[16,288,128]{2,1,0:T(8,128)(2,1)} custom-call(bf16[2,256,1024]{2,1,0:T(8,128)(2,1)S(1)} %copy-done.1), custom_call_target="tpu_custom_call" | custom-call | tf_op jit(solution)/shard_map/pack_columns/pallas_call | solution.py:176
  8.4 5.0 %all-to-all-start = ((bf16[16,288,128]{2,1,0:T(8,128)(2,1)}), bf16[16,288,128]{2,1,0:T(8,128)(2,1)S(1)}, u32[]{:S(2)}, u32[]{:S(2)}) async-start(bf16[16,288,128]{2,1,0:T(8,128)(2,1)} %pack_columns.1), calls=%async_computation | async-start | bytes 2359296 | tf_op jit(solution)/shard_map/all_to_all | solution.py:668
  13.4 0.0 copy-done.8
  13.4 0.0 collective-permute-done.1.inter_ref
  13.4 0.0 collective-permute-done.intra_ref
  13.4 0.0 copy-done.3
  13.4 0.0 copy-done.4
  13.4 0.0 copy-done.5
  13.5 0.0 copy-done.6
  13.5 0.0 copy-done.7
  13.5 13.9 %row_heads.1.refs_0_ = f32[512,1024]{1,0:T(8,128)} custom-call(bf16[2,256,1024]{2,1,0:T(8,128)(2,1)S(1)} %copy-done.1, bf16[1,256,1024]{2,1,0:T(8,128)(2,1)} %collective-permute-done.intra_ref, bf16[1,256,1024]{2,1,0:T(8,128)(2,1)} %collective-permute-done.1.inter_ref, f32[3,3,1024]{2,1,0:T(4,128)S(1)} %copy-done.3, f32[1,1024]{1,0:T(1,128)S(1)} %bitcast.6, ...), custom_call_target="tpu_custom_call" | custom-call | flops 42949672960 | bytes 10485760 | tf_op jit(solution)/shard_map/row_heads/pallas_call | solution.py:529
  27.4 11.1 %all-to-all-done.recv_ref.edge_ref = bf16[16,288,128]{2,1,0:T(8,128)(2,1)S(1)} async-done(((bf16[16,288,128]{2,1,0:T(8,128)(2,1)}), bf16[16,288,128]{2,1,0:T(8,128)(2,1)S(1)}, u32[]{:S(2)}, u32[]{:S(2)}) %all-to-all-start) | async-done | bytes 1179680 | tf_op jit(solution)/shard_map/all_to_all | solution.py:668
  38.5 0.0 copy-start
  38.5 0.0 copy-start.2
  38.5 7.8 %column_heads.1 = bf16[16,4,8,512]{3,2,1,0:T(8,128)(2,1)} custom-call(bf16[16,288,128]{2,1,0:T(8,128)(2,1)S(1)} %all-to-all-done.recv_ref.edge_ref, bf16[16,288,128]{2,1,0:T(8,128)(2,1)S(1)} %all-to-all-done.recv_ref.edge_ref, f32[3,3,1024]{2,1,0:T(4,128)S(1)} %copy-done.3, f32[1,1024]{1,0:T(1,128)S(1)} %bitcast.7, f32[1,1024]{1,0:T(1,128)S(1)} %bitcast.9, ...), custom_call_target="tpu_custom_call" | custom-call | flops 1610612736 | bytes 8388608 | tf_op jit(solution)/shard_map/column_heads/pallas_call | solution.py:379
  46.3 22.0 %all_to_all.10.heads_ref = bf16[16,4,8,512]{3,2,1,0:T(8,128)(2,1)S(1)} all-to-all(bf16[16,4,8,512]{3,2,1,0:T(8,128)(2,1)} %column_heads.1), channel_id=1, replica_groups=mesh['groups'=2,'rows'=16] {'rows'}, dimensions={0} | all-to-all | bytes 1048576 | tf_op jit(solution)/shard_map/all_to_all | solution.py:685
  68.3 0.0 copy-done
  68.3 0.0 copy-done.2
  68.3 2.4 %last_projection.1 = bf16[2,256,1024]{2,1,0:T(8,128)(2,1)} custom-call(f32[2,256,1024]{2,1,0:T(8,128)S(1)} %bitcast.5, bf16[16,4,8,512]{3,2,1,0:T(8,128)(2,1)S(1)} %all_to_all.10.heads_ref, bf16[1024,1024]{1,0:T(8,128)(2,1)S(1)} %copy-done.2), custom_call_target="tpu_custom_call" | custom-call | flops 536870912 | bytes 5242880 | tf_op jit(solution)/shard_map/last_projection/pallas_call | solution.py:608
  (2 shorter events, 0.0 us)
Async XLA Ops:
  0.0 6.5 %copy-start.1 = (bf16[2,256,1024]{2,1,0:T(8,128)(2,1)S(1)}, bf16[2,256,1024]{2,1,0:T(8,128)(2,1)}, u32[]{:S(2)}) copy-start(bf16[2,256,1024]{2,1,0:T(8,128)(2,1)} %tokens_ref.3) | copy-start | bytes 3145732
  1.4 12.0 %collective-permute-start.1 = (bf16[1,256,1024]{2,1,0:T(8,128)(2,1)S(1)}, bf16[1,256,1024]{2,1,0:T(8,128)(2,1)}, u32[]{:S(2)}, u32[]{:S(2)}) collective-permute-start(bf16[1,256,1024]{2,1,0:T(8,128)(2,1)S(1)} %get-tuple-element.5), channel_id=1, source_target_pairs={{1,2},{2,1},{3,4},{4,3},{5,6},{6,5},{7,8},{8,7},{9,10},{10,9},{11,... | collective-permute-start | bytes 1572872 | tf_op jit(solution)/shard_map/ppermute | solution.py:667
  2.8 10.5 %copy-start.8 = (f32[3072]{0:T(1024)S(1)}, f32[3072]{0:T(1024)}, u32[]{:S(2)}) copy-start(f32[3072]{0:T(1024)} %param.15) | copy-start | bytes 36868
  2.8 10.6 %copy-start.3 = (f32[3,3,1024]{2,1,0:T(4,128)S(1)}, f32[3,3,1024]{2,1,0:T(4,128)}, u32[]{:S(2)}) copy-start(f32[3,3,1024]{2,1,0:T(4,128)} %peg_ref.3) | copy-start | bytes 110596
  2.8 10.6 %copy-start.4 = (f32[1024]{0:T(1024)S(1)}, f32[1024]{0:T(1024)}, u32[]{:S(2)}) copy-start(f32[1024]{0:T(1024)} %param.11) | copy-start | bytes 12292
  2.8 10.6 %copy-start.5 = (f32[1024]{0:T(1024)S(1)}, f32[1024]{0:T(1024)}, u32[]{:S(2)}) copy-start(f32[1024]{0:T(1024)} %param.12) | copy-start | bytes 12292
  2.8 10.6 %copy-start.6 = (f32[1024]{0:T(1024)S(1)}, f32[1024]{0:T(1024)}, u32[]{:S(2)}) copy-start(f32[1024]{0:T(1024)} %param.13) | copy-start | bytes 12292
  2.8 10.6 %copy-start.7 = (f32[1024]{0:T(1024)S(1)}, f32[1024]{0:T(1024)}, u32[]{:S(2)}) copy-start(f32[1024]{0:T(1024)} %param.17) | copy-start | bytes 12292
  2.9 10.6 %collective-permute-start = (bf16[1,256,1024]{2,1,0:T(8,128)(2,1)S(1)}, bf16[1,256,1024]{2,1,0:T(8,128)(2,1)}, u32[]{:S(2)}, u32[]{:S(2)}) collective-permute-start(bf16[1,256,1024]{2,1,0:T(8,128)(2,1)S(1)} %get-tuple-element.6), channel_id=1, source_target_pairs={{0,1},{1,0},{2,3},{3,2},{4,5},{5,4},{6,7},{7,6},{8,9},{9,8},{10,11... | collective-permute-start | bytes 1572872 | tf_op jit(solution)/shard_map/ppermute | solution.py:666
  8.4 30.1 %all-to-all-start = ((bf16[16,288,128]{2,1,0:T(8,128)(2,1)}), bf16[16,288,128]{2,1,0:T(8,128)(2,1)S(1)}, u32[]{:S(2)}, u32[]{:S(2)}) async-start(bf16[16,288,128]{2,1,0:T(8,128)(2,1)} %pack_columns.1), calls=%async_computation | async-start | bytes 2359296 | tf_op jit(solution)/shard_map/all_to_all | solution.py:668
  38.5 29.8 %copy-start = (f32[512,1024]{1,0:T(8,128)S(1)}, f32[512,1024]{1,0:T(8,128)}, u32[]{:S(2)}) copy-start(f32[512,1024]{1,0:T(8,128)} %row_heads.1.refs_0_) | copy-start | bytes 6291460
  38.5 29.8 %copy-start.2 = (bf16[1024,1024]{1,0:T(8,128)(2,1)S(1)}, bf16[1024,1024]{1,0:T(8,128)(2,1)}, u32[]{:S(2)}) copy-start(bf16[1024,1024]{1,0:T(8,128)(2,1)} %out_weight_ref.1) | copy-start | bytes 6291460

commit v3 on v2

--- a/solution.py
+++ b/solution.py
@@ -128,15 +128,17 @@
     return low, high
 
 
-def pack_kernel(devices, per_step, tokens_ref, out_ref):
+def pack_kernel(devices, per_step, tokens_ref, out_hbm, out_scr, sems):
     _, width, model = tokens_ref.shape
     cols = width // devices
     slabs = model // LANES
     tiles = cols // HALF
-    step = pl.program_id(0)
     place = lax.broadcasted_iota(jnp.int32, (SUB, LANES), 0)
-    for k in range(per_step):
-        dest = step * per_step + k
+
+    def copy(dest):
+        return pltpu.make_async_copy(out_scr.at[dest], out_hbm.at[dest], sems.at[dest])
+
+    def fill(dest):
         start = pl.multiple_of(dest * cols, cols)
         left_start = pl.multiple_of(jnp.maximum(dest - 1, 0) * cols, cols)
         right_start = pl.multiple_of(jnp.minimum(dest + 1, devices - 1) * cols, cols)
@@ -148,7 +150,7 @@
                 tile = pair[which].astype(jnp.bfloat16)
                 for slab in range(slabs):
                     base = (slab * tiles + eight * 2 + which) * SUB
-                    out_ref[k, base : base + SUB, :] = tile[:, slab * LANES : (slab + 1) * LANES]
+                    out_scr[dest, base : base + SUB, :] = tile[:, slab * LANES : (slab + 1) * LANES]
         lefts, rights = [], []
         for band in range(2):
             left = tokens_ref[band, pl.ds(left_start, cols), :].astype(jnp.float32)
@@ -164,7 +166,20 @@
             for index in range(1, SUB):
                 tile = jnp.where(place == index, order[index], tile)
             base = (slabs * tiles + two) * SUB
-            out_ref[k, base : base + SUB, :] = tile.astype(jnp.bfloat16)
+            out_scr[dest, base : base + SUB, :] = tile.astype(jnp.bfloat16)
+
+    def send(step, carry):
+        for k in range(per_step):
+            fill(step * per_step + k)
+            copy(step * per_step + k).start()
+        return carry
+
+    def finish(dest, carry):
+        copy(dest).wait()
+        return carry
+
+    lax.fori_loop(0, devices // per_step, send, 0)
+    lax.fori_loop(0, devices, finish, 0)
 
 
 def pack(tokens, devices):
@@ -175,10 +190,13 @@
     per_step = 4
     return pl.pallas_call(
         functools.partial(pack_kernel, devices, per_step),
-        grid=(devices // per_step,),
         in_specs=[pl.BlockSpec(memory_space=pltpu.VMEM)],
-        out_specs=pl.BlockSpec((per_step, rows, LANES), lambda i: (i, 0, 0)),
+        out_specs=pl.BlockSpec(memory_space=pltpu.HBM),
         out_shape=jax.ShapeDtypeStruct((devices, rows, LANES), jnp.bfloat16),
+        scratch_shapes=[
+            pltpu.VMEM((devices, rows, LANES), jnp.bfloat16),
+            pltpu.SemaphoreType.DMA((devices,)),
+        ],
         compiler_params=pltpu.CompilerParams(vmem_limit_bytes=6 * MIB),
         name="pack_columns",
     )(tokens)
@@ -224,7 +242,8 @@
         both, key, (((1,), (1,)), ((), ())), preferred_element_type=jnp.float32
     )
     if mask is not None:
-        scores = jnp.where(mask, scores, -1e30)
+        scores = jnp.where(mask, scores.reshape((-1,) + mask.shape[1:]), -1e30)
+        scores = scores.reshape(PAIR * count, -1)
     highest = jnp.max(scores, axis=-1, keepdims=True)
     probs = jnp.exp2((scores - highest) * (scale * LOG2E))
     total = jnp.sum(probs, axis=-1, keepdims=True)
@@ -236,18 +255,23 @@
 def weight_copies(qkv_hbm, weight_scr, sems, first):
     model = qkv_hbm.shape[0]
     width = weight_scr.shape[2]
+    pieces = sems.shape[1]
+    depth = model // pieces
     return [
-        pltpu.make_async_copy(
-            qkv_hbm.at[:, pl.ds(part * model + first, width)], weight_scr.at[part], sems.at[part]
-        )
+        [
+            pltpu.make_async_copy(
+                qkv_hbm.at[pl.ds(piece * depth, depth), pl.ds(part * model + first, width)],
+                weight_scr.at[part, pl.ds(piece * depth, depth)],
+                sems.at[part, piece],
+            )
+            for piece in range(pieces)
+        ]
         for part in range(3)
     ]
 
 
 def column_kernel(
-    waits,
     recv_ref,
-    edge_ref,
     peg_ref,
     peg_bias_ref,
     gain_ref,
@@ -256,81 +280,106 @@
     qkv_hbm,
     *refs,
 ):
-    out_ref, mixed_scr, normed_scr, qkv_scr, weight_scr, sems = refs[waits:]
-    step = pl.program_id(0)
+    out_ref, mixed_scr, normed_scr, qkv_scr, weight_scr, sems = refs[-6:]
+
     devices = recv_ref.shape[0]
-    tiles = recv_ref.shape[1] // (2 * SUB)
+    slabs, _, tiles, _, _ = mixed_scr.shape
     height = 2 * devices
     first = ROW_HEADS * DH
     features = weight_scr.shape[2]
     group = devices * SUB
 
-    @pl.when(step == 0)
-    def _():
-        for copy in weight_copies(qkv_hbm, weight_scr, sems, first):
+    weights = weight_copies(qkv_hbm, weight_scr, sems, first)
+    for copies in weights:
+        for copy in copies:
             copy.start()
 
-    place = lax.broadcasted_iota(jnp.int32, (1, 1, SUB, LANES), 2)
+    place = lax.broadcasted_iota(jnp.int32, (SUB, LANES), 0)
     upper = place < HALF
     column = lax.rem(place, HALF)
-
-    def with_neighbours(value):
-        swapped = pltpu.roll(value, HALF, 2)
-        zero = jnp.zeros((1,) + value.shape[1:], jnp.float32)
-        between = jnp.where(
-            upper,
-            jnp.concatenate([zero, swapped], axis=0),
-            jnp.concatenate([swapped, zero], axis=0),
-        )
-        return between[:-1], value, between[1:]
-
-    def stencil(triple, lanes, offset_col):
-        total = None
-        for offset_row in range(3):
-            weight = peg_ref[offset_row, offset_col : offset_col + 1, lanes]
-            term = triple[offset_row] * weight
-            total = term if total is None else total + term
-        return total
-
-    edges = edge_ref[...].astype(jnp.float32).reshape(devices, 1, SUB, LANES)
-    for local in range(2):
-        lanes = slice(local * LANES, (local + 1) * LANES)
-        own = recv_ref[:, local * tiles * SUB : (local + 1) * tiles * SUB, :]
-        own = own.astype(jnp.float32).reshape(devices, tiles, SUB, LANES)
-        triple = with_neighbours(own)
-        if local == 0:
-            left_edge = right_edge = with_neighbours(edges)
-        else:
-            left_edge = with_neighbours(pltpu.roll(edges, 1, 2))
-            right_edge = with_neighbours(pltpu.roll(edges, SUB - 1, 2))
-        wide = jnp.concatenate(
-            [stencil(left_edge, lanes, 0), stencil(triple, lanes, 0)], axis=1
-        )
-        from_left = jnp.where(
-            column == 0, pltpu.roll(wide[:, :-1], SUB - 3, 2), pltpu.roll(wide[:, 1:], 1, 2)
-        )
-        wide = jnp.concatenate(
-            [stencil(triple, lanes, 2), stencil(right_edge, lanes, 2)], axis=1
-        )
-        from_right = jnp.where(
-            column == HALF - 1,
-            pltpu.roll(wide[:, 1:], 3, 2),
-            pltpu.roll(wide[:, :-1], SUB - 1, 2),
-        )
-        total = (
-            own + peg_bias_ref[:, lanes] + stencil(triple, lanes, 1) + from_left + from_right
-        )
-        mixed_scr[2 * step + local] = total.astype(jnp.bfloat16).astype(jnp.float32)
-
-    @pl.when(step == pl.num_programs(0) - 1)
-    def _():
-        count = mixed_scr.shape[0]
-        for tile in range(tiles):
+    zero = jnp.zeros((SUB, LANES), jnp.float32)
+
+    def convolve_slab(slab, base, edge_base, local):
+        lanes = pl.ds(pl.multiple_of(slab * LANES, LANES), LANES)
+        weights = [
+            [jnp.broadcast_to(peg_ref[a, b : b + 1, lanes], (SUB, LANES)) for b in range(3)]
+            for a in range(3)
+        ]
+        weights[1][1] = weights[1][1] + 1.0
+        bias = jnp.broadcast_to(peg_bias_ref[:, lanes], (SUB, LANES))
+
+        def load(device):
+            own = [
+                recv_ref[device, pl.ds(pl.multiple_of(base + tile * SUB, SUB), SUB), :].astype(
+                    jnp.float32
+                )
+                for tile in range(tiles)
+            ]
+            edge = recv_ref[device, pl.ds(pl.multiple_of(edge_base, SUB), SUB), :]
+            edge = edge.astype(jnp.float32)
+            if local == 0:
+                return [edge] + own + [edge]
+            return [pltpu.roll(edge, 1, 0)] + own + [pltpu.roll(edge, SUB - 1, 0)]
+
+        swapped = [zero] * (tiles + 2)
+        values = load(0)
+        following = [pltpu.roll(value, HALF, 0) for value in values]
+        above = [jnp.where(upper, p, n) for p, n in zip(swapped, following)]
+        for device in range(devices):
+            swapped = following
+            if device + 1 < devices:
+                coming = load(device + 1)
+                following = [pltpu.roll(value, HALF, 0) for value in coming]
+            else:
+                coming, following = None, [zero] * (tiles + 2)
+            below = [jnp.where(upper, p, n) for p, n in zip(swapped, following)]
+
+            def stencil(index, offset):
+                return (
+                    above[index] * weights[0][offset]
+                    + values[index] * weights[1][offset]
+                    + below[index] * weights[2][offset]
+                )
+
+            lefts = [stencil(index, 0) for index in range(tiles + 1)]
+            rights = [stencil(index, 2) for index in range(1, tiles + 2)]
+            for tile in range(tiles):
+                from_left = jnp.where(
+                    column == 0,
+                    pltpu.roll(lefts[tile], SUB - 3, 0),
+                    pltpu.roll(lefts[tile + 1], 1, 0),
+                )
+                from_right = jnp.where(
+                    column == HALF - 1,
+                    pltpu.roll(rights[tile + 1], 3, 0),
+                    pltpu.roll(rights[tile], SUB - 1, 0),
+                )
+                total = (stencil(tile + 1, 1) + bias) + (from_left + from_right)
+                mixed_scr[slab, device, tile] = total.astype(jnp.bfloat16).astype(jnp.float32)
+            values, above = coming, below
+
+    def two_slabs(two, carry):
+        for local in range(2):
+            slab = 2 * two + local
+            convolve_slab(slab, slab * tiles * SUB, (slabs * tiles + two) * SUB, local)
+        return carry
+
+    lax.fori_loop(0, slabs // 2, two_slabs, 0)
+
+    row_id = lax.broadcasted_iota(jnp.int32, (1, SUB, group), 1)
+    col_id = lax.broadcasted_iota(jnp.int32, (1, SUB, group), 2)
+    mask = lax.rem(row_id, HALF) == lax.rem(col_id, HALF)
+    scale = score_scale(height)
+    block = 2 * group
+    for half in range(tiles // 2):
+        for tile in range(2 * half, 2 * half + 2):
             for start in range(0, devices, HALF):
                 values = jnp.concatenate(
                     [
-                        mixed_scr[slab, start : start + HALF, tile].reshape(HALF * SUB, LANES)
-                        for slab in range(count)
+                        mixed_scr[slab, start : start + HALF, tile].reshape(
+                            HALF * SUB, LANES
+                        )
+                        for slab in range(slabs)
                     ],
                     axis=1,
                 )
@@ -338,18 +387,21 @@
                 normed_scr[base : base + HALF * SUB, :] = normalise(
                     values, gain_ref[...], nbias_ref[...]
                 )
-        for part, copy in enumerate(weight_copies(qkv_hbm, weight_scr, sems, first)):
-            copy.wait()
+        span = slice(half * block, (half + 1) * block)
+        for part in range(3):
+            if half == 0:
+                for copy in weights[part]:
+                    copy.wait()
             projected = (
-                jnp.dot(normed_scr[...], weight_scr[part], preferred_element_type=jnp.float32)
+                jnp.dot(
+                    normed_scr[span, :],
+                    weight_scr[part],
+                    preferred_element_type=jnp.float32,
+                )
                 + qkv_bias_ref[part : part + 1, :]
             )
-            qkv_scr[part] = projected.astype(jnp.bfloat16)
-        row_id = lax.broadcasted_iota(jnp.int32, (PAIR * group, group), 0)
-        col_id = lax.broadcasted_iota(jnp.int32, (PAIR * group, group), 1)
-        mask = lax.rem(row_id, HALF) == lax.rem(col_id, HALF)
-        scale = score_scale(height)
-        for tile in range(tiles):
+            qkv_scr[part, span, :] = projected.astype(jnp.bfloat16)
+        for tile in range(2 * half, 2 * half + 2):
             rows = slice(tile * group, (tile + 1) * group)
             for pair in range(features // LANES):
                 lanes = slice(pair * LANES, (pair + 1) * LANES)
@@ -374,39 +426,36 @@
     first = ROW_HEADS * DH
     features = model - first
     tokens = 2 * devices * cols
-    whole2 = lambda i: (0, 0)
-    steps = slabs // 2
+    vmem = pl.BlockSpec(memory_space=pltpu.VMEM)
     return pl.pallas_call(
-        functools.partial(column_kernel, len(after)),
-        grid=(steps,),
-        in_specs=[
-            pl.BlockSpec((devices, 2 * tiles * SUB, LANES), lambda i: (0, i, 0)),
-            pl.BlockSpec((devices, SUB, LANES), lambda i: (0, slabs * tiles + i, 0)),
-            pl.BlockSpec((3, 3, 2 * LANES), lambda i: (0, 0, i)),
-            pl.BlockSpec((1, 2 * LANES), lambda i: (0, i)),
-            pl.BlockSpec((1, model), whole2),
-            pl.BlockSpec((1, model), whole2),
-            pl.BlockSpec((3, features), whole2),
-            pl.BlockSpec(memory_space=pltpu.HBM),
-        ]
-        + [pl.BlockSpec(memory_space=pltpu.HBM)] * len(after),
-        out_specs=pl.BlockSpec((devices, tiles, SUB, features), lambda i: (0, 0, 0, 0)),
+        column_kernel,
+        in_specs=[vmem] * 6 + [pl.BlockSpec(memory_space=pltpu.HBM)] * (1 + len(after)),
+        out_specs=vmem,
         out_shape=pltpu.HBM((devices, tiles, SUB, features), jnp.bfloat16),
         scratch_shapes=[
             pltpu.VMEM((slabs, devices, tiles, SUB, LANES), jnp.float32),
             pltpu.VMEM((tokens, model), jnp.bfloat16),
             pltpu.VMEM((3, tokens, features), jnp.bfloat16),
             pltpu.VMEM((3, model, features), jnp.bfloat16),
-            pltpu.SemaphoreType.DMA((3,)),
+            pltpu.SemaphoreType.DMA((3, 1)),
         ],
-        compiler_params=pltpu.CompilerParams(vmem_limit_bytes=20 * MIB),
+        compiler_params=pltpu.CompilerParams(vmem_limit_bytes=9 * MIB),
         cost_estimate=pl.CostEstimate(
             flops=2 * tokens * model * 3 * features,
             transcendentals=tokens * LANES * features // DH,
             bytes_accessed=8 * MIB,
         ),
         name="column_heads",
-    )(recv, recv, peg_weight, peg_bias, gain, nbias, qkv_bias[:, first:], in_hbm(qkv_weight), *map(in_hbm, after))
+    )(
+        recv,
+        peg_weight,
+        peg_bias,
+        gain,
+        nbias,
+        qkv_bias[:, first:],
+        in_hbm(qkv_weight),
+        *map(in_hbm, after),
+    )
 
 
 def row_kernel(
@@ -429,6 +478,7 @@
     weight_scr,
     out_scr,
     sems,
+    out_sem,
 ):
     step = pl.program_id(0)
     slabs = pl.num_programs(0)
@@ -436,13 +486,14 @@
     features = weight_scr.shape[2]
 
     def copies():
-        copy = pltpu.make_async_copy(out_hbm.at[pl.ds(0, features), :], out_scr, sems.at[3])
-        return weight_copies(qkv_hbm, weight_scr, sems, 0) + [copy]
+        copy = pltpu.make_async_copy(out_hbm.at[pl.ds(0, features), :], out_scr, out_sem)
+        return weight_copies(qkv_hbm, weight_scr, sems, 0) + [[copy]]
 
     @pl.when(step == 0)
     def _():
-        for copy in copies():
-            copy.start()
+        for group in copies():
+            for copy in group:
+                copy.start()
 
     odd = lax.rem(lax.axis_index("rows"), 2) == 1
     intra = intra_ref[0].astype(jnp.float32)
@@ -480,7 +531,8 @@
             )
         waits = copies()
         for part in range(3):
-            waits[part].wait()
+            for copy in waits[part]:
+                copy.wait()
             projected = (
                 jnp.dot(normed_scr[...], weight_scr[part], preferred_element_type=jnp.float32)
                 + qkv_bias_ref[part : part + 1, :]
@@ -498,7 +550,7 @@
                     scale,
                     None,
                 ).astype(jnp.bfloat16)
-        waits[3].wait()
+        waits[3][0].wait()
         for slab in range(count):
             lanes = slice(slab * LANES, (slab + 1) * LANES)
             partial_ref[:, lanes] = (
@@ -551,9 +603,10 @@
             pltpu.VMEM((count, features), jnp.bfloat16),
             pltpu.VMEM((3, model, features), jnp.bfloat16),
             pltpu.VMEM((features, model), jnp.bfloat16),
-            pltpu.SemaphoreType.DMA((4,)),
+            pltpu.SemaphoreType.DMA((3, 4)),
+            pltpu.SemaphoreType.DMA,
         ],
-        compiler_params=pltpu.CompilerParams(vmem_limit_bytes=20 * MIB),
+        compiler_params=pltpu.CompilerParams(vmem_limit_bytes=14 * MIB),
         cost_estimate=pl.CostEstimate(
             flops=40 * count * model * 4 * features,
             transcendentals=count * width * ROW_HEADS,

time: 71.2 us -> 70 us (0.983)
  Pallas kernels: 25.9 us -> 24.8 us
    pallas_call x2, Pallas kernels: 9.64 us -> 8.45 us  [the longest x1 7.09 us: column_part(): pl.pallas_call(column_kernel, in_specs=[vmem] * 6 + [pl.BlockSpec(memory_...]
where the time goes in v3:
time: 70 us; the launch traced here: 69.5 us
  Pallas kernels  24.8 us (35%)
  blocking collectives  22 us (31%)
  waiting for transfers between devices  11 us (16%)
  starting transfers between devices  10.1 us (14%)
  local copies, waits for them, and re-layouts  1.41 us (2%)
    all_to_all x1, blocking collectives, on_device(): lax.all_to_all(col_heads, 'rows', split_axis=0, concat_axis=0, tiled=True)  22 us
    pallas_call x1, Pallas kernels, row_part(): pl.pallas_call(row_kernel, grid=(slabs,), in_specs=[pl.BlockSpec((bands,...  14 us
    all_to_all x1, waiting for transfers between devices, on_device(): lax.all_to_all(packed, 'rows', split_axis=0, concat_axis=0, tiled=True)  11 us
    pallas_call x1, Pallas kernels, column_part(): pl.pallas_call(column_kernel, in_specs=[vmem] * 6 + [pl.BlockSpec(memory_...  7.09 us
    all_to_all x1, starting transfers between devices, on_device(): lax.all_to_all(packed, 'rows', split_axis=0, concat_axis=0, tiled=True)  4.99 us
    ppermute x1, starting transfers between devices, on_device(): intra = lax.ppermute(intra, 'rows', same_chip)  3.64 us
    pallas_call x1, Pallas kernels, last_part(): pl.pallas_call(last_kernel, grid=(steps,), in_specs=[vmem, pl.BlockSpec((...  2.37 us
    ppermute x1, starting transfers between devices, on_device(): inter = lax.ppermute(inter, 'rows', other_chip)  1.47 us
  transfers between devices with their start and end apart: 3, of which 1 were waited for; matrix products, arithmetic and copies ran while one was open for 0% of the time, Pallas kernels for 22%

profile of v3, /device:TPU:0, one launch (start us, length us, event | category | flops | bytes accessed | tf_op | source)
XLA Modules:
  0.0 69.5 jit_solution(9798328270130955879)
XLA Ops:
  0.0 0.0 copy-start.1
  0.0 1.4 %constant_dynamic-slice_fusion = (bf16[1,256,1024]{2,1,0:T(8,128)(2,1)S(1)}, bf16[1,256,1024]{2,1,0:T(8,128)(2,1)S(1)}) fusion(bf16[2,256,1024]{2,1,0:T(8,128)(2,1)} %tokens_ref.3, s32[]{:T(128)S(6)} %select_n.7, s32[]{:T(128)S(6)} %select_n.6), kind=kLoop, calls=%fused_computation | loop fusion | bytes 2097160 | tf_op jit(solution)/shard_map/dynamic_slice | solution.py:716
  1.4 1.5 %collective-permute-start.1 = (bf16[1,256,1024]{2,1,0:T(8,128)(2,1)S(1)}, bf16[1,256,1024]{2,1,0:T(8,128)(2,1)}, u32[]{:S(2)}, u32[]{:S(2)}) collective-permute-start(bf16[1,256,1024]{2,1,0:T(8,128)(2,1)S(1)} %get-tuple-element.5), channel_id=1, source_target_pairs={{1,2},{2,1},{3,4},{4,3},{5,6},{6,5},{7,8},{8,7},{9,10},{10,9},{11,... | collective-permute-start | bytes 1572872 | tf_op jit(solution)/shard_map/ppermute | solution.py:720
  2.8 0.0 copy-start.8
  2.8 0.0 copy-start.3
  2.8 0.0 copy-start.4
  2.8 0.0 copy-start.5
  2.8 0.0 copy-start.6
  2.8 0.0 copy-start.7
  2.9 3.6 %collective-permute-start = (bf16[1,256,1024]{2,1,0:T(8,128)(2,1)S(1)}, bf16[1,256,1024]{2,1,0:T(8,128)(2,1)}, u32[]{:S(2)}, u32[]{:S(2)}) collective-permute-start(bf16[1,256,1024]{2,1,0:T(8,128)(2,1)S(1)} %get-tuple-element.6), channel_id=1, source_target_pairs={{0,1},{1,0},{2,3},{3,2},{4,5},{5,4},{6,7},{7,6},{8,9},{9,8},{10,11... | collective-permute-start | bytes 1572872 | tf_op jit(solution)/shard_map/ppermute | solution.py:719
  6.5 0.0 copy-done.1
  6.5 1.4 %pack_columns.1 = bf16[16,288,128]{2,1,0:T(8,128)(2,1)} custom-call(bf16[2,256,1024]{2,1,0:T(8,128)(2,1)S(1)} %copy-done.1), custom_call_target="tpu_custom_call" | custom-call | tf_op jit(solution)/shard_map/pack_columns/pallas_call | solution.py:191
  7.9 5.0 %all-to-all-start = ((bf16[16,288,128]{2,1,0:T(8,128)(2,1)}), bf16[16,288,128]{2,1,0:T(8,128)(2,1)S(1)}, u32[]{:S(2)}, u32[]{:S(2)}) async-start(bf16[16,288,128]{2,1,0:T(8,128)(2,1)} %pack_columns.1), calls=%async_computation | async-start | bytes 2359296 | tf_op jit(solution)/shard_map/all_to_all | solution.py:721
  12.9 0.0 copy-done.8
  12.9 0.0 collective-permute-done.1.inter_ref
  12.9 0.0 collective-permute-done.intra_ref
  12.9 0.0 copy-done.3
  12.9 0.0 copy-done.4
  12.9 0.0 copy-done.5
  13.0 0.0 copy-done.6
  13.0 0.0 copy-done.7
  13.0 14.0 %row_heads.1.refs_0_ = f32[512,1024]{1,0:T(8,128)} custom-call(bf16[2,256,1024]{2,1,0:T(8,128)(2,1)S(1)} %copy-done.1, bf16[1,256,1024]{2,1,0:T(8,128)(2,1)} %collective-permute-done.intra_ref, bf16[1,256,1024]{2,1,0:T(8,128)(2,1)} %collective-permute-done.1.inter_ref, f32[3,3,1024]{2,1,0:T(4,128)S(1)} %copy-done.3, f32[1,1024]{1,0:T(1,128)S(1)} %bitcast.6, ...), custom_call_target="tpu_custom_call" | custom-call | flops 42949672960 | bytes 10485760 | tf_op jit(solution)/shard_map/row_heads/pallas_call | solution.py:581
  27.0 11.0 %all-to-all-done.recv_ref = bf16[16,288,128]{2,1,0:T(8,128)(2,1)S(1)} async-done(((bf16[16,288,128]{2,1,0:T(8,128)(2,1)}), bf16[16,288,128]{2,1,0:T(8,128)(2,1)S(1)}, u32[]{:S(2)}, u32[]{:S(2)}) %all-to-all-start) | async-done | bytes 1179680 | tf_op jit(solution)/shard_map/all_to_all | solution.py:721
  38.0 0.0 copy-start
  38.0 0.0 copy-start.2
  38.0 7.1 %column_heads.1 = bf16[16,4,8,512]{3,2,1,0:T(8,128)(2,1)} custom-call(bf16[16,288,128]{2,1,0:T(8,128)(2,1)S(1)} %all-to-all-done.recv_ref, f32[3,3,1024]{2,1,0:T(4,128)S(1)} %copy-done.3, f32[1,1024]{1,0:T(1,128)S(1)} %bitcast.7, f32[1,1024]{1,0:T(1,128)S(1)} %bitcast.9, f32[1,1024]{1,0:T(1,128)S(1)} %bitcast.11, ...), custom_call_target="tpu_custom_call" | custom-call | flops 1610612736 | bytes 8388608 | tf_op jit(solution)/shard_map/column_heads/pallas_call | solution.py:430
  45.1 22.0 %all_to_all.10.heads_ref = bf16[16,4,8,512]{3,2,1,0:T(8,128)(2,1)S(1)} all-to-all(bf16[16,4,8,512]{3,2,1,0:T(8,128)(2,1)} %column_heads.1), channel_id=1, replica_groups=mesh['groups'=2,'rows'=16] {'rows'}, dimensions={0} | all-to-all | bytes 1048576 | tf_op jit(solution)/shard_map/all_to_all | solution.py:738
  67.1 0.0 copy-done
  67.1 0.0 copy-done.2
  67.1 2.4 %last_projection.1 = bf16[2,256,1024]{2,1,0:T(8,128)(2,1)} custom-call(f32[2,256,1024]{2,1,0:T(8,128)S(1)} %bitcast.5, bf16[16,4,8,512]{3,2,1,0:T(8,128)(2,1)S(1)} %all_to_all.10.heads_ref, bf16[1024,1024]{1,0:T(8,128)(2,1)S(1)} %copy-done.2), custom_call_target="tpu_custom_call" | custom-call | flops 536870912 | bytes 5242880 | tf_op jit(solution)/shard_map/last_projection/pallas_call | solution.py:661
  (2 shorter events, 0.0 us)
Async XLA Ops:
  0.0 6.5 %copy-start.1 = (bf16[2,256,1024]{2,1,0:T(8,128)(2,1)S(1)}, bf16[2,256,1024]{2,1,0:T(8,128)(2,1)}, u32[]{:S(2)}) copy-start(bf16[2,256,1024]{2,1,0:T(8,128)(2,1)} %tokens_ref.3) | copy-start | bytes 3145732
  1.4 11.5 %collective-permute-start.1 = (bf16[1,256,1024]{2,1,0:T(8,128)(2,1)S(1)}, bf16[1,256,1024]{2,1,0:T(8,128)(2,1)}, u32[]{:S(2)}, u32[]{:S(2)}) collective-permute-start(bf16[1,256,1024]{2,1,0:T(8,128)(2,1)S(1)} %get-tuple-element.5), channel_id=1, source_target_pairs={{1,2},{2,1},{3,4},{4,3},{5,6},{6,5},{7,8},{8,7},{9,10},{10,9},{11,... | collective-permute-start | bytes 1572872 | tf_op jit(solution)/shard_map/ppermute | solution.py:720
  2.8 10.0 %copy-start.8 = (f32[3072]{0:T(1024)S(1)}, f32[3072]{0:T(1024)}, u32[]{:S(2)}) copy-start(f32[3072]{0:T(1024)} %param.15) | copy-start | bytes 36868
  2.8 10.1 %copy-start.3 = (f32[3,3,1024]{2,1,0:T(4,128)S(1)}, f32[3,3,1024]{2,1,0:T(4,128)}, u32[]{:S(2)}) copy-start(f32[3,3,1024]{2,1,0:T(4,128)} %peg_ref.3) | copy-start | bytes 110596
  2.8 10.1 %copy-start.4 = (f32[1024]{0:T(1024)S(1)}, f32[1024]{0:T(1024)}, u32[]{:S(2)}) copy-start(f32[1024]{0:T(1024)} %param.11) | copy-start | bytes 12292
  2.8 10.1 %copy-start.5 = (f32[1024]{0:T(1024)S(1)}, f32[1024]{0:T(1024)}, u32[]{:S(2)}) copy-start(f32[1024]{0:T(1024)} %param.12) | copy-start | bytes 12292
  2.8 10.1 %copy-start.6 = (f32[1024]{0:T(1024)S(1)}, f32[1024]{0:T(1024)}, u32[]{:S(2)}) copy-start(f32[1024]{0:T(1024)} %param.13) | copy-start | bytes 12292
  2.8 10.1 %copy-start.7 = (f32[1024]{0:T(1024)S(1)}, f32[1024]{0:T(1024)}, u32[]{:S(2)}) copy-start(f32[1024]{0:T(1024)} %param.17) | copy-start | bytes 12292
  2.9 10.1 %collective-permute-start = (bf16[1,256,1024]{2,1,0:T(8,128)(2,1)S(1)}, bf16[1,256,1024]{2,1,0:T(8,128)(2,1)}, u32[]{:S(2)}, u32[]{:S(2)}) collective-permute-start(bf16[1,256,1024]{2,1,0:T(8,128)(2,1)S(1)} %get-tuple-element.6), channel_id=1, source_target_pairs={{0,1},{1,0},{2,3},{3,2},{4,5},{5,4},{6,7},{7,6},{8,9},{9,8},{10,11... | collective-permute-start | bytes 1572872 | tf_op jit(solution)/shard_map/ppermute | solution.py:719
  7.9 30.1 %all-to-all-start = ((bf16[16,288,128]{2,1,0:T(8,128)(2,1)}), bf16[16,288,128]{2,1,0:T(8,128)(2,1)S(1)}, u32[]{:S(2)}, u32[]{:S(2)}) async-start(bf16[16,288,128]{2,1,0:T(8,128)(2,1)} %pack_columns.1), calls=%async_computation | async-start | bytes 2359296 | tf_op jit(solution)/shard_map/all_to_all | solution.py:721
  38.0 29.1 %copy-start = (f32[512,1024]{1,0:T(8,128)S(1)}, f32[512,1024]{1,0:T(8,128)}, u32[]{:S(2)}) copy-start(f32[512,1024]{1,0:T(8,128)} %row_heads.1.refs_0_) | copy-start | bytes 6291460
  38.0 29.1 %copy-start.2 = (bf16[1024,1024]{1,0:T(8,128)(2,1)S(1)}, bf16[1024,1024]{1,0:T(8,128)(2,1)}, u32[]{:S(2)}) copy-start(bf16[1024,1024]{1,0:T(8,128)(2,1)} %out_weight_ref.1) | copy-start | bytes 6291460

commit v4 on v3

--- a/solution.py
+++ b/solution.py
@@ -280,7 +280,7 @@
     qkv_hbm,
     *refs,
 ):
-    out_ref, mixed_scr, normed_scr, qkv_scr, weight_scr, sems = refs[-6:]
+    out_hbm, mixed_scr, normed_scr, qkv_scr, weight_scr, heads_scr, sems, out_sems = refs[-8:]
 
     devices = recv_ref.shape[0]
     slabs, _, tiles, _, _ = mixed_scr.shape
@@ -371,6 +371,7 @@
     mask = lax.rem(row_id, HALF) == lax.rem(col_id, HALF)
     scale = score_scale(height)
     block = 2 * group
+    sent = []
     for half in range(tiles // 2):
         for tile in range(2 * half, 2 * half + 2):
             for start in range(0, devices, HALF):
@@ -412,9 +413,15 @@
                     scale,
                     mask,
                 )
-                out_ref[:, tile, :, lanes] = heads.astype(jnp.bfloat16).reshape(
+                heads_scr[tile, :, :, lanes] = heads.astype(jnp.bfloat16).reshape(
                     devices, SUB, LANES
                 )
+            sent.append(
+                pltpu.make_async_copy(heads_scr.at[tile], out_hbm.at[:, tile], out_sems.at[tile])
+            )
+            sent[-1].start()
+    for copy in sent:
+        copy.wait()
 
 
 def column_part(recv, after, peg_weight, peg_bias, gain, nbias, qkv_weight, qkv_bias):
@@ -430,14 +437,16 @@
     return pl.pallas_call(
         column_kernel,
         in_specs=[vmem] * 6 + [pl.BlockSpec(memory_space=pltpu.HBM)] * (1 + len(after)),
-        out_specs=vmem,
+        out_specs=pl.BlockSpec(memory_space=pltpu.HBM),
         out_shape=pltpu.HBM((devices, tiles, SUB, features), jnp.bfloat16),
         scratch_shapes=[
             pltpu.VMEM((slabs, devices, tiles, SUB, LANES), jnp.float32),
             pltpu.VMEM((tokens, model), jnp.bfloat16),
             pltpu.VMEM((3, tokens, features), jnp.bfloat16),
             pltpu.VMEM((3, model, features), jnp.bfloat16),
+            pltpu.VMEM((tiles, devices, SUB, features), jnp.bfloat16),
             pltpu.SemaphoreType.DMA((3, 1)),
+            pltpu.SemaphoreType.DMA((tiles,)),
         ],
         compiler_params=pltpu.CompilerParams(vmem_limit_bytes=9 * MIB),
         cost_estimate=pl.CostEstimate(
@@ -628,46 +637,50 @@
     )
 
 
-def last_kernel(partial_ref, heads_ref, out_weight_ref, result_ref):
+def last_kernel(partial_ref, heads_ref, out_weight_ref, out_hbm, result_scr, sems):
     devices, tiles, sub, features = heads_ref.shape
-    _, width, model = result_ref.shape
+    bands, width, model = result_scr.shape
     first = ROW_HEADS * DH
+    block = model // sems.shape[0]
     heads = heads_ref[...].reshape(devices * tiles * sub, features)
-    upper = lax.broadcasted_iota(jnp.int32, (1, sub, 2 * LANES), 1) < HALF
-    start = pl.multiple_of(pl.program_id(0) * width, width)
-    for slab in range(model // (2 * LANES)):
-        lanes = slice(slab * 2 * LANES, (slab + 1) * 2 * LANES)
+    upper = lax.broadcasted_iota(jnp.int32, (1, sub, block), 1) < HALF
+    copies = []
+    for step in range(sems.shape[0]):
+        lanes = slice(step * block, (step + 1) * block)
         projected = jnp.dot(
             heads, out_weight_ref[first:, lanes], preferred_element_type=jnp.float32
         )
-        pairs = projected.reshape(devices * tiles // 2, 2, sub, 2 * LANES)
+        pairs = projected.reshape(devices * tiles // 2, 2, sub, block)
         low, high = pairs[:, 0], pairs[:, 1]
         rows = (
             jnp.where(upper, low, pltpu.roll(high, HALF, 1)),
             jnp.where(upper, pltpu.roll(low, HALF, 1), high),
         )
         for band, value in enumerate(rows):
-            result_ref[band, :, lanes] = (
-                partial_ref[band, pl.ds(start, width), lanes]
-                + value.reshape(width, 2 * LANES)
+            result_scr[band, :, lanes] = (
+                partial_ref[band, :, lanes] + value.reshape(width, block)
             ).astype(jnp.bfloat16)
+        copy = pltpu.make_async_copy(
+            result_scr.at[:, :, lanes], out_hbm.at[:, :, lanes], sems.at[step]
+        )
+        copy.start()
+        copies.append(copy)
+    for copy in copies:
+        copy.wait()
 
 
 def last_part(partial, heads, out_weight, bands, width):
-    devices, tiles, sub, features = heads.shape
+    features = heads.shape[3]
     model = out_weight.shape[1]
-    steps = 4
-    vmem = pl.BlockSpec(memory_space=pltpu.VMEM)
     return pl.pallas_call(
         last_kernel,
-        grid=(steps,),
-        in_specs=[
-            vmem,
-            pl.BlockSpec((devices // steps, tiles, sub, features), lambda i: (i, 0, 0, 0)),
-            vmem,
+        in_specs=[pl.BlockSpec(memory_space=pltpu.VMEM)] * 3,
+        out_specs=pl.BlockSpec(memory_space=pltpu.HBM),
+        out_shape=jax.ShapeDtypeStruct((bands, width, model), jnp.bfloat16),
+        scratch_shapes=[
+            pltpu.VMEM((bands, width, model), jnp.bfloat16),
+            pltpu.SemaphoreType.DMA((4,)),
         ],
-        out_specs=pl.BlockSpec((bands, width // steps, model), lambda i: (0, i, 0)),
-        out_shape=jax.ShapeDtypeStruct((bands, width, model), jnp.bfloat16),
         compiler_params=pltpu.CompilerParams(vmem_limit_bytes=8 * MIB),
         cost_estimate=pl.CostEstimate(
             flops=2 * bands * width * features * model,

time: 70 us -> 69.1 us (0.987)
  Pallas kernels: 24.8 us -> 23.9 us
    pallas_call x1, Pallas kernels: 2.37 us -> 1.59 us  [last_part(): pl.pallas_call(last_kernel, in_specs=[pl.BlockSpec(memory_space=pltpu.VME...]
where the time goes in v4:
time: 69.1 us; the launch traced here: 68.6 us
  Pallas kernels  23.9 us (35%)
  blocking collectives  22 us (32%)
  waiting for transfers between devices  11 us (16%)
  starting transfers between devices  10.1 us (15%)
  local copies, waits for them, and re-layouts  1.41 us (2%)
    all_to_all x1, blocking collectives, on_device(): lax.all_to_all(col_heads, 'rows', split_axis=0, concat_axis=0, tiled=True)  22 us
    pallas_call x1, Pallas kernels, row_part(): pl.pallas_call(row_kernel, grid=(slabs,), in_specs=[pl.BlockSpec((bands,...  14 us
    all_to_all x1, waiting for transfers between devices, on_device(): lax.all_to_all(packed, 'rows', split_axis=0, concat_axis=0, tiled=True)  11 us
    pallas_call x1, Pallas kernels, column_part(): pl.pallas_call(column_kernel, in_specs=[vmem] * 6 + [pl.BlockSpec(memory_...  7 us
    all_to_all x1, starting transfers between devices, on_device(): lax.all_to_all(packed, 'rows', split_axis=0, concat_axis=0, tiled=True)  4.99 us
    ppermute x1, starting transfers between devices, on_device(): intra = lax.ppermute(intra, 'rows', same_chip)  3.64 us
    pallas_call x1, Pallas kernels, last_part(): pl.pallas_call(last_kernel, in_specs=[pl.BlockSpec(memory_space=pltpu.VME...  1.59 us
    ppermute x1, starting transfers between devices, on_device(): inter = lax.ppermute(inter, 'rows', other_chip)  1.47 us
  transfers between devices with their start and end apart: 3, of which 1 were waited for; matrix products, arithmetic and copies ran while one was open for 0% of the time, Pallas kernels for 22%

profile of v4, /device:TPU:0, one launch (start us, length us, event | category | flops | bytes accessed | tf_op | source)
XLA Modules:
  0.0 68.6 jit_solution(1636575192458021408)
XLA Ops:
  0.0 0.0 copy-start.1
  0.0 1.4 %constant_dynamic-slice_fusion = (bf16[1,256,1024]{2,1,0:T(8,128)(2,1)S(1)}, bf16[1,256,1024]{2,1,0:T(8,128)(2,1)S(1)}) fusion(bf16[2,256,1024]{2,1,0:T(8,128)(2,1)} %tokens_ref.3, s32[]{:T(128)S(6)} %select_n.7, s32[]{:T(128)S(6)} %select_n.6), kind=kLoop, calls=%fused_computation | loop fusion | bytes 2097160 | tf_op jit(solution)/shard_map/dynamic_slice | solution.py:729
  1.4 1.5 %collective-permute-start.1 = (bf16[1,256,1024]{2,1,0:T(8,128)(2,1)S(1)}, bf16[1,256,1024]{2,1,0:T(8,128)(2,1)}, u32[]{:S(2)}, u32[]{:S(2)}) collective-permute-start(bf16[1,256,1024]{2,1,0:T(8,128)(2,1)S(1)} %get-tuple-element.5), channel_id=1, source_target_pairs={{1,2},{2,1},{3,4},{4,3},{5,6},{6,5},{7,8},{8,7},{9,10},{10,9},{11,... | collective-permute-start | bytes 1572872 | tf_op jit(solution)/shard_map/ppermute | solution.py:733
  2.8 0.0 copy-start.8
  2.8 0.0 copy-start.3
  2.8 0.0 copy-start.4
  2.8 0.0 copy-start.5
  2.8 0.0 copy-start.6
  2.8 0.0 copy-start.7
  2.9 3.6 %collective-permute-start = (bf16[1,256,1024]{2,1,0:T(8,128)(2,1)S(1)}, bf16[1,256,1024]{2,1,0:T(8,128)(2,1)}, u32[]{:S(2)}, u32[]{:S(2)}) collective-permute-start(bf16[1,256,1024]{2,1,0:T(8,128)(2,1)S(1)} %get-tuple-element.6), channel_id=1, source_target_pairs={{0,1},{1,0},{2,3},{3,2},{4,5},{5,4},{6,7},{7,6},{8,9},{9,8},{10,11... | collective-permute-start | bytes 1572872 | tf_op jit(solution)/shard_map/ppermute | solution.py:732
  6.5 0.0 copy-done.1
  6.5 1.4 %pack_columns.1 = bf16[16,288,128]{2,1,0:T(8,128)(2,1)} custom-call(bf16[2,256,1024]{2,1,0:T(8,128)(2,1)S(1)} %copy-done.1), custom_call_target="tpu_custom_call" | custom-call | tf_op jit(solution)/shard_map/pack_columns/pallas_call | solution.py:191
  7.9 5.0 %all-to-all-start = ((bf16[16,288,128]{2,1,0:T(8,128)(2,1)}), bf16[16,288,128]{2,1,0:T(8,128)(2,1)S(1)}, u32[]{:S(2)}, u32[]{:S(2)}) async-start(bf16[16,288,128]{2,1,0:T(8,128)(2,1)} %pack_columns.1), calls=%async_computation | async-start | bytes 2359296 | tf_op jit(solution)/shard_map/all_to_all | solution.py:734
  12.9 0.0 copy-done.8
  12.9 0.0 collective-permute-done.1.inter_ref
  12.9 0.0 collective-permute-done.intra_ref
  12.9 0.0 copy-done.3
  12.9 0.0 copy-done.4
  12.9 0.0 copy-done.5
  13.0 0.0 copy-done.6
  13.0 0.0 copy-done.7
  13.0 14.0 %row_heads.1.refs_0_ = f32[512,1024]{1,0:T(8,128)} custom-call(bf16[2,256,1024]{2,1,0:T(8,128)(2,1)S(1)} %copy-done.1, bf16[1,256,1024]{2,1,0:T(8,128)(2,1)} %collective-permute-done.intra_ref, bf16[1,256,1024]{2,1,0:T(8,128)(2,1)} %collective-permute-done.1.inter_ref, f32[3,3,1024]{2,1,0:T(4,128)S(1)} %copy-done.3, f32[1,1024]{1,0:T(1,128)S(1)} %bitcast.6, ...), custom_call_target="tpu_custom_call" | custom-call | flops 42949672960 | bytes 10485760 | tf_op jit(solution)/shard_map/row_heads/pallas_call | solution.py:590
  27.0 11.0 %all-to-all-done.recv_ref = bf16[16,288,128]{2,1,0:T(8,128)(2,1)S(1)} async-done(((bf16[16,288,128]{2,1,0:T(8,128)(2,1)}), bf16[16,288,128]{2,1,0:T(8,128)(2,1)S(1)}, u32[]{:S(2)}, u32[]{:S(2)}) %all-to-all-start) | async-done | bytes 1179680 | tf_op jit(solution)/shard_map/all_to_all | solution.py:734
  38.0 0.0 copy-start
  38.0 0.0 copy-start.2
  38.0 7.0 %column_heads.1 = bf16[16,4,8,512]{3,2,1,0:T(8,128)(2,1)} custom-call(bf16[16,288,128]{2,1,0:T(8,128)(2,1)S(1)} %all-to-all-done.recv_ref, f32[3,3,1024]{2,1,0:T(4,128)S(1)} %copy-done.3, f32[1,1024]{1,0:T(1,128)S(1)} %bitcast.7, f32[1,1024]{1,0:T(1,128)S(1)} %bitcast.9, f32[1,1024]{1,0:T(1,128)S(1)} %bitcast.11, ...), custom_call_target="tpu_custom_call" | custom-call | flops 1610612736 | bytes 8388608 | tf_op jit(solution)/shard_map/column_heads/pallas_call | solution.py:437
  45.0 22.0 %all_to_all.10.heads_ref = bf16[16,4,8,512]{3,2,1,0:T(8,128)(2,1)S(1)} all-to-all(bf16[16,4,8,512]{3,2,1,0:T(8,128)(2,1)} %column_heads.1), channel_id=1, replica_groups=mesh['groups'=2,'rows'=16] {'rows'}, dimensions={0} | all-to-all | bytes 1048576 | tf_op jit(solution)/shard_map/all_to_all | solution.py:751
  67.0 0.0 copy-done
  67.0 0.0 copy-done.2
  67.0 1.6 %last_projection.1 = bf16[2,256,1024]{2,1,0:T(8,128)(2,1)} custom-call(f32[2,256,1024]{2,1,0:T(8,128)S(1)} %bitcast.5, bf16[16,4,8,512]{3,2,1,0:T(8,128)(2,1)S(1)} %all_to_all.10.heads_ref, bf16[1024,1024]{1,0:T(8,128)(2,1)S(1)} %copy-done.2), custom_call_target="tpu_custom_call" | custom-call | flops 536870912 | bytes 5242880 | tf_op jit(solution)/shard_map/last_projection/pallas_call | solution.py:675
  (2 shorter events, 0.0 us)
Async XLA Ops:
  0.0 6.5 %copy-start.1 = (bf16[2,256,1024]{2,1,0:T(8,128)(2,1)S(1)}, bf16[2,256,1024]{2,1,0:T(8,128)(2,1)}, u32[]{:S(2)}) copy-start(bf16[2,256,1024]{2,1,0:T(8,128)(2,1)} %tokens_ref.3) | copy-start | bytes 3145732
  1.4 11.5 %collective-permute-start.1 = (bf16[1,256,1024]{2,1,0:T(8,128)(2,1)S(1)}, bf16[1,256,1024]{2,1,0:T(8,128)(2,1)}, u32[]{:S(2)}, u32[]{:S(2)}) collective-permute-start(bf16[1,256,1024]{2,1,0:T(8,128)(2,1)S(1)} %get-tuple-element.5), channel_id=1, source_target_pairs={{1,2},{2,1},{3,4},{4,3},{5,6},{6,5},{7,8},{8,7},{9,10},{10,9},{11,... | collective-permute-start | bytes 1572872 | tf_op jit(solution)/shard_map/ppermute | solution.py:733
  2.8 10.0 %copy-start.8 = (f32[3072]{0:T(1024)S(1)}, f32[3072]{0:T(1024)}, u32[]{:S(2)}) copy-start(f32[3072]{0:T(1024)} %param.15) | copy-start | bytes 36868
  2.8 10.1 %copy-start.3 = (f32[3,3,1024]{2,1,0:T(4,128)S(1)}, f32[3,3,1024]{2,1,0:T(4,128)}, u32[]{:S(2)}) copy-start(f32[3,3,1024]{2,1,0:T(4,128)} %peg_ref.3) | copy-start | bytes 110596
  2.8 10.1 %copy-start.4 = (f32[1024]{0:T(1024)S(1)}, f32[1024]{0:T(1024)}, u32[]{:S(2)}) copy-start(f32[1024]{0:T(1024)} %param.11) | copy-start | bytes 12292
  2.8 10.1 %copy-start.5 = (f32[1024]{0:T(1024)S(1)}, f32[1024]{0:T(1024)}, u32[]{:S(2)}) copy-start(f32[1024]{0:T(1024)} %param.12) | copy-start | bytes 12292
  2.8 10.1 %copy-start.6 = (f32[1024]{0:T(1024)S(1)}, f32[1024]{0:T(1024)}, u32[]{:S(2)}) copy-start(f32[1024]{0:T(1024)} %param.13) | copy-start | bytes 12292
  2.8 10.1 %copy-start.7 = (f32[1024]{0:T(1024)S(1)}, f32[1024]{0:T(1024)}, u32[]{:S(2)}) copy-start(f32[1024]{0:T(1024)} %param.17) | copy-start | bytes 12292
  2.9 10.1 %collective-permute-start = (bf16[1,256,1024]{2,1,0:T(8,128)(2,1)S(1)}, bf16[1,256,1024]{2,1,0:T(8,128)(2,1)}, u32[]{:S(2)}, u32[]{:S(2)}) collective-permute-start(bf16[1,256,1024]{2,1,0:T(8,128)(2,1)S(1)} %get-tuple-element.6), channel_id=1, source_target_pairs={{0,1},{1,0},{2,3},{3,2},{4,5},{5,4},{6,7},{7,6},{8,9},{9,8},{10,11... | collective-permute-start | bytes 1572872 | tf_op jit(solution)/shard_map/ppermute | solution.py:732
  7.9 30.1 %all-to-all-start = ((bf16[16,288,128]{2,1,0:T(8,128)(2,1)}), bf16[16,288,128]{2,1,0:T(8,128)(2,1)S(1)}, u32[]{:S(2)}, u32[]{:S(2)}) async-start(bf16[16,288,128]{2,1,0:T(8,128)(2,1)} %pack_columns.1), calls=%async_computation | async-start | bytes 2359296 | tf_op jit(solution)/shard_map/all_to_all | solution.py:734
  38.0 29.0 %copy-start = (f32[512,1024]{1,0:T(8,128)S(1)}, f32[512,1024]{1,0:T(8,128)}, u32[]{:S(2)}) copy-start(f32[512,1024]{1,0:T(8,128)} %row_heads.1.refs_0_) | copy-start | bytes 6291460
  38.0 29.0 %copy-start.2 = (bf16[1024,1024]{1,0:T(8,128)(2,1)S(1)}, bf16[1024,1024]{1,0:T(8,128)(2,1)}, u32[]{:S(2)}) copy-start(bf16[1024,1024]{1,0:T(8,128)(2,1)} %out_weight_ref.1) | copy-start | bytes 6291460

commit v5 on v4

--- a/solution.py
+++ b/solution.py
@@ -128,21 +128,47 @@
     return low, high
 
 
-def pack_kernel(devices, per_step, tokens_ref, out_hbm, out_scr, sems):
-    _, width, model = tokens_ref.shape
+def front_kernel(
+    devices,
+    tokens_hbm,
+    packed_hbm,
+    intra_ref,
+    inter_ref,
+    tokens_scr,
+    packed_scr,
+    in_sems,
+    row_sems,
+    out_sems,
+):
+    _, width, model = tokens_scr.shape
     cols = width // devices
     slabs = model // LANES
     tiles = cols // HALF
+    steps = in_sems.shape[0]
+    per_step = devices // steps
     place = lax.broadcasted_iota(jnp.int32, (SUB, LANES), 0)
 
-    def copy(dest):
-        return pltpu.make_async_copy(out_scr.at[dest], out_hbm.at[dest], sems.at[dest])
+    arrivals = []
+    for step in range(steps):
+        span = pl.ds(step * per_step * cols, per_step * cols)
+        arrivals.append(
+            pltpu.make_async_copy(
+                tokens_hbm.at[:, span], tokens_scr.at[:, span], in_sems.at[step]
+            )
+        )
+    odd = lax.rem(lax.axis_index("rows"), 2)
+    cuts = [
+        pltpu.make_async_copy(tokens_hbm.at[pl.ds(odd, 1)], inter_ref, row_sems.at[0]),
+        pltpu.make_async_copy(tokens_hbm.at[pl.ds(1 - odd, 1)], intra_ref, row_sems.at[1]),
+    ]
+    for copy in arrivals + cuts:
+        copy.start()
+
+    def columns(dest, band):
+        return tokens_scr[band, dest * cols : (dest + 1) * cols, :].astype(jnp.float32)
 
     def fill(dest):
-        start = pl.multiple_of(dest * cols, cols)
-        left_start = pl.multiple_of(jnp.maximum(dest - 1, 0) * cols, cols)
-        right_start = pl.multiple_of(jnp.minimum(dest + 1, devices - 1) * cols, cols)
-        own = [tokens_ref[band, pl.ds(start, cols), :].astype(jnp.float32) for band in range(2)]
+        own = [columns(dest, band) for band in range(2)]
         for eight in range(cols // SUB):
             rows = slice(eight * SUB, (eight + 1) * SUB)
             pair = interleave(own[0][rows], own[1][rows])
@@ -150,13 +176,15 @@
                 tile = pair[which].astype(jnp.bfloat16)
                 for slab in range(slabs):
                     base = (slab * tiles + eight * 2 + which) * SUB
-                    out_scr[dest, base : base + SUB, :] = tile[:, slab * LANES : (slab + 1) * LANES]
-        lefts, rights = [], []
-        for band in range(2):
-            left = tokens_ref[band, pl.ds(left_start, cols), :].astype(jnp.float32)
-            right = tokens_ref[band, pl.ds(right_start, cols), :].astype(jnp.float32)
-            lefts.append(jnp.where(dest > 0, left[cols - 1 : cols], 0.0))
-            rights.append(jnp.where(dest < devices - 1, right[0:1], 0.0))
+                    packed_scr[dest, base : base + SUB, :] = tile[
+                        :, slab * LANES : (slab + 1) * LANES
+                    ]
+        outside = jnp.zeros((1, model), jnp.float32)
+        lefts, rights = [outside, outside], [outside, outside]
+        if dest > 0:
+            lefts = [columns(dest - 1, band)[cols - 1 : cols] for band in range(2)]
+        if dest < devices - 1:
+            rights = [columns(dest + 1, band)[0:1] for band in range(2)]
         for two in range(slabs // 2):
             one = slice(2 * two * LANES, (2 * two + 1) * LANES)
             other = slice((2 * two + 1) * LANES, (2 * two + 2) * LANES)
@@ -166,58 +194,47 @@
             for index in range(1, SUB):
                 tile = jnp.where(place == index, order[index], tile)
             base = (slabs * tiles + two) * SUB
-            out_scr[dest, base : base + SUB, :] = tile.astype(jnp.bfloat16)
-
-    def send(step, carry):
-        for k in range(per_step):
-            fill(step * per_step + k)
-            copy(step * per_step + k).start()
-        return carry
-
-    def finish(dest, carry):
-        copy(dest).wait()
-        return carry
-
-    lax.fori_loop(0, devices // per_step, send, 0)
-    lax.fori_loop(0, devices, finish, 0)
-
-
-def pack(tokens, devices):
+            packed_scr[dest, base : base + SUB, :] = tile.astype(jnp.bfloat16)
+
+    sent = []
+    arrivals[0].wait()
+    for step in range(steps):
+        if step + 1 < steps:
+            arrivals[step + 1].wait()
+        for dest in range(step * per_step, (step + 1) * per_step):
+            fill(dest)
+            sent.append(
+                pltpu.make_async_copy(
+                    packed_scr.at[dest], packed_hbm.at[dest], out_sems.at[dest]
+                )
+            )
+            sent[-1].start()
+    for copy in cuts + sent:
+        copy.wait()
+
+
+def front(tokens, devices):
     bands, width, model = tokens.shape
     cols = width // devices
     slabs = model // LANES
     rows = slabs * bands * (cols + 2)
-    per_step = 4
     return pl.pallas_call(
-        functools.partial(pack_kernel, devices, per_step),
-        in_specs=[pl.BlockSpec(memory_space=pltpu.VMEM)],
-        out_specs=pl.BlockSpec(memory_space=pltpu.HBM),
-        out_shape=jax.ShapeDtypeStruct((devices, rows, LANES), jnp.bfloat16),
+        functools.partial(front_kernel, devices),
+        in_specs=[pl.BlockSpec(memory_space=pltpu.HBM)],
+        out_specs=[pl.BlockSpec(memory_space=pltpu.HBM)]
+        + [pl.BlockSpec(memory_space=pltpu.VMEM)] * 2,
+        out_shape=[jax.ShapeDtypeStruct((devices, rows, LANES), jnp.bfloat16)]
+        + [pltpu.VMEM((1, width, model), jnp.bfloat16)] * 2,
         scratch_shapes=[
+            pltpu.VMEM((bands, width, model), jnp.bfloat16),
             pltpu.VMEM((devices, rows, LANES), jnp.bfloat16),
+            pltpu.SemaphoreType.DMA((4,)),
+            pltpu.SemaphoreType.DMA((2,)),
             pltpu.SemaphoreType.DMA((devices,)),
         ],
         compiler_params=pltpu.CompilerParams(vmem_limit_bytes=6 * MIB),
-        name="pack_columns",
-    )(tokens)
-
-
-def gate_kernel(*refs):
-    pass
-
-
-def gate(values, *after):
-    hbm = pl.BlockSpec(memory_space=pltpu.HBM)
-    anywhere = pl.BlockSpec(memory_space=pl.ANY)
-    count = len(values)
-    return pl.pallas_call(
-        gate_kernel,
-        in_specs=[hbm] * count + [anywhere] * len(after),
-        out_specs=[hbm] * count,
-        out_shape=[jax.ShapeDtypeStruct(value.shape, value.dtype) for value in values],
-        input_output_aliases={index: index for index in range(count)},
-        name="gate",
-    )(*values, *after)
+        name="front",
+    )(in_hbm(tokens))
 
 
 def in_hbm(value):
@@ -492,6 +509,7 @@
     step = pl.program_id(0)
     slabs = pl.num_programs(0)
     bands, width, _ = tokens_ref.shape
+    here = pl.ds(pl.multiple_of(step * LANES, LANES), LANES)
     features = weight_scr.shape[2]
 
     def copies():
@@ -505,10 +523,10 @@
                 copy.start()
 
     odd = lax.rem(lax.axis_index("rows"), 2) == 1
-    intra = intra_ref[0].astype(jnp.float32)
-    inter = inter_ref[0].astype(jnp.float32)
+    intra = intra_ref[0, :, here].astype(jnp.float32)
+    inter = inter_ref[0, :, here].astype(jnp.float32)
     rows = [jnp.where(odd, intra, inter)]
-    rows += [tokens_ref[band].astype(jnp.float32) for band in range(bands)]
+    rows += [tokens_ref[band, :, here].astype(jnp.float32) for band in range(bands)]
     rows += [jnp.where(odd, inter, intra)]
     position = lax.broadcasted_iota(jnp.int32, (width, LANES), 0)
     for band in range(bands):
@@ -591,9 +609,9 @@
         row_kernel,
         grid=(slabs,),
         in_specs=[
-            pl.BlockSpec((bands, width, LANES), lambda i: (0, 0, i)),
-            pl.BlockSpec((1, width, LANES), lambda i: (0, 0, i)),
-            pl.BlockSpec((1, width, LANES), lambda i: (0, 0, i)),
+            pl.BlockSpec(memory_space=pltpu.VMEM),
+            pl.BlockSpec(memory_space=pltpu.VMEM),
+            pl.BlockSpec(memory_space=pltpu.VMEM),
             pl.BlockSpec((3, 3, LANES), lambda i: (0, 0, i)),
             pl.BlockSpec((1, LANES), lambda i: (0, i)),
             pl.BlockSpec((1, model), whole2),
@@ -723,14 +741,11 @@
     out_bias = out_bias.reshape(1, model)
     qkv_bias = qkv_bias.reshape(3, model)
 
-    packed = pack(tokens, devices)
-    odd = lax.rem(lax.axis_index("rows"), 2)
-    intra = lax.dynamic_slice_in_dim(tokens, 1 - odd, 1, axis=0)
-    inter = lax.dynamic_slice_in_dim(tokens, odd, 1, axis=0)
+    packed, intra, inter = front(tokens, devices)
     same_chip = [(i, i ^ 1) for i in range(devices)]
     other_chip = [(i, i + 1 if i % 2 else i - 1) for i in range(1, devices - 1)]
+    inter = lax.ppermute(inter, "rows", other_chip)
     intra = lax.ppermute(intra, "rows", same_chip)
-    inter = lax.ppermute(inter, "rows", other_chip)
     received = lax.all_to_all(packed, "rows", split_axis=0, concat_axis=0, tiled=True)
     partial = row_part(
         tokens,

time: 69.1 us -> 68.5 us (level)
  waiting for transfers between devices: 11 us -> 13.5 us
  Pallas kernels: 23.9 us -> 22.5 us
  local copies, waits for them, and re-layouts: 1.41 us -> 0.05 us
    ppermute x1, starting transfers between devices: 3.64 us -> 0.57 us  [on_device(): intra = lax.ppermute(intra, 'rows', same_chip)]
    all_to_all x1, starting transfers between devices: 4.99 us -> 7.98 us  [on_device(): lax.all_to_all(packed, 'rows', split_axis=0, concat_axis=0, tiled=True)]
    all_to_all x1, waiting for transfers between devices: 11 us -> 13.5 us  [on_device(): lax.all_to_all(packed, 'rows', split_axis=0, concat_axis=0, tiled=True)]
    pallas_call x2, Pallas kernels: 15.3 us -> 13.9 us  [the longest x1 11.5 us: row_part(): pl.pallas_call(row_kernel, grid=(slabs,), in_specs=[pl.BlockSpec(memory_s...]
    dynamic_slice x1 -> x0, local copies, waits for them, and re-layouts: 1.36 us -> none  [on_device(): inter = lax.dynamic_slice_in_dim(tokens, odd, 1, axis=0)]
  transfers between devices with their start and end apart: 3 -> 3, of which waited for: 1 -> 1; matrix products, arithmetic and copies ran while one was open for 0% -> 0% of each run, Pallas kernels for 22% -> 17%
where the time goes in v5:
time: 68.5 us; the launch traced here: 68.2 us
  Pallas kernels  22.5 us (33%)
  blocking collectives  22 us (32%)
  waiting for transfers between devices  13.5 us (20%)
  starting transfers between devices  10 us (15%)
    all_to_all x1, blocking collectives, on_device(): lax.all_to_all(col_heads, 'rows', split_axis=0, concat_axis=0, tiled=True)  22 us
    all_to_all x1, waiting for transfers between devices, on_device(): lax.all_to_all(packed, 'rows', split_axis=0, concat_axis=0, tiled=True)  13.5 us
    pallas_call x1, Pallas kernels, row_part(): pl.pallas_call(row_kernel, grid=(slabs,), in_specs=[pl.BlockSpec(memory_s...  11.5 us
    all_to_all x1, starting transfers between devices, on_device(): lax.all_to_all(packed, 'rows', split_axis=0, concat_axis=0, tiled=True)  7.98 us
    pallas_call x1, Pallas kernels, column_part(): pl.pallas_call(column_kernel, in_specs=[vmem] * 6 + [pl.BlockSpec(memory_...  6.99 us
    pallas_call x1, Pallas kernels, front(): pl.pallas_call(functools.partial(front_kernel, devices), in_specs=[pl.Blo...  2.39 us
    pallas_call x1, Pallas kernels, last_part(): pl.pallas_call(last_kernel, in_specs=[pl.BlockSpec(memory_space=pltpu.VME...  1.6 us
    ppermute x1, starting transfers between devices, on_device(): inter = lax.ppermute(inter, 'rows', other_chip)  1.46 us
  transfers between devices with their start and end apart: 3, of which 1 were waited for; matrix products, arithmetic and copies ran while one was open for 0% of the time, Pallas kernels for 17%

profile of v5, /device:TPU:0, one launch (start us, length us, event | category | flops | bytes accessed | tf_op | source)
XLA Modules:
  0.0 68.2 jit_solution(160356838074521568)
XLA Ops:
  0.0 0.0 copy-start.2
  0.0 0.0 copy-start.8
  0.0 0.0 copy-start.3
  0.0 0.0 copy-start.7
  0.0 0.0 copy-start.6
  0.0 0.0 copy-start.5
  0.0 0.0 copy-start.4
  0.0 2.4 %front.1 = (bf16[16,288,128]{2,1,0:T(8,128)(2,1)}, bf16[1,256,1024]{2,1,0:T(8,128)(2,1)S(1)}, bf16[1,256,1024]{2,1,0:T(8,128)(2,1)S(1)}) custom-call(bf16[2,256,1024]{2,1,0:T(8,128)(2,1)} %tokens_ref.1), custom_call_target="tpu_custom_call" | custom-call | tf_op jit(solution)/shard_map/front/pallas_call | solution.py:221
  2.4 0.6 collective-permute-start
  3.0 1.5 %collective-permute-start.1 = (bf16[1,256,1024]{2,1,0:T(8,128)(2,1)S(1)}, bf16[1,256,1024]{2,1,0:T(8,128)(2,1)}, u32[]{:S(2)}, u32[]{:S(2)}) collective-permute-start(bf16[1,256,1024]{2,1,0:T(8,128)(2,1)S(1)} %get-tuple-element.9), channel_id=1, source_target_pairs={{1,2},{2,1},{3,4},{4,3},{5,6},{6,5},{7,8},{8,7},{9,10},{10,9},{11,... | collective-permute-start | bytes 1572872 | tf_op jit(solution)/shard_map/ppermute | solution.py:747
  4.5 8.0 %all-to-all-start = ((bf16[16,288,128]{2,1,0:T(8,128)(2,1)}), bf16[16,288,128]{2,1,0:T(8,128)(2,1)S(1)}, u32[]{:S(2)}, u32[]{:S(2)}) async-start(bf16[16,288,128]{2,1,0:T(8,128)(2,1)} %get-tuple-element.10), calls=%async_computation | async-start | bytes 2359296 | tf_op jit(solution)/shard_map/all_to_all | solution.py:749
  12.4 0.0 copy-done.8
  12.5 0.0 collective-permute-done.intra_ref
  12.5 0.0 collective-permute-done.1.inter_ref
  12.5 0.0 copy-done.2
  12.5 0.0 copy-done.3
  12.5 0.0 copy-done.7
  12.5 0.0 copy-done.6
  12.5 0.0 copy-done.5
  12.6 0.0 copy-done.4
  12.6 11.5 %row_heads.1.refs_0_ = f32[512,1024]{1,0:T(8,128)} custom-call(bf16[2,256,1024]{2,1,0:T(8,128)(2,1)S(1)} %copy-done.2, bf16[1,256,1024]{2,1,0:T(8,128)(2,1)} %collective-permute-done.intra_ref, bf16[1,256,1024]{2,1,0:T(8,128)(2,1)} %collective-permute-done.1.inter_ref, f32[3,3,1024]{2,1,0:T(4,128)S(1)} %copy-done.3, f32[1,1024]{1,0:T(1,128)S(1)} %bitcast.6, ...), custom_call_target="tpu_custom_call" | custom-call | flops 42949672960 | bytes 10485760 | tf_op jit(solution)/shard_map/row_heads/pallas_call | solution.py:608
  24.1 13.5 %all-to-all-done.recv_ref = bf16[16,288,128]{2,1,0:T(8,128)(2,1)S(1)} async-done(((bf16[16,288,128]{2,1,0:T(8,128)(2,1)}), bf16[16,288,128]{2,1,0:T(8,128)(2,1)S(1)}, u32[]{:S(2)}, u32[]{:S(2)}) %all-to-all-start) | async-done | bytes 1179680 | tf_op jit(solution)/shard_map/all_to_all | solution.py:749
  37.6 0.0 copy-start
  37.6 0.0 copy-start.1
  37.6 7.0 %column_heads.1 = bf16[16,4,8,512]{3,2,1,0:T(8,128)(2,1)} custom-call(bf16[16,288,128]{2,1,0:T(8,128)(2,1)S(1)} %all-to-all-done.recv_ref, f32[3,3,1024]{2,1,0:T(4,128)S(1)} %copy-done.3, f32[1,1024]{1,0:T(1,128)S(1)} %bitcast.7, f32[1,1024]{1,0:T(1,128)S(1)} %bitcast.9, f32[1,1024]{1,0:T(1,128)S(1)} %bitcast.11, ...), custom_call_target="tpu_custom_call" | custom-call | flops 1610612736 | bytes 8388608 | tf_op jit(solution)/shard_map/column_heads/pallas_call | solution.py:454
  44.6 22.0 %all_to_all.10.heads_ref = bf16[16,4,8,512]{3,2,1,0:T(8,128)(2,1)S(1)} all-to-all(bf16[16,4,8,512]{3,2,1,0:T(8,128)(2,1)} %column_heads.1), channel_id=1, replica_groups=mesh['groups'=2,'rows'=16] {'rows'}, dimensions={0} | all-to-all | bytes 1048576 | tf_op jit(solution)/shard_map/all_to_all | solution.py:766
  66.6 0.0 copy-done
  66.6 0.0 copy-done.1
  66.6 1.6 %last_projection.1 = bf16[2,256,1024]{2,1,0:T(8,128)(2,1)} custom-call(f32[2,256,1024]{2,1,0:T(8,128)S(1)} %bitcast.5, bf16[16,4,8,512]{3,2,1,0:T(8,128)(2,1)S(1)} %all_to_all.10.heads_ref, bf16[1024,1024]{1,0:T(8,128)(2,1)S(1)} %copy-done.1), custom_call_target="tpu_custom_call" | custom-call | flops 536870912 | bytes 5242880 | tf_op jit(solution)/shard_map/last_projection/pallas_call | solution.py:693
  (2 shorter events, 0.0 us)
Async XLA Ops:
  0.0 12.5 %copy-start.2 = (bf16[2,256,1024]{2,1,0:T(8,128)(2,1)S(1)}, bf16[2,256,1024]{2,1,0:T(8,128)(2,1)}, u32[]{:S(2)}) copy-start(bf16[2,256,1024]{2,1,0:T(8,128)(2,1)} %tokens_ref.1) | copy-start | bytes 3145732
  0.0 12.4 %copy-start.8 = (f32[3072]{0:T(1024)S(1)}, f32[3072]{0:T(1024)}, u32[]{:S(2)}) copy-start(f32[3072]{0:T(1024)} %param.15) | copy-start | bytes 36868
  0.0 12.5 %copy-start.3 = (f32[3,3,1024]{2,1,0:T(4,128)S(1)}, f32[3,3,1024]{2,1,0:T(4,128)}, u32[]{:S(2)}) copy-start(f32[3,3,1024]{2,1,0:T(4,128)} %peg_ref.3) | copy-start | bytes 110596
  0.0 12.5 %copy-start.7 = (f32[1024]{0:T(1024)S(1)}, f32[1024]{0:T(1024)}, u32[]{:S(2)}) copy-start(f32[1024]{0:T(1024)} %param.17) | copy-start | bytes 12292
  0.0 12.5 %copy-start.6 = (f32[1024]{0:T(1024)S(1)}, f32[1024]{0:T(1024)}, u32[]{:S(2)}) copy-start(f32[1024]{0:T(1024)} %param.13) | copy-start | bytes 12292
  0.0 12.5 %copy-start.5 = (f32[1024]{0:T(1024)S(1)}, f32[1024]{0:T(1024)}, u32[]{:S(2)}) copy-start(f32[1024]{0:T(1024)} %param.12) | copy-start | bytes 12292
  0.0 12.5 %copy-start.4 = (f32[1024]{0:T(1024)S(1)}, f32[1024]{0:T(1024)}, u32[]{:S(2)}) copy-start(f32[1024]{0:T(1024)} %param.11) | copy-start | bytes 12292
  2.4 10.1 %collective-permute-start = (bf16[1,256,1024]{2,1,0:T(8,128)(2,1)S(1)}, bf16[1,256,1024]{2,1,0:T(8,128)(2,1)}, u32[]{:S(2)}, u32[]{:S(2)}) collective-permute-start(bf16[1,256,1024]{2,1,0:T(8,128)(2,1)S(1)} %get-tuple-element.8), channel_id=1, source_target_pairs={{0,1},{1,0},{2,3},{3,2},{4,5},{5,4},{6,7},{7,6},{8,9},{9,8},{10,11... | collective-permute-start | bytes 1572872 | tf_op jit(solution)/shard_map/ppermute | solution.py:748
  3.0 9.5 %collective-permute-start.1 = (bf16[1,256,1024]{2,1,0:T(8,128)(2,1)S(1)}, bf16[1,256,1024]{2,1,0:T(8,128)(2,1)}, u32[]{:S(2)}, u32[]{:S(2)}) collective-permute-start(bf16[1,256,1024]{2,1,0:T(8,128)(2,1)S(1)} %get-tuple-element.9), channel_id=1, source_target_pairs={{1,2},{2,1},{3,4},{4,3},{5,6},{6,5},{7,8},{8,7},{9,10},{10,9},{11,... | collective-permute-start | bytes 1572872 | tf_op jit(solution)/shard_map/ppermute | solution.py:747
  4.5 33.1 %all-to-all-start = ((bf16[16,288,128]{2,1,0:T(8,128)(2,1)}), bf16[16,288,128]{2,1,0:T(8,128)(2,1)S(1)}, u32[]{:S(2)}, u32[]{:S(2)}) async-start(bf16[16,288,128]{2,1,0:T(8,128)(2,1)} %get-tuple-element.10), calls=%async_computation | async-start | bytes 2359296 | tf_op jit(solution)/shard_map/all_to_all | solution.py:749
  37.6 29.0 %copy-start = (f32[512,1024]{1,0:T(8,128)S(1)}, f32[512,1024]{1,0:T(8,128)}, u32[]{:S(2)}) copy-start(f32[512,1024]{1,0:T(8,128)} %row_heads.1.refs_0_) | copy-start | bytes 6291460
  37.6 29.0 %copy-start.1 = (bf16[1024,1024]{1,0:T(8,128)(2,1)S(1)}, bf16[1024,1024]{1,0:T(8,128)(2,1)}, u32[]{:S(2)}) copy-start(bf16[1024,1024]{1,0:T(8,128)(2,1)} %out_weight_ref.1) | copy-start | bytes 6291460

commit v6 on v5

--- a/solution.py
+++ b/solution.py
@@ -324,6 +324,7 @@
         ]
         weights[1][1] = weights[1][1] + 1.0
         bias = jnp.broadcast_to(peg_bias_ref[:, lanes], (SUB, LANES))
+        outer = [jnp.where(column >= 2, weights[a][0], weights[a][2]) for a in range(3)]
 
         def load(device):
             own = [
@@ -333,12 +334,9 @@
                 for tile in range(tiles)
             ]
             edge = recv_ref[device, pl.ds(pl.multiple_of(edge_base, SUB), SUB), :]
-            edge = edge.astype(jnp.float32)
-            if local == 0:
-                return [edge] + own + [edge]
-            return [pltpu.roll(edge, 1, 0)] + own + [pltpu.roll(edge, SUB - 1, 0)]
-
-        swapped = [zero] * (tiles + 2)
+            return own + [edge.astype(jnp.float32)]
+
+        swapped = [zero] * (tiles + 1)
         values = load(0)
         following = [pltpu.roll(value, HALF, 0) for value in values]
         above = [jnp.where(upper, p, n) for p, n in zip(swapped, following)]
@@ -348,7 +346,7 @@
                 coming = load(device + 1)
                 following = [pltpu.roll(value, HALF, 0) for value in coming]
             else:
-                coming, following = None, [zero] * (tiles + 2)
+                coming, following = None, [zero] * (tiles + 1)
             below = [jnp.where(upper, p, n) for p, n in zip(swapped, following)]
 
             def stencil(index, offset):
@@ -358,20 +356,25 @@
                     + below[index] * weights[2][offset]
                 )
 
-            lefts = [stencil(index, 0) for index in range(tiles + 1)]
-            rights = [stencil(index, 2) for index in range(1, tiles + 2)]
+            lefts = [stencil(index, 0) for index in range(tiles)]
+            rights = [stencil(index, 2) for index in range(tiles)]
+            beside = (
+                above[tiles] * outer[0] + values[tiles] * outer[1] + below[tiles] * outer[2]
+            )
             for tile in range(tiles):
-                from_left = jnp.where(
-                    column == 0,
-                    pltpu.roll(lefts[tile], SUB - 3, 0),
-                    pltpu.roll(lefts[tile + 1], 1, 0),
-                )
+                if tile > 0:
+                    before = pltpu.roll(lefts[tile - 1], SUB - 3, 0)
+                else:
+                    before = pltpu.roll(beside, SUB - 3 + local, 0)
+                if tile < tiles - 1:
+                    after = pltpu.roll(rights[tile + 1], 3, 0)
+                else:
+                    after = pltpu.roll(beside, 3 - local, 0)
+                from_left = jnp.where(column == 0, before, pltpu.roll(lefts[tile], 1, 0))
                 from_right = jnp.where(
-                    column == HALF - 1,
-                    pltpu.roll(rights[tile + 1], 3, 0),
-                    pltpu.roll(rights[tile], SUB - 1, 0),
-                )
-                total = (stencil(tile + 1, 1) + bias) + (from_left + from_right)
+                    column == HALF - 1, after, pltpu.roll(rights[tile], SUB - 1, 0)
+                )
+                total = (stencil(tile, 1) + bias) + (from_left + from_right)
                 mixed_scr[slab, device, tile] = total.astype(jnp.bfloat16).astype(jnp.float32)
             values, above = coming, below
 
@@ -381,7 +384,7 @@
             convolve_slab(slab, slab * tiles * SUB, (slabs * tiles + two) * SUB, local)
         return carry
 
-    lax.fori_loop(0, slabs // 2, two_slabs, 0)
+    lax.fori_loop(0, slabs // 2, two_slabs, 0, unroll=True)
 
     row_id = lax.broadcasted_iota(jnp.int32, (1, SUB, group), 1)
     col_id = lax.broadcasted_iota(jnp.int32, (1, SUB, group), 2)

time: 68.5 us -> 68.3 us (level)
  no operation moved by 1% of the time
where the time goes in v6:
time: 68.3 us; the launch traced here: 68 us
  Pallas kernels  22.3 us (33%)
  blocking collectives  22 us (32%)
  waiting for transfers between devices  13.5 us (20%)
  starting transfers between devices  10 us (15%)
    all_to_all x1, blocking collectives, on_device(): lax.all_to_all(col_heads, 'rows', split_axis=0, concat_axis=0, tiled=True)  22 us
    all_to_all x1, waiting for transfers between devices, on_device(): lax.all_to_all(packed, 'rows', split_axis=0, concat_axis=0, tiled=True)  13.5 us
    pallas_call x1, Pallas kernels, row_part(): pl.pallas_call(row_kernel, grid=(slabs,), in_specs=[pl.BlockSpec(memory_s...  11.5 us
    all_to_all x1, starting transfers between devices, on_device(): lax.all_to_all(packed, 'rows', split_axis=0, concat_axis=0, tiled=True)  7.98 us
    pallas_call x1, Pallas kernels, column_part(): pl.pallas_call(column_kernel, in_specs=[vmem] * 6 + [pl.BlockSpec(memory_...  6.79 us
    pallas_call x1, Pallas kernels, front(): pl.pallas_call(functools.partial(front_kernel, devices), in_specs=[pl.Blo...  2.39 us
    pallas_call x1, Pallas kernels, last_part(): pl.pallas_call(last_kernel, in_specs=[pl.BlockSpec(memory_space=pltpu.VME...  1.6 us
    ppermute x1, starting transfers between devices, on_device(): inter = lax.ppermute(inter, 'rows', other_chip)  1.46 us
  transfers between devices with their start and end apart: 3, of which 1 were waited for; matrix products, arithmetic and copies ran while one was open for 0% of the time, Pallas kernels for 17%

profile of v6, /device:TPU:0, one launch (start us, length us, event | category | flops | bytes accessed | tf_op | source)
XLA Modules:
  0.0 68.0 jit_solution(15156451713274313770)
XLA Ops:
  0.0 0.0 copy-start.2
  0.0 0.0 copy-start.8
  0.0 0.0 copy-start.3
  0.0 0.0 copy-start.7
  0.0 0.0 copy-start.6
  0.0 0.0 copy-start.5
  0.0 0.0 copy-start.4
  0.0 2.4 %front.1 = (bf16[16,288,128]{2,1,0:T(8,128)(2,1)}, bf16[1,256,1024]{2,1,0:T(8,128)(2,1)S(1)}, bf16[1,256,1024]{2,1,0:T(8,128)(2,1)S(1)}) custom-call(bf16[2,256,1024]{2,1,0:T(8,128)(2,1)} %tokens_ref.1), custom_call_target="tpu_custom_call" | custom-call | tf_op jit(solution)/shard_map/front/pallas_call | solution.py:221
  2.4 0.6 collective-permute-start
  3.0 1.5 %collective-permute-start.1 = (bf16[1,256,1024]{2,1,0:T(8,128)(2,1)S(1)}, bf16[1,256,1024]{2,1,0:T(8,128)(2,1)}, u32[]{:S(2)}, u32[]{:S(2)}) collective-permute-start(bf16[1,256,1024]{2,1,0:T(8,128)(2,1)S(1)} %get-tuple-element.9), channel_id=1, source_target_pairs={{1,2},{2,1},{3,4},{4,3},{5,6},{6,5},{7,8},{8,7},{9,10},{10,9},{11,... | collective-permute-start | bytes 1572872 | tf_op jit(solution)/shard_map/ppermute | solution.py:750
  4.5 8.0 %all-to-all-start = ((bf16[16,288,128]{2,1,0:T(8,128)(2,1)}), bf16[16,288,128]{2,1,0:T(8,128)(2,1)S(1)}, u32[]{:S(2)}, u32[]{:S(2)}) async-start(bf16[16,288,128]{2,1,0:T(8,128)(2,1)} %get-tuple-element.10), calls=%async_computation | async-start | bytes 2359296 | tf_op jit(solution)/shard_map/all_to_all | solution.py:752
  12.4 0.0 copy-done.8
  12.5 0.0 collective-permute-done.intra_ref
  12.5 0.0 collective-permute-done.1.inter_ref
  12.5 0.0 copy-done.2
  12.5 0.0 copy-done.3
  12.5 0.0 copy-done.7
  12.5 0.0 copy-done.6
  12.5 0.0 copy-done.5
  12.6 0.0 copy-done.4
  12.6 11.5 %row_heads.1.refs_0_ = f32[512,1024]{1,0:T(8,128)} custom-call(bf16[2,256,1024]{2,1,0:T(8,128)(2,1)S(1)} %copy-done.2, bf16[1,256,1024]{2,1,0:T(8,128)(2,1)} %collective-permute-done.intra_ref, bf16[1,256,1024]{2,1,0:T(8,128)(2,1)} %collective-permute-done.1.inter_ref, f32[3,3,1024]{2,1,0:T(4,128)S(1)} %copy-done.3, f32[1,1024]{1,0:T(1,128)S(1)} %bitcast.6, ...), custom_call_target="tpu_custom_call" | custom-call | flops 42949672960 | bytes 10485760 | tf_op jit(solution)/shard_map/row_heads/pallas_call | solution.py:611
  24.1 13.5 %all-to-all-done.recv_ref = bf16[16,288,128]{2,1,0:T(8,128)(2,1)S(1)} async-done(((bf16[16,288,128]{2,1,0:T(8,128)(2,1)}), bf16[16,288,128]{2,1,0:T(8,128)(2,1)S(1)}, u32[]{:S(2)}, u32[]{:S(2)}) %all-to-all-start) | async-done | bytes 1179680 | tf_op jit(solution)/shard_map/all_to_all | solution.py:752
  37.6 0.0 copy-start
  37.6 0.0 copy-start.1
  37.6 6.8 %column_heads.1 = bf16[16,4,8,512]{3,2,1,0:T(8,128)(2,1)} custom-call(bf16[16,288,128]{2,1,0:T(8,128)(2,1)S(1)} %all-to-all-done.recv_ref, f32[3,3,1024]{2,1,0:T(4,128)S(1)} %copy-done.3, f32[1,1024]{1,0:T(1,128)S(1)} %bitcast.7, f32[1,1024]{1,0:T(1,128)S(1)} %bitcast.9, f32[1,1024]{1,0:T(1,128)S(1)} %bitcast.11, ...), custom_call_target="tpu_custom_call" | custom-call | flops 1610612736 | bytes 8388608 | tf_op jit(solution)/shard_map/column_heads/pallas_call | solution.py:457
  44.4 22.0 %all_to_all.10.heads_ref = bf16[16,4,8,512]{3,2,1,0:T(8,128)(2,1)S(1)} all-to-all(bf16[16,4,8,512]{3,2,1,0:T(8,128)(2,1)} %column_heads.1), channel_id=1, replica_groups=mesh['groups'=2,'rows'=16] {'rows'}, dimensions={0} | all-to-all | bytes 1048576 | tf_op jit(solution)/shard_map/all_to_all | solution.py:769
  66.4 0.0 copy-done
  66.4 0.0 copy-done.1
  66.4 1.6 %last_projection.1 = bf16[2,256,1024]{2,1,0:T(8,128)(2,1)} custom-call(f32[2,256,1024]{2,1,0:T(8,128)S(1)} %bitcast.5, bf16[16,4,8,512]{3,2,1,0:T(8,128)(2,1)S(1)} %all_to_all.10.heads_ref, bf16[1024,1024]{1,0:T(8,128)(2,1)S(1)} %copy-done.1), custom_call_target="tpu_custom_call" | custom-call | flops 536870912 | bytes 5242880 | tf_op jit(solution)/shard_map/last_projection/pallas_call | solution.py:696
  (2 shorter events, 0.0 us)
Async XLA Ops:
  0.0 12.5 %copy-start.2 = (bf16[2,256,1024]{2,1,0:T(8,128)(2,1)S(1)}, bf16[2,256,1024]{2,1,0:T(8,128)(2,1)}, u32[]{:S(2)}) copy-start(bf16[2,256,1024]{2,1,0:T(8,128)(2,1)} %tokens_ref.1) | copy-start | bytes 3145732
  0.0 12.4 %copy-start.8 = (f32[3072]{0:T(1024)S(1)}, f32[3072]{0:T(1024)}, u32[]{:S(2)}) copy-start(f32[3072]{0:T(1024)} %param.15) | copy-start | bytes 36868
  0.0 12.5 %copy-start.3 = (f32[3,3,1024]{2,1,0:T(4,128)S(1)}, f32[3,3,1024]{2,1,0:T(4,128)}, u32[]{:S(2)}) copy-start(f32[3,3,1024]{2,1,0:T(4,128)} %peg_ref.3) | copy-start | bytes 110596
  0.0 12.5 %copy-start.7 = (f32[1024]{0:T(1024)S(1)}, f32[1024]{0:T(1024)}, u32[]{:S(2)}) copy-start(f32[1024]{0:T(1024)} %param.17) | copy-start | bytes 12292
  0.0 12.5 %copy-start.6 = (f32[1024]{0:T(1024)S(1)}, f32[1024]{0:T(1024)}, u32[]{:S(2)}) copy-start(f32[1024]{0:T(1024)} %param.13) | copy-start | bytes 12292
  0.0 12.5 %copy-start.5 = (f32[1024]{0:T(1024)S(1)}, f32[1024]{0:T(1024)}, u32[]{:S(2)}) copy-start(f32[1024]{0:T(1024)} %param.12) | copy-start | bytes 12292
  0.0 12.5 %copy-start.4 = (f32[1024]{0:T(1024)S(1)}, f32[1024]{0:T(1024)}, u32[]{:S(2)}) copy-start(f32[1024]{0:T(1024)} %param.11) | copy-start | bytes 12292
  2.4 10.1 %collective-permute-start = (bf16[1,256,1024]{2,1,0:T(8,128)(2,1)S(1)}, bf16[1,256,1024]{2,1,0:T(8,128)(2,1)}, u32[]{:S(2)}, u32[]{:S(2)}) collective-permute-start(bf16[1,256,1024]{2,1,0:T(8,128)(2,1)S(1)} %get-tuple-element.8), channel_id=1, source_target_pairs={{0,1},{1,0},{2,3},{3,2},{4,5},{5,4},{6,7},{7,6},{8,9},{9,8},{10,11... | collective-permute-start | bytes 1572872 | tf_op jit(solution)/shard_map/ppermute | solution.py:751
  3.0 9.5 %collective-permute-start.1 = (bf16[1,256,1024]{2,1,0:T(8,128)(2,1)S(1)}, bf16[1,256,1024]{2,1,0:T(8,128)(2,1)}, u32[]{:S(2)}, u32[]{:S(2)}) collective-permute-start(bf16[1,256,1024]{2,1,0:T(8,128)(2,1)S(1)} %get-tuple-element.9), channel_id=1, source_target_pairs={{1,2},{2,1},{3,4},{4,3},{5,6},{6,5},{7,8},{8,7},{9,10},{10,9},{11,... | collective-permute-start | bytes 1572872 | tf_op jit(solution)/shard_map/ppermute | solution.py:750
  4.5 33.1 %all-to-all-start = ((bf16[16,288,128]{2,1,0:T(8,128)(2,1)}), bf16[16,288,128]{2,1,0:T(8,128)(2,1)S(1)}, u32[]{:S(2)}, u32[]{:S(2)}) async-start(bf16[16,288,128]{2,1,0:T(8,128)(2,1)} %get-tuple-element.10), calls=%async_computation | async-start | bytes 2359296 | tf_op jit(solution)/shard_map/all_to_all | solution.py:752
  37.6 28.8 %copy-start = (f32[512,1024]{1,0:T(8,128)S(1)}, f32[512,1024]{1,0:T(8,128)}, u32[]{:S(2)}) copy-start(f32[512,1024]{1,0:T(8,128)} %row_heads.1.refs_0_) | copy-start | bytes 6291460
  37.6 28.8 %copy-start.1 = (bf16[1024,1024]{1,0:T(8,128)(2,1)S(1)}, bf16[1024,1024]{1,0:T(8,128)(2,1)}, u32[]{:S(2)}) copy-start(bf16[1024,1024]{1,0:T(8,128)(2,1)} %out_weight_ref.1) | copy-start | bytes 6291460

commit v7 on v6

--- a/solution.py
+++ b/solution.py
@@ -228,7 +228,7 @@
         scratch_shapes=[
             pltpu.VMEM((bands, width, model), jnp.bfloat16),
             pltpu.VMEM((devices, rows, LANES), jnp.bfloat16),
-            pltpu.SemaphoreType.DMA((4,)),
+            pltpu.SemaphoreType.DMA((8,)),
             pltpu.SemaphoreType.DMA((2,)),
             pltpu.SemaphoreType.DMA((devices,)),
         ],

time: 68.3 us -> 68.3 us (level)
  no operation moved by 1% of the time
where the time goes in v7:
time: 68.3 us; the launch traced here: 68 us
  Pallas kernels  22.3 us (33%)
  blocking collectives  22 us (32%)
  waiting for transfers between devices  13.5 us (20%)
  starting transfers between devices  10 us (15%)
    all_to_all x1, blocking collectives, on_device(): lax.all_to_all(col_heads, 'rows', split_axis=0, concat_axis=0, tiled=True)  22 us
    all_to_all x1, waiting for transfers between devices, on_device(): lax.all_to_all(packed, 'rows', split_axis=0, concat_axis=0, tiled=True)  13.5 us
    pallas_call x1, Pallas kernels, row_part(): pl.pallas_call(row_kernel, grid=(slabs,), in_specs=[pl.BlockSpec(memory_s...  11.5 us
    all_to_all x1, starting transfers between devices, on_device(): lax.all_to_all(packed, 'rows', split_axis=0, concat_axis=0, tiled=True)  7.95 us
    pallas_call x1, Pallas kernels, column_part(): pl.pallas_call(column_kernel, in_specs=[vmem] * 6 + [pl.BlockSpec(memory_...  6.79 us
    pallas_call x1, Pallas kernels, front(): pl.pallas_call(functools.partial(front_kernel, devices), in_specs=[pl.Blo...  2.4 us
    pallas_call x1, Pallas kernels, last_part(): pl.pallas_call(last_kernel, in_specs=[pl.BlockSpec(memory_space=pltpu.VME...  1.6 us
    ppermute x1, starting transfers between devices, on_device(): inter = lax.ppermute(inter, 'rows', other_chip)  1.46 us
  transfers between devices with their start and end apart: 3, of which 1 were waited for; matrix products, arithmetic and copies ran while one was open for 0% of the time, Pallas kernels for 17%

profile of v7, /device:TPU:0, one launch (start us, length us, event | category | flops | bytes accessed | tf_op | source)
XLA Modules:
  0.0 68.0 jit_solution(6706861310711178849)
XLA Ops:
  0.0 0.0 copy-start.2
  0.0 0.0 copy-start.8
  0.0 0.0 copy-start.3
  0.0 0.0 copy-start.7
  0.0 0.0 copy-start.6
  0.0 0.0 copy-start.5
  0.0 0.0 copy-start.4
  0.0 2.4 %front.1 = (bf16[16,288,128]{2,1,0:T(8,128)(2,1)}, bf16[1,256,1024]{2,1,0:T(8,128)(2,1)S(1)}, bf16[1,256,1024]{2,1,0:T(8,128)(2,1)S(1)}) custom-call(bf16[2,256,1024]{2,1,0:T(8,128)(2,1)} %tokens_ref.1), custom_call_target="tpu_custom_call" | custom-call | tf_op jit(solution)/shard_map/front/pallas_call | solution.py:221
  2.4 0.6 collective-permute-start
  3.0 1.5 %collective-permute-start.1 = (bf16[1,256,1024]{2,1,0:T(8,128)(2,1)S(1)}, bf16[1,256,1024]{2,1,0:T(8,128)(2,1)}, u32[]{:S(2)}, u32[]{:S(2)}) collective-permute-start(bf16[1,256,1024]{2,1,0:T(8,128)(2,1)S(1)} %get-tuple-element.9), channel_id=1, source_target_pairs={{1,2},{2,1},{3,4},{4,3},{5,6},{6,5},{7,8},{8,7},{9,10},{10,9},{11,... | collective-permute-start | bytes 1572872 | tf_op jit(solution)/shard_map/ppermute | solution.py:750
  4.5 8.0 %all-to-all-start = ((bf16[16,288,128]{2,1,0:T(8,128)(2,1)}), bf16[16,288,128]{2,1,0:T(8,128)(2,1)S(1)}, u32[]{:S(2)}, u32[]{:S(2)}) async-start(bf16[16,288,128]{2,1,0:T(8,128)(2,1)} %get-tuple-element.10), calls=%async_computation | async-start | bytes 2359296 | tf_op jit(solution)/shard_map/all_to_all | solution.py:752
  12.5 0.0 copy-done.8
  12.5 0.0 collective-permute-done.intra_ref
  12.5 0.0 collective-permute-done.1.inter_ref
  12.5 0.0 copy-done.2
  12.5 0.0 copy-done.3
  12.5 0.0 copy-done.7
  12.5 0.0 copy-done.6
  12.6 0.0 copy-done.5
  12.6 0.0 copy-done.4
  12.6 11.5 %row_heads.1.refs_0_ = f32[512,1024]{1,0:T(8,128)} custom-call(bf16[2,256,1024]{2,1,0:T(8,128)(2,1)S(1)} %copy-done.2, bf16[1,256,1024]{2,1,0:T(8,128)(2,1)} %collective-permute-done.intra_ref, bf16[1,256,1024]{2,1,0:T(8,128)(2,1)} %collective-permute-done.1.inter_ref, f32[3,3,1024]{2,1,0:T(4,128)S(1)} %copy-done.3, f32[1,1024]{1,0:T(1,128)S(1)} %bitcast.6, ...), custom_call_target="tpu_custom_call" | custom-call | flops 42949672960 | bytes 10485760 | tf_op jit(solution)/shard_map/row_heads/pallas_call | solution.py:611
  24.1 13.5 %all-to-all-done.recv_ref = bf16[16,288,128]{2,1,0:T(8,128)(2,1)S(1)} async-done(((bf16[16,288,128]{2,1,0:T(8,128)(2,1)}), bf16[16,288,128]{2,1,0:T(8,128)(2,1)S(1)}, u32[]{:S(2)}, u32[]{:S(2)}) %all-to-all-start) | async-done | bytes 1179680 | tf_op jit(solution)/shard_map/all_to_all | solution.py:752
  37.6 0.0 copy-start
  37.6 0.0 copy-start.1
  37.6 6.8 %column_heads.1 = bf16[16,4,8,512]{3,2,1,0:T(8,128)(2,1)} custom-call(bf16[16,288,128]{2,1,0:T(8,128)(2,1)S(1)} %all-to-all-done.recv_ref, f32[3,3,1024]{2,1,0:T(4,128)S(1)} %copy-done.3, f32[1,1024]{1,0:T(1,128)S(1)} %bitcast.7, f32[1,1024]{1,0:T(1,128)S(1)} %bitcast.9, f32[1,1024]{1,0:T(1,128)S(1)} %bitcast.11, ...), custom_call_target="tpu_custom_call" | custom-call | flops 1610612736 | bytes 8388608 | tf_op jit(solution)/shard_map/column_heads/pallas_call | solution.py:457
  44.4 22.0 %all_to_all.10.heads_ref = bf16[16,4,8,512]{3,2,1,0:T(8,128)(2,1)S(1)} all-to-all(bf16[16,4,8,512]{3,2,1,0:T(8,128)(2,1)} %column_heads.1), channel_id=1, replica_groups=mesh['groups'=2,'rows'=16] {'rows'}, dimensions={0} | all-to-all | bytes 1048576 | tf_op jit(solution)/shard_map/all_to_all | solution.py:769
  66.4 0.0 copy-done
  66.4 0.0 copy-done.1
  66.4 1.6 %last_projection.1 = bf16[2,256,1024]{2,1,0:T(8,128)(2,1)} custom-call(f32[2,256,1024]{2,1,0:T(8,128)S(1)} %bitcast.5, bf16[16,4,8,512]{3,2,1,0:T(8,128)(2,1)S(1)} %all_to_all.10.heads_ref, bf16[1024,1024]{1,0:T(8,128)(2,1)S(1)} %copy-done.1), custom_call_target="tpu_custom_call" | custom-call | flops 536870912 | bytes 5242880 | tf_op jit(solution)/shard_map/last_projection/pallas_call | solution.py:696
  (2 shorter events, 0.0 us)
Async XLA Ops:
  0.0 12.5 %copy-start.2 = (bf16[2,256,1024]{2,1,0:T(8,128)(2,1)S(1)}, bf16[2,256,1024]{2,1,0:T(8,128)(2,1)}, u32[]{:S(2)}) copy-start(bf16[2,256,1024]{2,1,0:T(8,128)(2,1)} %tokens_ref.1) | copy-start | bytes 3145732
  0.0 12.5 %copy-start.8 = (f32[3072]{0:T(1024)S(1)}, f32[3072]{0:T(1024)}, u32[]{:S(2)}) copy-start(f32[3072]{0:T(1024)} %param.15) | copy-start | bytes 36868
  0.0 12.5 %copy-start.3 = (f32[3,3,1024]{2,1,0:T(4,128)S(1)}, f32[3,3,1024]{2,1,0:T(4,128)}, u32[]{:S(2)}) copy-start(f32[3,3,1024]{2,1,0:T(4,128)} %peg_ref.3) | copy-start | bytes 110596
  0.0 12.5 %copy-start.7 = (f32[1024]{0:T(1024)S(1)}, f32[1024]{0:T(1024)}, u32[]{:S(2)}) copy-start(f32[1024]{0:T(1024)} %param.17) | copy-start | bytes 12292
  0.0 12.5 %copy-start.6 = (f32[1024]{0:T(1024)S(1)}, f32[1024]{0:T(1024)}, u32[]{:S(2)}) copy-start(f32[1024]{0:T(1024)} %param.13) | copy-start | bytes 12292
  0.0 12.5 %copy-start.5 = (f32[1024]{0:T(1024)S(1)}, f32[1024]{0:T(1024)}, u32[]{:S(2)}) copy-start(f32[1024]{0:T(1024)} %param.12) | copy-start | bytes 12292
  0.0 12.5 %copy-start.4 = (f32[1024]{0:T(1024)S(1)}, f32[1024]{0:T(1024)}, u32[]{:S(2)}) copy-start(f32[1024]{0:T(1024)} %param.11) | copy-start | bytes 12292
  2.4 10.1 %collective-permute-start = (bf16[1,256,1024]{2,1,0:T(8,128)(2,1)S(1)}, bf16[1,256,1024]{2,1,0:T(8,128)(2,1)}, u32[]{:S(2)}, u32[]{:S(2)}) collective-permute-start(bf16[1,256,1024]{2,1,0:T(8,128)(2,1)S(1)} %get-tuple-element.8), channel_id=1, source_target_pairs={{0,1},{1,0},{2,3},{3,2},{4,5},{5,4},{6,7},{7,6},{8,9},{9,8},{10,11... | collective-permute-start | bytes 1572872 | tf_op jit(solution)/shard_map/ppermute | solution.py:751
  3.0 9.5 %collective-permute-start.1 = (bf16[1,256,1024]{2,1,0:T(8,128)(2,1)S(1)}, bf16[1,256,1024]{2,1,0:T(8,128)(2,1)}, u32[]{:S(2)}, u32[]{:S(2)}) collective-permute-start(bf16[1,256,1024]{2,1,0:T(8,128)(2,1)S(1)} %get-tuple-element.9), channel_id=1, source_target_pairs={{1,2},{2,1},{3,4},{4,3},{5,6},{6,5},{7,8},{8,7},{9,10},{10,9},{11,... | collective-permute-start | bytes 1572872 | tf_op jit(solution)/shard_map/ppermute | solution.py:750
  4.5 33.1 %all-to-all-start = ((bf16[16,288,128]{2,1,0:T(8,128)(2,1)}), bf16[16,288,128]{2,1,0:T(8,128)(2,1)S(1)}, u32[]{:S(2)}, u32[]{:S(2)}) async-start(bf16[16,288,128]{2,1,0:T(8,128)(2,1)} %get-tuple-element.10), calls=%async_computation | async-start | bytes 2359296 | tf_op jit(solution)/shard_map/all_to_all | solution.py:752
  37.6 28.8 %copy-start = (f32[512,1024]{1,0:T(8,128)S(1)}, f32[512,1024]{1,0:T(8,128)}, u32[]{:S(2)}) copy-start(f32[512,1024]{1,0:T(8,128)} %row_heads.1.refs_0_) | copy-start | bytes 6291460
  37.6 28.8 %copy-start.1 = (bf16[1024,1024]{1,0:T(8,128)(2,1)S(1)}, bf16[1024,1024]{1,0:T(8,128)(2,1)}, u32[]{:S(2)}) copy-start(bf16[1024,1024]{1,0:T(8,128)(2,1)} %out_weight_ref.1) | copy-start | bytes 6291460
